TPU v7x, 32 devices: a whole 2x2x4 slice. The times are simulated.
32 devices in a mesh: dp: 8 (over y, x, core), head: 4 (over z).
Axes of the slice: x: 2, y: 2, z: 4, core: 2. Of those that a mesh axis runs over, the one named last changes fastest.
Arguments:
- block_input: bfloat16 [512, 50, 512], P(('dp', 'head')), may hold values from -6 to 6
- out_grad: bfloat16 [512, 50, 512], P(('dp', 'head')), may hold values from -6 to 6
- kernel_radius: int32 [8], replicated, may hold values from 1 to 3, as said below
- qkv_weight: float32 [512, 3, 512], P('dp', None, 'head'), may hold values from -0.25 to 0.25
- qkv_first: float32 [512, 3, 512], P('dp', None, 'head'), may hold values from -0.0004 to 0.0004
- qkv_second: float32 [512, 3, 512], P('dp', None, 'head'), may hold values from 3e-10 to 1.3e-09
- qkv_average: float32 [512, 3, 512], P('dp', None, 'head'), may hold values from -0.25 to 0.25
- proj_weight: float32 [512, 512], P('dp', 'head'), may hold values from -0.25 to 0.25
- proj_first: float32 [512, 512], P('dp', 'head'), may hold values from -0.0004 to 0.0004
- proj_second: float32 [512, 512], P('dp', 'head'), may hold values from 3e-10 to 1.3e-09
- proj_average: float32 [512, 512], P('dp', 'head'), may hold values from -0.25 to 0.25
- up_weight: float32 [512, 2048], P('dp', 'head'), may hold values from -0.25 to 0.25
- up_first: float32 [512, 2048], P('dp', 'head'), may hold values from -0.0004 to 0.0004
- up_second: float32 [512, 2048], P('dp', 'head'), may hold values from 3e-10 to 1.3e-09
- up_average: float32 [512, 2048], P('dp', 'head'), may hold values from -0.25 to 0.25
- down_weight: float32 [512, 2048], P('dp', 'head'), may hold values from -0.125 to 0.125
- down_first: float32 [512, 2048], P('dp', 'head'), may hold values from -0.0004 to 0.0004
- down_second: float32 [512, 2048], P('dp', 'head'), may hold values from 3e-10 to 1.3e-09
- down_average: float32 [512, 2048], P('dp', 'head'), may hold values from -0.125 to 0.125
- head_params: float32 [56, 512], replicated, may hold values from -1.2 to 1.2
- head_first: float32 [56, 512], replicated, may hold values from -0.0015 to 0.0015
- head_second: float32 [56, 512], replicated, may hold values from 5e-09 to 2e-08
- head_average: float32 [56, 512], replicated, may hold values from -1.2 to 1.2
- rep_params: float32 [16, 512], replicated, may hold values from -1.2 to 1.4, as said below
- rep_first: float32 [16, 512], replicated, may hold values from -0.0015 to 0.0015
- rep_second: float32 [16, 512], replicated, may hold values from 5e-09 to 2e-08
- rep_average: float32 [16, 512], replicated, may hold values from -1.8 to 1.8
Outputs:
- block_output: bfloat16 [512, 50, 512], P(('dp', 'head'))
- input_grad: bfloat16 [512, 50, 512], P(('dp', 'head'))
- grad_norm: float32 [], replicated
- qkv_grad: float32 [512, 3, 512], P('dp', None, 'head')
- qkv_first_new: float32 [512, 3, 512], P('dp', None, 'head')
- qkv_second_new: float32 [512, 3, 512], P('dp', None, 'head')
- qkv_weight_new: float32 [512, 3, 512], P('dp', None, 'head')
- qkv_weight_low: bfloat16 [512, 3, 512], P('dp', None, 'head')
- qkv_average_new: float32 [512, 3, 512], P('dp', None, 'head')
- proj_grad: float32 [512, 512], P('dp', 'head')
- proj_first_new: float32 [512, 512], P('dp', 'head')
- proj_second_new: float32 [512, 512], P('dp', 'head')
- proj_weight_new: float32 [512, 512], P('dp', 'head')
- proj_weight_low: bfloat16 [512, 512], P('dp', 'head')
- proj_average_new: float32 [512, 512], P('dp', 'head')
- up_grad: float32 [512, 2048], P('dp', 'head')
- up_first_new: float32 [512, 2048], P('dp', 'head')
- up_second_new: float32 [512, 2048], P('dp', 'head')
- up_weight_new: float32 [512, 2048], P('dp', 'head')
- up_weight_low: bfloat16 [512, 2048], P('dp', 'head')
- up_average_new: float32 [512, 2048], P('dp', 'head')
- down_grad: float32 [512, 2048], P('dp', 'head')
- down_first_new: float32 [512, 2048], P('dp', 'head')
- down_second_new: float32 [512, 2048], P('dp', 'head')
- down_weight_new: float32 [512, 2048], P('dp', 'head')
- down_weight_low: bfloat16 [512, 2048], P('dp', 'head')
- down_average_new: float32 [512, 2048], P('dp', 'head')
- head_grad: float32 [56, 512], replicated
- head_first_new: float32 [56, 512], replicated
- head_second_new: float32 [56, 512], replicated
- head_weight_new: float32 [56, 512], replicated
- head_weight_low: bfloat16 [56, 512], replicated
- head_average_new: float32 [56, 512], replicated
- rep_grad: float32 [16, 512], replicated
- rep_first_new: float32 [16, 512], replicated
- rep_second_new: float32 [16, 512], replicated
- rep_weight_new: float32 [16, 512], replicated
- rep_weight_low: bfloat16 [16, 512], replicated
- rep_average_new: float32 [16, 512], replicated
Inputs may be any that keep to these rules, and one draw needn't show every extreme that they name: `kernel_radius`: two heads have radius 1, three radius 2 and three radius 3; which heads is drawn. `rep_params`: rows 10 and 12 are gains near 1; the other rows are of order 0.2.
All inputs are finite; a program needn't handle non-finite values.
Results may differ from a plain program's by a relative error of at most 0.014.
Values may be sent and summed in bfloat16 or wider, within the bound.
No kernel may reach another device: no remote copies, remote signals or barrier semaphores. Data moves between devices by JAX's collectives and lax.ppermute only.
A program may use at most 192 MiB of HBM per device.

v0:
```python
from functools import partial

import jax
import jax.numpy as jnp
from jax import lax
from jax.sharding import PartitionSpec as P

HD = 64
GRID = 7
TAPS = 49
STEP = 5
SEQ = 50


NORM_EPS = 1e-06
BETA_FIRST = 0.9
BETA_SECOND = 0.999
ADAM_EPS = 1e-08
LEARN_RATE = 0.1
WEIGHT_DECAY = 0.05
CLIP_NORM = 1.0
AVG_KEEP = 0.9
HIGHEST = lax.Precision.HIGHEST


def cut_along(shard, dim, length):
    before, after = (shard.shape[:dim], shard.shape[dim + 1 :])
    return jnp.moveaxis(shard.reshape(*before, length, -1, *after), dim, 0)


def sum_at_owner(shard, axis, dim):
    length = lax.axis_size(axis)
    pieces = lax.all_to_all(cut_along(shard, dim, length), axis, 0, 0, tiled=True)
    return jnp.sum(pieces.astype(jnp.float32), axis=0)


def tap_mask(radius):
    reach = jnp.repeat(radius, HD)
    taps = lax.broadcasted_iota(jnp.int32, (TAPS, reach.shape[0]), 0)
    vertical = jnp.abs(taps // 7 - 3)
    horizontal = jnp.abs(taps % 7 - 3)
    inside = (vertical <= reach[None, :]) & (horizontal <= reach[None, :])
    return inside.astype(jnp.float32)


def depthwise(grid, taps, reach):
    side = 2 * reach + 1
    extent = grid.shape[1]
    padded = jnp.pad(grid, ((0, 0), (reach, reach), (reach, reach), (0, 0)))
    total = jnp.zeros(grid.shape, jnp.float32)
    for tap_row in range(side):
        for tap_col in range(side):
            total = (
                total
                + taps[tap_row * side + tap_col]
                * padded[:, tap_row : tap_row + extent, tap_col : tap_col + extent, :]
            )
    return total


def depthwise_back(grad, taps, reach):
    side = 2 * reach + 1
    extent = grad.shape[1]
    padded = jnp.pad(grad, ((0, 0), (reach, reach), (reach, reach), (0, 0)))
    total = jnp.zeros(grad.shape, jnp.float32)
    for tap_row in range(side):
        for tap_col in range(side):
            start_row = 2 * reach - tap_row
            start_col = 2 * reach - tap_col
            total = (
                total
                + taps[tap_row * side + tap_col]
                * padded[:, start_row : start_row + extent, start_col : start_col + extent, :]
            )
    return total


def tap_sums(grid, grad, reach):
    side = 2 * reach + 1
    extent = grid.shape[1]
    padded = jnp.pad(grid, ((0, 0), (reach, reach), (reach, reach), (0, 0)))
    listed = []
    for tap_row in range(side):
        for tap_col in range(side):
            listed.append(
                jnp.sum(
                    grad * padded[:, tap_row : tap_row + extent, tap_col : tap_col + extent, :],
                    axis=(0, 1, 2),
                )
            )
    return jnp.stack(listed)


def norm_forward(values, gain, shift):
    center = values - jnp.mean(values, axis=-1, keepdims=True)
    scale_inv = lax.rsqrt(jnp.mean(center * center, axis=-1, keepdims=True) + NORM_EPS)
    unit = center * scale_inv
    return (unit * gain + shift, unit, scale_inv)


def norm_backward(grad_out, gain, unit, scale_inv):
    grad_unit = grad_out * gain
    mean_one = jnp.mean(grad_unit, axis=-1, keepdims=True)
    mean_two = jnp.mean(grad_unit * unit, axis=-1, keepdims=True)
    return scale_inv * (grad_unit - mean_one - unit * mean_two)


def soft_tokens(scores):
    top = jnp.max(scores, axis=1, keepdims=True)
    expo = jnp.exp(scores - top)
    return expo / jnp.sum(expo, axis=1, keepdims=True)


def block_pass(inputs, cotangent, weights, head_par, up_bias, rep_par, mask, movers):
    (
        spread_one,
        collect_one,
        spread_two,
        collect_two,
        spread_three,
        collect_three,
        spread_four,
        collect_four,
    ) = movers
    w_qkv, w_proj, w_up, w_down = weights
    images = inputs.shape[0]
    width = inputs.shape[2]
    channels = w_qkv.shape[2]
    head_count = channels // HD
    att_scale = HD ** (-0.5)
    x_value = inputs.astype(jnp.float32)
    pixels = x_value[:, 1:].reshape(images, GRID, GRID, width)
    mixed = pixels + depthwise(pixels, rep_par[0:9], 1) + rep_par[9]
    stream_zero = jnp.concatenate(
        [x_value[:, :1], mixed.reshape(images, GRID * GRID, width)], axis=1
    )
    normed_one, unit_one, inv_one = norm_forward(stream_zero, rep_par[10], rep_par[11])
    rows_one = spread_one(normed_one.astype(jnp.bfloat16))
    batch = rows_one.shape[0]
    bias_qkv = jnp.stack(
        [head_par[TAPS + 1], jnp.zeros((channels,), jnp.float32), head_par[TAPS + 2]]
    )
    proj_qkv = (
        jnp.einsum("bnd,dte->bnte", rows_one, w_qkv, preferred_element_type=jnp.float32) + bias_qkv
    )
    queries = proj_qkv[:, :, 0]
    keys_soft = soft_tokens(proj_qkv[:, :, 1])
    values_v = proj_qkv[:, :, 2]
    query_heads = queries.reshape(batch, SEQ, head_count, HD)
    key_heads = keys_soft.reshape(batch, SEQ, head_count, HD)
    value_heads = values_v.reshape(batch, SEQ, head_count, HD)
    context = jnp.einsum("bnhi,bnhj->bhij", key_heads, value_heads, precision=HIGHEST)
    factor = att_scale * jnp.einsum(
        "bnhi,bhij->bnhj", query_heads, context, precision=HIGHEST
    ).reshape(batch, SEQ, channels)
    crpe_taps = head_par[0:TAPS] * mask
    value_grid = values_v[:, 1:].reshape(batch, GRID, GRID, channels)
    conv_flat = (depthwise(value_grid, crpe_taps, 3) + head_par[TAPS]).reshape(
        batch, GRID * GRID, channels
    )
    blank = jnp.zeros((batch, 1, channels), jnp.float32)
    attended = (factor + jnp.concatenate([blank, queries[:, 1:] * conv_flat], axis=1)).astype(
        jnp.bfloat16
    )
    proj_part = jnp.einsum("bnc,oc->bno", attended, w_proj, preferred_element_type=jnp.float32)
    stream_one = stream_zero + collect_one(proj_part) + rep_par[14]
    normed_two, unit_two, inv_two = norm_forward(stream_one, rep_par[12], rep_par[13])
    rows_two = spread_two(normed_two.astype(jnp.bfloat16))
    hidden_pre = (
        jnp.einsum("bnd,df->bnf", rows_two, w_up, preferred_element_type=jnp.float32) + up_bias
    )
    hidden_act, gelu_pull = jax.vjp(partial(jax.nn.gelu, approximate=False), hidden_pre)
    hidden = hidden_act.astype(jnp.bfloat16)
    mlp_part = jnp.einsum("bnf,df->bnd", hidden, w_down, preferred_element_type=jnp.float32)
    output = (stream_one + collect_two(mlp_part) + rep_par[15]).astype(jnp.bfloat16)
    grad_out = cotangent.astype(jnp.float32)
    rows_grad = spread_three(cotangent)
    grad_down = jnp.einsum("bnd,bnf->df", rows_grad, hidden, preferred_element_type=jnp.float32)
    grad_hidden = jnp.einsum("bnd,df->bnf", rows_grad, w_down, preferred_element_type=jnp.float32)
    grad_pre = gelu_pull(grad_hidden)[0].astype(jnp.bfloat16)
    grad_up_bias = jnp.sum(grad_pre, axis=(0, 1), dtype=jnp.float32)
    grad_up = jnp.einsum("bnd,bnf->df", rows_two, grad_pre, preferred_element_type=jnp.float32)
    grad_norm_two = collect_three(
        jnp.einsum("bnf,df->bnd", grad_pre, w_up, preferred_element_type=jnp.float32)
    )
    grad_stream_one = grad_out + norm_backward(grad_norm_two, rep_par[12], unit_two, inv_two)
    grad_attn_low = grad_stream_one.astype(jnp.bfloat16)
    rows_attn = spread_four(grad_attn_low)
    grad_proj = jnp.einsum("bno,bnc->oc", rows_attn, attended, preferred_element_type=jnp.float32)
    grad_att = jnp.einsum("bno,oc->bnc", rows_attn, w_proj, preferred_element_type=jnp.float32)
    grad_heads = grad_att.reshape(batch, SEQ, head_count, HD)
    grad_encoded = grad_att[:, 1:]
    grad_conv = (grad_encoded * queries[:, 1:]).reshape(batch, GRID, GRID, channels)
    grad_query = att_scale * jnp.einsum(
        "bnhj,bhij->bnhi", grad_heads, context, precision=HIGHEST
    ).reshape(batch, SEQ, channels)
    grad_query = grad_query + jnp.concatenate([blank, grad_encoded * conv_flat], axis=1)
    grad_context = att_scale * jnp.einsum(
        "bnhi,bnhj->bhij", query_heads, grad_heads, precision=HIGHEST
    )
    grad_soft = jnp.einsum("bnhj,bhij->bnhi", value_heads, grad_context, precision=HIGHEST).reshape(
        batch, SEQ, channels
    )
    grad_value = jnp.einsum("bnhi,bhij->bnhj", key_heads, grad_context, precision=HIGHEST).reshape(
        batch, SEQ, channels
    )
    grad_value = grad_value + jnp.concatenate(
        [blank, depthwise_back(grad_conv, crpe_taps, 3).reshape(batch, GRID * GRID, channels)],
        axis=1,
    )
    grad_key = keys_soft * (grad_soft - jnp.sum(keys_soft * grad_soft, axis=1, keepdims=True))
    grad_qkv = jnp.stack([grad_query, grad_key, grad_value], axis=2).astype(jnp.bfloat16)
    grad_crpe = tap_sums(value_grid, grad_conv, 3) * mask
    grad_kind_sum = jnp.sum(grad_qkv, axis=(0, 1), dtype=jnp.float32)
    grad_w_qkv = jnp.einsum("bnd,bnte->dte", rows_one, grad_qkv, preferred_element_type=jnp.float32)
    grad_norm_one = collect_four(
        jnp.einsum("bnte,dte->bnd", grad_qkv, w_qkv, preferred_element_type=jnp.float32)
    )
    grad_stream_zero = grad_stream_one + norm_backward(
        grad_norm_one, rep_par[10], unit_one, inv_one
    )
    grad_patch = grad_stream_zero[:, 1:].reshape(images, GRID, GRID, width)
    grad_pixels = grad_patch + depthwise_back(grad_patch, rep_par[0:9], 1)
    input_grad = jnp.concatenate(
        [grad_stream_zero[:, :1], grad_pixels.reshape(images, GRID * GRID, width)], axis=1
    ).astype(jnp.bfloat16)
    head_grad = jnp.concatenate(
        [
            grad_crpe,
            jnp.sum(grad_conv, axis=(0, 1, 2))[None],
            grad_kind_sum[0][None],
            grad_kind_sum[2][None],
        ],
        axis=0,
    )
    rep_grad = jnp.concatenate(
        [
            tap_sums(pixels, grad_patch, 1),
            jnp.sum(grad_patch, axis=(0, 1, 2))[None],
            jnp.sum(grad_norm_one * unit_one, axis=(0, 1))[None],
            jnp.sum(grad_norm_one, axis=(0, 1))[None],
            jnp.sum(grad_norm_two * unit_two, axis=(0, 1))[None],
            jnp.sum(grad_norm_two, axis=(0, 1))[None],
            jnp.sum(grad_attn_low, axis=(0, 1), dtype=jnp.float32)[None],
            jnp.sum(grad_out, axis=(0, 1))[None],
        ],
        axis=0,
    )
    return (
        output,
        input_grad,
        (grad_w_qkv, grad_proj, grad_up, grad_down),
        head_grad,
        grad_up_bias,
        rep_grad,
    )


def adam_step(raw, weight, first, second, average, scale_clip, decay):
    grad = raw * scale_clip
    first_new = BETA_FIRST * first + (1.0 - BETA_FIRST) * grad
    second_new = BETA_SECOND * second + (1.0 - BETA_SECOND) * grad * grad
    moment_hat = first_new / (1.0 - BETA_FIRST**STEP)
    second_hat = second_new / (1.0 - BETA_SECOND**STEP)
    weight_new = weight - LEARN_RATE * (
        moment_hat / (jnp.sqrt(second_hat) + ADAM_EPS) + decay * weight
    )
    average_new = AVG_KEEP * average + (1.0 - AVG_KEEP) * weight_new
    return (grad, first_new, second_new, weight_new, weight_new.astype(jnp.bfloat16), average_new)


def square_sum(values):
    return jnp.sum(values * values)


def per_device(
    block_input,
    out_grad,
    kernel_radius,
    qkv_weight,
    qkv_first,
    qkv_second,
    qkv_average,
    proj_weight,
    proj_first,
    proj_second,
    proj_average,
    up_weight,
    up_first,
    up_second,
    up_average,
    down_weight,
    down_first,
    down_second,
    down_average,
    head_params,
    head_first,
    head_second,
    head_average,
    rep_params,
    rep_first,
    rep_second,
    rep_average,
):
    shards = (
        lax.all_gather(qkv_weight.astype(jnp.bfloat16), "dp", axis=0, tiled=True),
        lax.all_gather(proj_weight.astype(jnp.bfloat16), "dp", axis=0, tiled=True),
        lax.all_gather(up_weight.astype(jnp.bfloat16), "dp", axis=0, tiled=True),
        lax.all_gather(down_weight.astype(jnp.bfloat16), "dp", axis=0, tiled=True),
    )
    head_index = lax.axis_index("head")
    local_cols = qkv_weight.shape[2]
    hidden_cols = up_weight.shape[1]
    full_width = head_params.shape[1]
    bias_flat = head_params[TAPS + 3 :].reshape(-1)

    def spread_one(values):
        return lax.all_gather(values, "head", axis=0, tiled=True)

    def collect_one(values):
        return lax.psum_scatter(
            values.astype(jnp.bfloat16), "head", scatter_dimension=0, tiled=True
        ).astype(jnp.float32)

    def spread_two(values):
        return lax.all_gather(values, "head", axis=0, tiled=True)

    def collect_two(values):
        return lax.psum_scatter(
            values.astype(jnp.bfloat16), "head", scatter_dimension=0, tiled=True
        ).astype(jnp.float32)

    def spread_three(values):
        return lax.all_gather(values, "head", axis=0, tiled=True)

    def collect_three(values):
        return lax.psum_scatter(
            values.astype(jnp.bfloat16), "head", scatter_dimension=0, tiled=True
        ).astype(jnp.float32)

    def spread_four(values):
        return lax.all_gather(values, "head", axis=0, tiled=True)

    def collect_four(values):
        return lax.psum_scatter(
            values.astype(jnp.bfloat16), "head", scatter_dimension=0, tiled=True
        ).astype(jnp.float32)

    movers = (
        spread_one,
        collect_one,
        spread_two,
        collect_two,
        spread_three,
        collect_three,
        spread_four,
        collect_four,
    )
    own_heads = local_cols // HD
    radius = lax.dynamic_slice_in_dim(kernel_radius, head_index * own_heads, own_heads)
    col_start = head_index * local_cols
    head_local = lax.dynamic_slice_in_dim(head_params[: TAPS + 3], col_start, local_cols, 1)
    up_bias = lax.dynamic_slice_in_dim(bias_flat, head_index * hidden_cols, hidden_cols)
    output, input_grad, mats, head_part, bias_grad, rep_grad = block_pass(
        block_input, out_grad, shards, head_local, up_bias, rep_params, tap_mask(radius), movers
    )
    head_block = lax.dynamic_update_slice_in_dim(
        jnp.zeros((TAPS + 3, full_width), jnp.float32), head_part, col_start, 1
    )
    bias_block = lax.dynamic_update_slice_in_dim(
        jnp.zeros(bias_flat.shape, jnp.float32), bias_grad, head_index * hidden_cols, 0
    )
    head_full = jnp.concatenate([head_block, bias_block.reshape(-1, full_width)], axis=0)
    qkv_raw, proj_raw, up_raw, down_raw = (
        sum_at_owner(mats[0].astype(jnp.bfloat16), "dp", 0),
        sum_at_owner(mats[1].astype(jnp.bfloat16), "dp", 0),
        sum_at_owner(mats[2].astype(jnp.bfloat16), "dp", 0),
        sum_at_owner(mats[3].astype(jnp.bfloat16), "dp", 0),
    )
    partial_sum = (
        square_sum(qkv_raw) + square_sum(proj_raw) + square_sum(up_raw) + square_sum(down_raw)
    )
    rep_sum, head_sum, mat_total = lax.psum((rep_grad, head_full, partial_sum), ("dp", "head"))
    total = mat_total + square_sum(head_sum) + square_sum(rep_sum)
    grad_norm = jnp.sqrt(total)
    scale_clip = jnp.minimum(1.0, CLIP_NORM / (grad_norm + 1e-06))
    qkv_out = adam_step(
        qkv_raw, qkv_weight, qkv_first, qkv_second, qkv_average, scale_clip, WEIGHT_DECAY
    )
    proj_out = adam_step(
        proj_raw, proj_weight, proj_first, proj_second, proj_average, scale_clip, WEIGHT_DECAY
    )
    up_out = adam_step(up_raw, up_weight, up_first, up_second, up_average, scale_clip, WEIGHT_DECAY)
    down_out = adam_step(
        down_raw, down_weight, down_first, down_second, down_average, scale_clip, WEIGHT_DECAY
    )
    head_out = adam_step(
        head_sum, head_params, head_first, head_second, head_average, scale_clip, 0.0
    )
    rep_out = adam_step(rep_sum, rep_params, rep_first, rep_second, rep_average, scale_clip, 0.0)
    return (
        output,
        input_grad,
        grad_norm,
        qkv_out[0],
        qkv_out[1],
        qkv_out[2],
        qkv_out[3],
        qkv_out[4],
        qkv_out[5],
        proj_out[0],
        proj_out[1],
        proj_out[2],
        proj_out[3],
        proj_out[4],
        proj_out[5],
        up_out[0],
        up_out[1],
        up_out[2],
        up_out[3],
        up_out[4],
        up_out[5],
        down_out[0],
        down_out[1],
        down_out[2],
        down_out[3],
        down_out[4],
        down_out[5],
        head_out[0],
        head_out[1],
        head_out[2],
        head_out[3],
        head_out[4],
        head_out[5],
        rep_out[0],
        rep_out[1],
        rep_out[2],
        rep_out[3],
        rep_out[4],
        rep_out[5],
    )


def solution(mesh):
    placed = (
        P(("dp", "head"), None, None),
        P(("dp", "head"), None, None),
        P(),
        P("dp", None, "head"),
        P("dp", None, "head"),
        P("dp", None, "head"),
        P("dp", None, "head"),
        P("dp", "head"),
        P("dp", "head"),
        P("dp", "head"),
        P("dp", "head"),
        P("dp", "head"),
        P("dp", "head"),
        P("dp", "head"),
        P("dp", "head"),
        P("dp", "head"),
        P("dp", "head"),
        P("dp", "head"),
        P("dp", "head"),
        P(),
        P(),
        P(),
        P(),
        P(),
        P(),
        P(),
        P(),
    )
    return jax.shard_map(
        per_device,
        mesh=mesh,
        in_specs=placed,
        out_specs=(
            P(("dp", "head"), None, None),
            P(("dp", "head"), None, None),
            P(),
            P("dp", None, "head"),
            P("dp", None, "head"),
            P("dp", None, "head"),
            P("dp", None, "head"),
            P("dp", None, "head"),
            P("dp", None, "head"),
            P("dp", "head"),
            P("dp", "head"),
            P("dp", "head"),
            P("dp", "head"),
            P("dp", "head"),
            P("dp", "head"),
            P("dp", "head"),
            P("dp", "head"),
            P("dp", "head"),
            P("dp", "head"),
            P("dp", "head"),
            P("dp", "head"),
            P("dp", "head"),
            P("dp", "head"),
            P("dp", "head"),
            P("dp", "head"),
            P("dp", "head"),
            P("dp", "head"),
            P(),
            P(),
            P(),
            P(),
            P(),
            P(),
            P(),
            P(),
            P(),
            P(),
            P(),
            P(),
        ),
        check_vma=False,
    )
```

profile of v0, /device:TPU:0, one launch (start us, length us, event | category | flops | bytes accessed | tf_op | source)
XLA Modules:
  0.0 946.8 jit_solution(7037899556073971517)
XLA Ops:
  14.3 10.7 %all_gather.26 = bf16[512,128]{1,0:T(8,128)(2,1)S(1)} all-gather(bf16[64,128]{1,0:T(8,128)(2,1)S(1)} %convert_element_type.132), channel_id=1, replica_groups=mesh['dp'=8,'head'=4] {'dp'}, dimensions={0}, use_global_device_ids=true | all-gather | bytes 147456 | tf_op jit(solution)/shard_map/all_gather | solution.py:307
  24.9 9.5 %all_gather.25 = bf16[512,3,128]{2,0,1:T(8,128)(2,1)S(1)} all-gather(bf16[64,3,128]{2,0,1:T(8,128)(2,1)S(1)} %convert_element_type.130), channel_id=1, replica_groups=mesh['dp'=8,'head'=4] {'dp'}, dimensions={0}, use_global_device_ids=true | all-gather | bytes 442368 | tf_op jit(solution)/shard_map/all_gather | solution.py:306
  38.4 43.9 %all-gather.5.cloned.1.call-done = bf16[64,50,512]{2,0,1:T(8,128)(2,1)} async-done(((bf16[16,50,512]{2,0,1:T(8,128)(2,1)}), bf16[64,50,512]{2,0,1:T(8,128)(2,1)}) %all-gather.5.cloned.1.call-update) | async-done | bytes 3276816 | tf_op jit(solution)/shard_map/all_gather | solution.py:318
  107.9 14.7 %fusion.20 = f32[64,2,64,64]{3,2,1,0:T(8,128)S(1)} fusion(f32[64,50,2,64]{3,2,0,1:T(2,128)} %reshape_squeeze.6, f32[64,50,2,64]{3,2,0,1:T(2,128)} %squeeze.11, f32[64,2,64]{2,1,0:T(2,128)} %div.131, f32[64,2,64]{2,1,0:T(2,128)} %sub.109), kind=kOutput, calls=%fused_computation.150 | convolution fusion | flops 315392000 | bytes 5439488 | tf_op jit(solution)/shard_map/bnhi,bnhj->bhij/dot_general | solution.py:152
  124.6 8.1 multiply_bitcast_fusion.1
  140.7 9.8 %add_add_fusion.1 = f32[64,7,7,128]{3,0,2,1:T(8,128)S(1)} fusion(f32[64,7,7,128]{3,0,2,1:T(8,128)S(1)} %bitcast.339, f32[128]{0:T(128)} %get-tuple-element.157, f32[128]{0:T(128)S(1)} %get-tuple-element.177, f32[128]{0:T(128)S(1)} %get-tuple-element.178, f32[128]{0:T(128)S(1)} %get-tuple-element.179, f32[128]{0:T(128)S(1)} %get-tuple-element.180, ...), kind=kLoop, calls=%fused_computation.377 | loop fusion | flops 39337984 | bytes 3236864 | tf_op jit(solution)/shard_map/add | solution.py:158
  156.6 61.2 %reduce-scatter.5.cloned.1.call-done = bf16[16,50,512]{2,0,1:T(8,128)(2,1)} async-done(((bf16[64,50,512]{2,0,1:T(8,128)(2,1)}), bf16[16,50,512]{2,0,1:T(8,128)(2,1)}) %reduce-scatter.5.cloned.1.call-update) | async-done | bytes 819216 | tf_op jit(solution)/shard_map/reduce_scatter | solution.py:321
  225.3 11.7 %all_gather.28 = bf16[512,512]{1,0:T(8,128)(2,1)} all-gather(bf16[64,512]{1,0:T(8,128)(2,1)} %convert_element_type.136), channel_id=1, replica_groups=mesh['dp'=8,'head'=4] {'dp'}, dimensions={0}, use_global_device_ids=true | all-gather | bytes 589824 | tf_op jit(solution)/shard_map/all_gather | solution.py:308
  236.9 10.8 %all_gather.29 = bf16[512,512]{1,0:T(8,128)(2,1)} all-gather(bf16[64,512]{1,0:T(8,128)(2,1)} %convert_element_type.138), channel_id=1, replica_groups=mesh['dp'=8,'head'=4] {'dp'}, dimensions={0}, use_global_device_ids=true | all-gather | bytes 589824 | tf_op jit(solution)/shard_map/all_gather | solution.py:309
  247.7 38.8 %all-gather.7.cloned.1.call-done = bf16[64,50,512]{2,0,1:T(8,128)(2,1)} async-done(((bf16[16,50,512]{2,0,1:T(8,128)(2,1)}), bf16[64,50,512]{2,0,1:T(8,128)(2,1)}) %all-gather.7.cloned.1.call-update) | async-done | bytes 3276816 | tf_op jit(solution)/shard_map/all_gather | solution.py:326
  286.5 19.0 %multiply_convert_fusion = (bf16[64,50,512]{2,0,1:T(8,128)(2,1)}, f32[64,50,512]{2,0,1:T(8,128)}, f32[64,50,512]{2,0,1:T(8,128)}) fusion(f32[512]{0:T(512)S(1)} %dynamic_slice.11, bf16[64,50,512]{2,0,1:T(8,128)(2,1)} %all-gather.7.cloned.1.call-done, bf16[512,512]{1,0:T(8,128)(2,1)} %all_gather.28), kind=kOutput, calls=%fused_computation.101 | convolution fusion | flops 1785856000 | bytes 20187136 | tf_op jit(solution)/shard_map/bnd,df->bnf/dot_general | solution.py:170
  305.5 46.7 %all-gather.9.cloned.1.call-done = bf16[64,50,512]{2,0,1:T(8,128)(2,1)} async-done(((bf16[16,50,512]{2,0,1:T(8,128)(2,1)}), bf16[64,50,512]{2,0,1:T(8,128)(2,1)}) %all-gather.9.cloned.1.call-update) | async-done | bytes 3276816 | tf_op jit(solution)/shard_map/all_gather | solution.py:334
  352.2 10.2 %convert_reduce_fusion = (f32[512]{0:T(512)S(1)}, bf16[64,50,512]{2,0,1:T(8,128)(2,1)S(1)}) fusion(f32[64,50,512]{2,0,1:T(8,128)} %get-tuple-element.143, bf16[64,50,512]{2,0,1:T(8,128)(2,1)} %all-gather.9.cloned.1.call-done, bf16[512,512]{1,0:T(8,128)(2,1)} %all_gather.29, f32[64,50,512]{2,0,1:T(8,128)} %get-tuple-element.227, f32[512]{0:T(512)S(1)} %dynamic_slice.11), kind=kOutput, calls=%fused_computation.99 | convolution fusion | flops 1705573888 | bytes 20189184 | tf_op jit(solution)/shard_map/bnd,df->bnf/dot_general | solution.py:179
  367.9 61.2 %reduce-scatter.9.cloned.1.call-done = bf16[16,50,512]{2,0,1:T(8,128)(2,1)} async-done(((bf16[64,50,512]{2,0,1:T(8,128)(2,1)}), bf16[16,50,512]{2,0,1:T(8,128)(2,1)}) %reduce-scatter.9.cloned.1.call-update) | async-done | bytes 819216 | tf_op jit(solution)/shard_map/reduce_scatter | solution.py:337
  434.3 65.0 %all-gather.11.cloned.1.call-done = bf16[64,50,512]{2,0,1:T(8,128)(2,1)} async-done(((bf16[16,50,512]{2,0,1:T(8,128)(2,1)}), bf16[64,50,512]{2,0,1:T(8,128)(2,1)}) %all-gather.11.cloned.1.call-update) | async-done | bytes 3276816 | tf_op jit(solution)/shard_map/all_gather | solution.py:342
  518.0 13.5 %multiply_bitcast_fusion = f32[64,50,2,64]{3,1,2,0:T(8,128)} fusion(f32[64,2,64,64]{3,2,1,0:T(8,128)} %copy-done.8, f32[64,50,2,64]{3,2,0,1:T(2,128)} %reshape.274), kind=kOutput, calls=%fused_computation.140 | convolution fusion | flops 314982400 | bytes 5373952 | tf_op jit(solution)/shard_map/bnhj,bhij->bnhi/dot_general | solution.py:194
  531.9 10.9 %fusion.12 = f32[64,2,64,64]{3,2,1,0:T(8,128)S(1)} fusion(f32[64,50,2,64]{3,2,0,1:T(2,128)S(1)} %copy-done.6, f32[64,50,2,64]{3,2,0,1:T(2,128)S(1)} %copy-done.5), kind=kOutput, calls=%fused_computation.142 | convolution fusion | flops 314572800 | bytes 5373952 | tf_op jit(solution)/shard_map/bnhi,bnhj->bhij/dot_general | solution.py:198
  543.2 9.8 %fusion.165 = f32[64,7,7,128]{3,0,2,1:T(8,128)} fusion(f32[64,7,7,128]{3,0,2,1:T(8,128)S(1)} %bitcast.338, f32[128]{0:T(128)S(1)} %copy-done.117, f32[128]{0:T(128)S(1)} %copy-done.119, f32[128]{0:T(128)S(1)} %copy-done.121, f32[128]{0:T(128)S(1)} %copy-done.123, f32[128]{0:T(128)S(1)} %copy-done.125, f32[128]{0:T(128)S(1)} %copy-done.127, ...), kind=kLoop, calls=%fused_computation.309 | loop fusion | flops 38936576 | bytes 3236352 | tf_op jit(solution)/shard_map/add | solution.py:71
  553.0 12.7 %multiply_reduce_fusion = (f32[64,2,64]{2,1,0:T(2,128)}, f32[64,50,2,64]{3,1,2,0:T(8,128)}) fusion(f32[64,2,64]{2,1,0:T(2,128)S(1)} %copy-done.68, f32[64,2,64]{2,1,0:T(2,128)S(1)} %copy-done.67, f32[64,50,2,64]{3,2,0,1:T(2,128)S(1)} %copy-done.25, f32[64,50,2,64]{3,2,0,1:T(2,128)S(1)} %copy-done.26, f32[64,2,64,64]{3,2,1,0:T(8,128)S(1)} %fusion.12), kind=kOutput, calls=%fused_computation.139 | convolution fusion | flops 316727296 | bytes 7110656 | tf_op jit(solution)/shard_map/bnhj,bhij->bnhi/dot_general | solution.py:201
  565.8 10.2 %fusion.45 = f32[64,50,2,64]{3,1,2,0:T(8,128)} fusion(f32[64,2,64,64]{3,2,1,0:T(8,128)S(1)} %fusion.12, f32[64,50,2,64]{3,2,0,1:T(2,128)S(1)} %copy-done.25, f32[64,2,64]{2,1,0:T(2,128)S(1)} %copy-done.68, f32[64,2,64]{2,1,0:T(2,128)S(1)} %copy-done.67), kind=kOutput, calls=%fused_computation.178 | convolution fusion | flops 315916288 | bytes 5439488 | tf_op jit(solution)/shard_map/bnhi,bhij->bnhj/dot_general | solution.py:204
  682.4 57.1 %all-reduce.10.cloned.1.call-done = f32[56,512]{1,0:T(8,128)} async-done(((f32[56,512]{1,0:T(8,128)}), f32[56,512]{1,0:T(8,128)}) %all-reduce.10.cloned.1.call-update) | async-done | bytes 114704 | tf_op jit(solution)/shard_map/psum | solution.py:383
  748.2 57.0 %reduce-scatter.11.cloned.1.call-done = bf16[16,50,512]{2,0,1:T(8,128)(2,1)} async-done(((bf16[64,50,512]{2,0,1:T(8,128)(2,1)}), bf16[16,50,512]{2,0,1:T(8,128)(2,1)}) %reduce-scatter.11.cloned.1.call-update) | async-done | bytes 819216 | tf_op jit(solution)/shard_map/reduce_scatter | solution.py:345
  809.1 60.9 %reduce-scatter.7.cloned.1.call-done = bf16[16,50,512]{2,0,1:T(8,128)(2,1)} async-done(((bf16[64,50,512]{2,0,1:T(8,128)(2,1)}), bf16[16,50,512]{2,0,1:T(8,128)(2,1)}) %reduce-scatter.7.cloned.1.call-update) | async-done | bytes 819216 | tf_op jit(solution)/shard_map/reduce_scatter | solution.py:329
  884.1 40.5 %all-reduce.7 = (f32[]{:T(128)}, f32[16,512]{1,0:T(8,128)S(1)}) all-reduce(f32[]{:T(128)S(6)} %add.776, f32[16,512]{1,0:T(8,128)S(1)} %concatenate.32), channel_id=1, replica_groups=mesh['dp'=8,'head'=4] {'dp','head'}, use_global_device_ids=true, to_apply=%region_23.24 | all-reduce | flops 8193 | bytes 65544 | tf_op jit(solution)/shard_map/psum | solution.py:383
  (499 shorter events, 230.9 us)
Async XLA Ops:
  7.2 75.1 %all-gather.5.cloned.1.call-start = ((), (), s32[]{:S(2)}) async-start(), calls=%async_computation.8 | async-start | bytes 4096000 | tf_op jit(solution)/shard_map/all_gather | solution.py:318
  13.8 203.9 %reduce-scatter.5.cloned.1.call-start = ((), (), s32[]{:S(2)}) async-start(), calls=%async_computation.9 | async-start | bytes 4096000 | tf_op jit(solution)/shard_map/reduce_scatter | solution.py:321
  37.0 103.5 %copy-start.94 = (f32[128]{0:T(128)}, f32[128]{0:T(128)S(1)}, u32[]{:S(2)}) copy-start(f32[128]{0:T(128)S(1)} %get-tuple-element.215) | copy-start | bytes 1540
  37.0 103.5 %copy-start.96 = (f32[128]{0:T(128)}, f32[128]{0:T(128)S(1)}, u32[]{:S(2)}) copy-start(f32[128]{0:T(128)S(1)} %get-tuple-element.216) | copy-start | bytes 1540
  37.0 103.5 %copy-start.98 = (f32[128]{0:T(128)}, f32[128]{0:T(128)S(1)}, u32[]{:S(2)}) copy-start(f32[128]{0:T(128)S(1)} %get-tuple-element.217) | copy-start | bytes 1540
  37.0 103.5 %copy-start.100 = (f32[128]{0:T(128)}, f32[128]{0:T(128)S(1)}, u32[]{:S(2)}) copy-start(f32[128]{0:T(128)S(1)} %get-tuple-element.218) | copy-start | bytes 1540
  37.0 103.5 %copy-start.102 = (f32[128]{0:T(128)}, f32[128]{0:T(128)S(1)}, u32[]{:S(2)}) copy-start(f32[128]{0:T(128)S(1)} %get-tuple-element.219) | copy-start | bytes 1540
  37.0 103.5 %copy-start.104 = (f32[128]{0:T(128)}, f32[128]{0:T(128)S(1)}, u32[]{:S(2)}) copy-start(f32[128]{0:T(128)S(1)} %get-tuple-element.220) | copy-start | bytes 1540
  37.1 103.5 %copy-start.106 = (f32[128]{0:T(128)}, f32[128]{0:T(128)S(1)}, u32[]{:S(2)}) copy-start(f32[128]{0:T(128)S(1)} %get-tuple-element.221) | copy-start | bytes 1540
  156.5 130.0 %all-gather.7.cloned.1.call-start = ((), (), s32[]{:S(2)}) async-start(), calls=%async_computation.10 | async-start | bytes 4096000 | tf_op jit(solution)/shard_map/all_gather | solution.py:326
  219.2 212.7 %copy-start.32 = (f32[16,50]{0,1:T(8,128)}, f32[16,50]{0,1:T(8,128)S(1)}, u32[]{:S(2)}) copy-start(f32[16,50]{0,1:T(8,128)S(1)} %broadcast_multiply_fusion.10) | copy-start | bytes 9604
  219.5 212.3 %copy-start.35 = (f32[16,50]{0,1:T(8,128)}, f32[16,50]{0,1:T(8,128)S(1)}, u32[]{:S(2)}) copy-start(f32[16,50]{0,1:T(8,128)S(1)} %add_rsqrt_fusion) | copy-start | bytes 9604
  220.8 131.4 %all-gather.9.cloned.1.call-start = ((), (), s32[]{:S(2)}) async-start(), calls=%async_computation.12 | async-start | bytes 4096000 | tf_op jit(solution)/shard_map/all_gather | solution.py:334
  221.4 207.7 %reduce-scatter.9.cloned.1.call-start = ((), (), s32[]{:S(2)}) async-start(), calls=%async_computation.13 | async-start | bytes 4096000 | tf_op jit(solution)/shard_map/reduce_scatter | solution.py:337
  367.8 131.5 %all-gather.11.cloned.1.call-start = ((), (), s32[]{:S(2)}) async-start(), calls=%async_computation.14 | async-start | bytes 4096000 | tf_op jit(solution)/shard_map/all_gather | solution.py:342
  433.6 306.0 %all-reduce.10.cloned.1.call-start = ((), (), s32[]{:S(2)}) async-start(), calls=%async_computation.16 | async-start | bytes 229376 | tf_op jit(solution)/shard_map/psum | solution.py:383
  618.2 187.1 %reduce-scatter.11.cloned.1.call-start = ((), (), s32[]{:S(2)}) async-start(), calls=%async_computation.15 | async-start | bytes 4096000 | tf_op jit(solution)/shard_map/reduce_scatter | solution.py:345
  623.6 246.5 %reduce-scatter.7.cloned.1.call-start = ((), (), s32[]{:S(2)}) async-start(), calls=%async_computation.11 | async-start | bytes 4096000 | tf_op jit(solution)/shard_map/reduce_scatter | solution.py:329
  635.2 13.9 %all-to-all-start.2 = ((bf16[8,64,512]{2,1,0:T(8,128)(2,1)}), bf16[8,64,512]{2,1,0:T(8,128)(2,1)}, u32[]{:S(2)}, u32[]{:S(2)}) async-start(bf16[8,64,512]{2,1,0:T(8,128)(2,1)} %bitcast.349), calls=%async_computation.6 | async-start | bytes 1048576 | tf_op jit(solution)/shard_map/all_to_all | solution.py:33
  649.1 13.9 %all-to-all-start.3 = ((bf16[8,64,512]{2,1,0:T(8,128)(2,1)}), bf16[8,64,512]{2,1,0:T(8,128)(2,1)}, u32[]{:S(2)}, u32[]{:S(2)}) async-start(bf16[8,64,512]{2,1,0:T(8,128)(2,1)} %bitcast.348), calls=%async_computation.7 | async-start | bytes 1048576 | tf_op jit(solution)/shard_map/all_to_all | solution.py:33
  668.6 9.5 %all-to-all-start.1 = ((bf16[8,64,128]{2,1,0:T(8,128)(2,1)}), bf16[8,64,128]{2,1,0:T(8,128)(2,1)}, u32[]{:S(2)}, u32[]{:S(2)}) async-start(bf16[8,64,128]{2,1,0:T(8,128)(2,1)} %bitcast.353), calls=%async_computation.5 | async-start | bytes 262144 | tf_op jit(solution)/shard_map/all_to_all | solution.py:33
  677.1 128.1 %copy-start.74 = (f32[1,512]{1,0:T(1,128)S(1)}, f32[1,512]{1,0:T(1,128)}, u32[]{:S(2)}) copy-start(f32[1,512]{1,0:T(1,128)} %copy-done.73) | copy-start | bytes 6148
  678.1 65.2 %all-to-all-start = ((bf16[8,64,3,128]{3,1,2,0:T(8,128)(2,1)}), bf16[8,64,3,128]{3,1,2,0:T(8,128)(2,1)}, u32[]{:S(2)}, u32[]{:S(2)}) async-start(bf16[8,64,3,128]{3,1,2,0:T(8,128)(2,1)} %copy.94), calls=%async_computation.4 | async-start | bytes 786432 | tf_op jit(solution)/shard_map/all_to_all | solution.py:33
  743.3 126.7 %copy-start.93 = (f32[1,512]{1,0:T(1,128)S(1)}, f32[1,512]{1,0:T(1,128)}, u32[]{:S(2)}) copy-start(f32[1,512]{1,0:T(1,128)} %get-tuple-element.160) | copy-start | bytes 6148
  (166 other events, 3055.9 us)
Sparse Core Ops, SparseCore 0:
  13.9 68.3 all-gather.4
  156.6 61.0 reduce-scatter.4
  220.9 65.5 all-gather.6
  288.0 64.2 all-gather.8
  368.0 61.0 reduce-scatter.8
  433.7 65.5 all-gather.10
  618.3 121.2 all-reduce.9
  741.9 63.2 reduce-scatter.10
  807.5 62.4 reduce-scatter.6
where the time goes:
time: 955 us; the launch traced here: 947 us
  waiting for transfers between devices  502 us (53%)
  matrix products  143 us (15%)
  other arithmetic  89.6 us (9%)
  local copies, waits for them, and re-layouts  89.3 us (9%)
  blocking collectives  83.2 us (9%)
  between operations  22.2 us (2%)
  starting transfers between devices  17.2 us (2%)
    all_gather x1, waiting for transfers between devices, spread_four(): return lax.all_gather(values, 'head', axis=0, tiled=True)  65 us
    reduce_scatter x1, waiting for transfers between devices, collect_three(): lax.psum_scatter(values.astype(jnp.bfloat16), 'head', scatter_dimension=0...  61.2 us
    reduce_scatter x1, waiting for transfers between devices, collect_one(): lax.psum_scatter(values.astype(jnp.bfloat16), 'head', scatter_dimension=0...  61.2 us
    reduce_scatter x1, waiting for transfers between devices, collect_two(): lax.psum_scatter(values.astype(jnp.bfloat16), 'head', scatter_dimension=0...  60.9 us
    psum x1, waiting for transfers between devices, per_device(): lax.psum((rep_grad, head_full, partial_sum), ('dp', 'head'))  57.1 us
    reduce_scatter x1, waiting for transfers between devices, collect_four(): lax.psum_scatter(values.astype(jnp.bfloat16), 'head', scatter_dimension=0...  57 us
    all_gather x1, waiting for transfers between devices, spread_three(): return lax.all_gather(values, 'head', axis=0, tiled=True)  46.7 us
    all_gather x1, waiting for transfers between devices, spread_one(): return lax.all_gather(values, 'head', axis=0, tiled=True)  43.9 us
  transfers between devices with their start and end apart: 13, of which 12 were waited for; matrix products, arithmetic and copies ran while one was open for 8% of the time, Pallas kernels for 0%

commit v1 on v0

v1 whole, which is shorter than its diff:
```python
from functools import partial

import jax
import jax.numpy as jnp
from jax import lax
from jax.experimental import pallas as pl
from jax.experimental.pallas import tpu as pltpu
from jax.sharding import PartitionSpec as P

HD = 64
GRID = 7
TAPS = 49
STEP = 5
SEQ = 50
LANE = 128
PAD_TOKENS = 64

NORM_EPS = 1e-06
BETA_FIRST = 0.9
BETA_SECOND = 0.999
ADAM_EPS = 1e-08
LEARN_RATE = 0.1
WEIGHT_DECAY = 0.05
CLIP_NORM = 1.0
AVG_KEEP = 0.9
F32 = jnp.float32
BF16 = jnp.bfloat16

NN = (((1,), (0,)), ((), ()))
NT = (((1,), (1,)), ((), ()))
TN = (((0,), (0,)), ((), ()))


def dot(left, right, dims=NN):
    return lax.dot_general(left, right, dims, preferred_element_type=F32)


def rows_at(start, size):
    return pl.ds(pl.multiple_of(start, 16), size)


def norm_parts(values):
    center = values - jnp.mean(values, axis=-1, keepdims=True)
    inv = lax.rsqrt(jnp.mean(center * center, axis=-1, keepdims=True) + NORM_EPS)
    return center * inv, inv


def norm_back(grad, gain, unit, inv):
    scaled = grad * gain
    mean_one = jnp.mean(scaled, axis=-1, keepdims=True)
    mean_two = jnp.mean(scaled * unit, axis=-1, keepdims=True)
    return inv * (scaled - mean_one - unit * mean_two)


def conv_row(src, taps, reach, y, cols, imgs, flip):
    side = 2 * reach + 1
    acc = [None] * GRID
    for a in range(side):
        start = (y + a) * (GRID * imgs)
        vals = [src[rows_at(start + x * imgs, imgs), cols] for x in range(GRID)]
        for b in range(side):
            t = a * side + b
            tap = taps[side * side - 1 - t if flip else t]
            for x in range(GRID):
                other = x + b - reach
                if 0 <= other < GRID:
                    term = tap * vals[other]
                    acc[x] = term if acc[x] is None else acc[x] + term
    return acc


def tap_products(src, grad_row, y, reach, cols, imgs, a, accs):
    side = 2 * reach + 1
    start = (y + a) * (GRID * imgs)
    vals = [src[rows_at(start + x * imgs, imgs), cols] for x in range(GRID)]
    out = []
    for b in range(side):
        acc = accs[b]
        for x in range(GRID):
            other = x + b - reach
            if 0 <= other < GRID:
                acc = acc + grad_row[x] * vals[other]
        out.append(acc)
    return tuple(out)


def pre_kernel(x_ref, og_ref, rp_ref, s0_ref, n1_ref, xp_ref, ogp_ref, ogsum_ref, xs, os):
    imgs, _, width = x_ref.shape
    row = GRID * imgs
    base = row - imgs
    rows = SEQ * imgs
    tiles = width // LANE
    for c in range(tiles):
        cols = slice(c * LANE, (c + 1) * LANE)
        xs[c, 0:row] = jnp.zeros((row, LANE), F32)
        xs[c, 8 * row : 9 * row] = jnp.zeros((row, LANE), F32)
        for i in range(imgs):
            xs[c, pl.ds(base + i, SEQ, stride=imgs), :] = x_ref[i, :, cols].astype(F32)
            os[c, pl.ds(i, SEQ, stride=imgs), :] = og_ref[i, :, cols].astype(F32)
        xp_ref[:, cols] = xs[c, base : base + rows].astype(BF16)
        ogp_ref[:, cols] = os[c].astype(BF16)
        ogsum_ref[:, cols] = jnp.broadcast_to(jnp.sum(os[c], axis=0, keepdims=True), (8, LANE))
        s0_ref[0:imgs, cols] = xs[c, base : base + imgs]
        xs[c, base : base + imgs] = jnp.zeros((imgs, LANE), F32)

    def conv_body(y, carry):
        for c in range(tiles):
            cols = slice(c * LANE, (c + 1) * LANE)
            taps = [rp_ref[t : t + 1, cols] for t in range(9)]
            acc = conv_row(xs.at[c], taps, 1, y, slice(None), imgs, False)
            for x in range(GRID):
                here = xs[c, rows_at((y + 1) * row + x * imgs, imgs)]
                s0_ref[rows_at(imgs + y * row + x * imgs, imgs), cols] = (
                    here + acc[x] + rp_ref[9:10, cols]
                )
        return carry

    lax.fori_loop(0, GRID, conv_body, 0)
    step = 5 * imgs

    def norm_body(r, carry):
        at = rows_at(r * step, step)
        unit, _ = norm_parts(s0_ref[at, :])
        n1_ref[at, :] = (unit * rp_ref[10:11] + rp_ref[11:12]).astype(BF16)
        return carry

    lax.fori_loop(0, rows // step, norm_body, 0)


def head_block_mask(scale):
    row = lax.broadcasted_iota(jnp.int32, (LANE, LANE), 0) // HD
    col = lax.broadcasted_iota(jnp.int32, (LANE, LANE), 1) // HD
    return jnp.where(row == col, F32(scale), F32(0.0))


def joined(refs, cols):
    return jnp.concatenate([ref[0, :, cols] for ref in refs], axis=0)


def attn_kernel(*refs, imgs, nblk):
    _, n1, s0 = refs[:3]
    w = refs[3 : 3 + nblk]
    hp, rp, q_o, k_o, v_o, cv_o, at_o, s1_o, n2_o, qs, ks, vs, fs, vp = refs[3 + nblk :]
    j = pl.program_id(0)
    rows = SEQ * imgs
    grid_row = GRID * imgs
    first = (3 * GRID - 1) * imgs

    @pl.when(j == 0)
    def _():
        for ref in (qs, ks, vs):
            ref[rows:] = jnp.zeros((ref.shape[0] - rows, LANE), F32)
        vp[0:first] = jnp.zeros((first, LANE), F32)
        vp[first + rows :] = jnp.zeros((vp.shape[0] - first - rows, LANE), F32)
        s1_o[...] = s0[...] + rp[14:15]

    wq = joined(w, slice(0, 3 * LANE))
    chunk = 10 * imgs
    for r in range(0, rows, chunk):
        qkv = dot(n1[r : r + chunk], wq)
        q = qkv[:, 0:LANE] + hp[50:51]
        qs[r : r + chunk] = q
        q_o[0, r : r + chunk] = q
        ks[r : r + chunk] = qkv[:, LANE : 2 * LANE]
        v = qkv[:, 2 * LANE :] + hp[51:52]
        vs[r : r + chunk] = v
        v_o[0, r : r + chunk] = v
        vp[first + r : first + r + chunk] = v
    vp[first : first + imgs] = jnp.zeros((imgs, LANE), F32)
    keys = ks[0:rows].reshape(SEQ, imgs, LANE)
    expo = jnp.exp(keys - jnp.max(keys, axis=0, keepdims=True))
    soft = (expo / jnp.sum(expo, axis=0, keepdims=True)).reshape(rows, LANE)
    ks[0:rows] = soft
    k_o[0] = soft
    scale = head_block_mask(HD**-0.5)

    def image_body(i, carry):
        at = pl.ds(i, PAD_TOKENS, stride=imgs)
        ctx = dot(ks[at, :].astype(BF16), vs[at, :].astype(BF16), TN) * scale
        fs[at, :] = dot(qs[at, :].astype(BF16), ctx.astype(BF16))
        return carry

    lax.fori_loop(0, imgs, image_body, 0, unroll=4)
    at_o[0, 0:imgs] = fs[0:imgs].astype(BF16)
    cv_o[0, 0:imgs] = jnp.zeros((imgs, LANE), F32)
    everything = slice(0, LANE)

    def conv_body(y, carry):
        taps = [hp[t : t + 1] for t in range(TAPS)]
        acc = conv_row(vp, taps, 3, y, everything, imgs, False)
        for x in range(GRID):
            at = rows_at(imgs + y * grid_row + x * imgs, imgs)
            value = acc[x] + hp[49:50]
            cv_o[0, at] = value
            at_o[0, at] = (fs[at] + qs[at] * value).astype(BF16)
        return carry

    lax.fori_loop(0, GRID, conv_body, 0)
    s1_o[...] += dot(at_o[0], joined(w, slice(3 * LANE, 4 * LANE)), NT)

    @pl.when(j == pl.num_programs(0) - 1)
    def _():
        step = 5 * imgs

        def norm_body(r, carry):
            at = rows_at(r * step, step)
            unit, _ = norm_parts(s1_o[at, :])
            n2_o[at, :] = (unit * rp[12:13] + rp[13:14]).astype(BF16)
            return carry

        lax.fori_loop(0, rows // step, norm_body, 0)


def mlp_kernel(*refs, imgs, nblk, hid):
    slots, n2, og, s1 = refs[:4]
    w = refs[4 : 4 + nblk]
    ub, rp, out_o, g_o, gal_o, gs1_o, ubg_o, rep_o, hs, ds, hb, gb, oacc, dacc, tile = refs[4 + nblk :]
    j = pl.program_id(0)
    nh = pl.num_programs(0)
    rows = SEQ * imgs
    wu = joined(w, slice(0, hid))
    wd = joined(w, slice(hid, 2 * hid))
    hs[...] = dot(n2[...], wu) + ub[0]
    ds[...] = dot(og[...], wd)
    step = 2 * imgs

    def gelu_body(r, total):
        at = rows_at(r * step, step)
        pre = hs[at, :]
        cdf = 0.5 * (1.0 + lax.erf(pre * F32(0.5**0.5)))
        pdf = jnp.exp(-0.5 * pre * pre) * F32(0.3989422804014327)
        hb[at, :] = (pre * cdf).astype(BF16)
        grad = (ds[at, :] * (cdf + pre * pdf)).astype(BF16)
        gb[at, :] = grad
        wide = grad.astype(F32).reshape(step // 8, 8, hid)
        return total + jnp.sum(wide, axis=0)

    total = lax.fori_loop(0, rows // step, gelu_body, jnp.zeros((8, hid), F32))
    ubg_o[0] = jnp.broadcast_to(jnp.sum(total, axis=0, keepdims=True), (8, hid))
    out_part = dot(hb[...], wd, NT)
    back_part = dot(gb[...], wu, NT)

    @pl.when(j == 0)
    def _():
        oacc[...] = out_part + s1[...] + rp[15:16]
        dacc[...] = back_part

    @pl.when(j > 0)
    def _():
        oacc[...] += out_part
        dacc[...] += back_part

    up = dot(n2[...], gb[...], TN).astype(BF16)
    down = dot(og[...], hb[...], TN).astype(BF16)
    size = up.shape[0] // nblk
    for d in range(nblk):
        at = slots[nblk * nh + d]
        g_o[at, 0, :, 0:hid] = up[d * size : (d + 1) * size]
        g_o[at, 0, :, hid : 2 * hid] = down[d * size : (d + 1) * size]

    @pl.when(j == nh - 1)
    def _():
        width = oacc.shape[1]
        for c in range(width // LANE):
            cols = slice(c * LANE, (c + 1) * LANE)
            tile[...] = oacc[:, cols]
            for i in range(imgs):
                out_o[i, :, cols] = tile[pl.ds(i, SEQ, stride=imgs), :].astype(BF16)
        part = 5 * imgs

        def back_body(r, sums):
            at = rows_at(r * part, part)
            grad = dacc[at, :]
            unit, inv = norm_parts(s1[at, :])
            one = og[at, :].astype(F32) + norm_back(grad, rp[12:13], unit, inv)
            gs1_o[at, :] = one
            low = one.astype(BF16)
            gal_o[at, :] = low

            def fold(v):
                return jnp.sum(v.reshape(part // 8, 8, width), axis=0)

            return (
                sums[0] + fold(grad * unit),
                sums[1] + fold(grad),
                sums[2] + fold(low.astype(F32)),
            )

        zero = jnp.zeros((8, width), F32)
        sums = lax.fori_loop(0, rows // part, back_body, (zero, zero, zero))
        rep_o[...] = jnp.concatenate(
            [jnp.sum(s, axis=0, keepdims=True) for s in sums] + [jnp.zeros((5, width), F32)], axis=0
        )


def attn_back_kernel(*refs, imgs, nblk):
    slots, n1, gal = refs[:3]
    w = refs[3 : 3 + nblk]
    (hp, q_i, k_i, v_i, cv, at_i, g_o, gn1_o, hg_o) = refs[3 + nblk : 12 + nblk]
    qs, ks, vs, gs, fq, fk, fv, vp, gp, gqkv = refs[12 + nblk :]
    j = pl.program_id(0)
    nh = pl.num_programs(0)
    rows = SEQ * imgs
    grid_row = GRID * imgs
    first = (3 * GRID - 1) * imgs

    @pl.when(j == 0)
    def _():
        for ref in (qs, ks, vs, gs):
            ref[rows:] = jnp.zeros((ref.shape[0] - rows, LANE), F32)
        for ref in (vp, gp):
            ref[0:first] = jnp.zeros((first, LANE), F32)
            ref[first + rows :] = jnp.zeros((ref.shape[0] - first - rows, LANE), F32)

    wp = joined(w, slice(3 * LANE, 4 * LANE))
    chunk = 10 * imgs
    for r in range(0, rows, chunk):
        at = slice(r, r + chunk)
        grad = dot(gal[at], wp)
        gs[at] = grad
        q = q_i[0, at]
        v = v_i[0, at]
        qs[at] = q
        ks[at] = k_i[0, at]
        vs[at] = v
        vp[first + r : first + r + chunk] = v
        gp[first + r : first + r + chunk] = grad * q
    vp[first : first + imgs] = jnp.zeros((imgs, LANE), F32)
    gp[first : first + imgs] = jnp.zeros((imgs, LANE), F32)
    scale = head_block_mask(HD**-0.5)

    def image_body(i, carry):
        at = pl.ds(i, PAD_TOKENS, stride=imgs)
        q = qs[at, :].astype(BF16)
        k = ks[at, :].astype(BF16)
        v = vs[at, :].astype(BF16)
        g = gs[at, :].astype(BF16)
        ctx = (dot(k, v, TN) * scale).astype(BF16)
        gctx = (dot(q, g, TN) * scale).astype(BF16)
        fq[at, :] = dot(g, ctx, NT)
        fk[at, :] = dot(v, gctx, NT)
        fv[at, :] = dot(k, gctx)
        return carry

    lax.fori_loop(0, imgs, image_body, 0, unroll=4)
    soft = ks[0:rows].reshape(SEQ, imgs, LANE)
    gsoft = fk[0:rows].reshape(SEQ, imgs, LANE)
    total = jnp.sum(soft * gsoft, axis=0, keepdims=True)
    gqkv[:, LANE : 2 * LANE] = (soft * (gsoft - total)).reshape(rows, LANE).astype(BF16)
    gquery = (fq[0:rows] + gs[0:rows] * cv[0]).astype(BF16)
    gqkv[:, 0:LANE] = gquery
    everything = slice(0, LANE)
    low = fv[0:imgs].astype(BF16)
    gqkv[0:imgs, 2 * LANE :] = low

    def conv_body(y, carry):
        taps = [hp[t : t + 1] for t in range(TAPS)]
        acc = conv_row(gp, taps, 3, y, everything, imgs, True)
        for x in range(GRID):
            at = rows_at(imgs + y * grid_row + x * imgs, imgs)
            value = (fv[at] + acc[x]).astype(BF16)
            gqkv[at, 2 * LANE :] = value
            carry = carry + value.astype(F32)
        return carry

    value_sum = lax.fori_loop(0, GRID, conv_body, low.astype(F32))
    side = GRID
    zero = jnp.zeros((imgs, LANE), F32)
    for a in range(side):

        def tap_body(y, accs, a=a):
            start = (y + 3) * grid_row
            grad_row = [gp[rows_at(start + x * imgs, imgs)] for x in range(GRID)]
            return tap_products(vp, grad_row, y, 3, everything, imgs, a, accs)

        accs = lax.fori_loop(0, GRID, tap_body, (zero,) * side)
        hg_o[0, a * side : (a + 1) * side] = jnp.concatenate(
            [jnp.sum(acc, axis=0, keepdims=True) for acc in accs], axis=0
        )
    conv_sum = jnp.sum(gp[first : first + rows], axis=0, keepdims=True)
    query_sum = jnp.sum(gquery.astype(F32), axis=0, keepdims=True)
    hg_o[0, 49:50] = conv_sum
    hg_o[0, 50:51] = query_sum
    hg_o[0, 51:52] = jnp.sum(value_sum, axis=0, keepdims=True)
    hg_o[0, 52:56] = jnp.zeros((4, LANE), F32)
    part = dot(gqkv[...], joined(w, slice(0, 3 * LANE)), NT)

    @pl.when(j == 0)
    def _():
        gn1_o[...] = part

    @pl.when(j > 0)
    def _():
        gn1_o[...] += part

    wide = dot(n1[...], gqkv[...], TN).astype(BF16)
    proj = dot(gal[...], at_i[0], TN).astype(BF16)
    size = wide.shape[0] // nblk
    for d in range(nblk):
        at = slots[nblk * nh + d]
        g_o[at, 0, :, 0 : 3 * LANE] = wide[d * size : (d + 1) * size]
        g_o[at, 0, :, 3 * LANE :] = proj[d * size : (d + 1) * size]


def tail_kernel(s0, gs1, gn1, xp, rp, ig_o, rep_o, gz, xs, res):
    imgs, _, width = ig_o.shape
    row = GRID * imgs
    base = row - imgs
    rows = SEQ * imgs
    part = 5 * imgs
    for ref in (gz, xs):
        ref[0:row] = jnp.zeros((row, width), F32)
        ref[8 * row : 9 * row] = jnp.zeros((row, width), F32)

    def fold(v):
        return jnp.sum(v.reshape(-1, 8, width), axis=0)

    def back_body(r, sums):
        at = rows_at(r * part, part)
        grad = gn1[at, :]
        unit, inv = norm_parts(s0[at, :])
        to = rows_at(base + r * part, part)
        gz[to, :] = gs1[at, :] + norm_back(grad, rp[10:11], unit, inv)
        xs[to, :] = xp[at, :].astype(F32)
        return (sums[0] + fold(grad * unit), sums[1] + fold(grad))

    zero = jnp.zeros((8, width), F32)
    sums = lax.fori_loop(0, rows // part, back_body, (zero, zero))
    for c in range(width // LANE):
        res[c, 0:imgs] = gz[base : base + imgs, c * LANE : (c + 1) * LANE]
    gz[base : base + imgs] = jnp.zeros((imgs, width), F32)
    xs[base : base + imgs] = jnp.zeros((imgs, width), F32)
    rep_o[10:11] = jnp.sum(sums[0], axis=0, keepdims=True)
    rep_o[11:12] = jnp.sum(sums[1], axis=0, keepdims=True)
    rep_o[12:16] = jnp.zeros((4, width), F32)
    rep_o[9:10] = jnp.sum(gz[row : 8 * row], axis=0, keepdims=True)

    def conv_body(y, carry):
        for c in range(0, width, LANE):
            cols = slice(c, c + LANE)
            taps = [rp[t : t + 1, cols] for t in range(9)]
            acc = conv_row(gz, taps, 1, y, cols, imgs, True)
            for x in range(GRID):
                here = gz[rows_at((y + 1) * row + x * imgs, imgs), cols]
                res[c // LANE, rows_at(imgs + y * row + x * imgs, imgs)] = here + acc[x]
        return carry

    lax.fori_loop(0, GRID, conv_body, 0)
    nothing = jnp.zeros((imgs, LANE), F32)
    for c in range(0, width, LANE):
        cols = slice(c, c + LANE)

        def tap_body(y, accs, cols=cols):
            start = (y + 1) * row
            grad_row = [gz[rows_at(start + x * imgs, imgs), cols] for x in range(GRID)]
            out = []
            for a in range(3):
                out.extend(tap_products(xs, grad_row, y, 1, cols, imgs, a, accs[3 * a : 3 * a + 3]))
            return tuple(out)

        accs = lax.fori_loop(0, GRID, tap_body, (nothing,) * 9)
        rep_o[0:9, cols] = jnp.concatenate(
            [jnp.sum(acc, axis=0, keepdims=True) for acc in accs], axis=0
        )
    for i in range(imgs):
        for c in range(0, width, LANE):
            ig_o[i, :, c : c + LANE] = res[c // LANE, pl.ds(i, SEQ, stride=imgs), :].astype(BF16)


def whole(shape):
    return pl.BlockSpec(shape, lambda *_: (0,) * len(shape))


def tap_mask(radius):
    reach = jnp.repeat(radius, HD)
    taps = lax.broadcasted_iota(jnp.int32, (TAPS, reach.shape[0]), 0)
    vertical = jnp.abs(taps // 7 - 3)
    horizontal = jnp.abs(taps % 7 - 3)
    inside = (vertical <= reach[None, :]) & (horizontal <= reach[None, :])
    return inside.astype(F32)


def adam_step(raw, weight, first, second, average, scale_clip, decay):
    grad = raw * scale_clip
    first_new = BETA_FIRST * first + (1.0 - BETA_FIRST) * grad
    second_new = BETA_SECOND * second + (1.0 - BETA_SECOND) * grad * grad
    moment_hat = first_new / (1.0 - BETA_FIRST**STEP)
    second_hat = second_new / (1.0 - BETA_SECOND**STEP)
    weight_new = weight - LEARN_RATE * (
        moment_hat / (jnp.sqrt(second_hat) + ADAM_EPS) + decay * weight
    )
    average_new = AVG_KEEP * average + (1.0 - AVG_KEEP) * weight_new
    return (grad, first_new, second_new, weight_new, weight_new.astype(BF16), average_new)


def square_sum(values):
    return jnp.sum(values * values)


class Ring:
    def __init__(self, nd, nh):
        self.low = 2 if nd % 2 == 0 else 1
        self.nd, self.nh, self.up = nd, nh, nd // self.low
        dp = lax.axis_index("dp")
        self.mine = (dp % self.low, dp // self.low, lax.axis_index("head"))

    def turn(self, value, stage, k):
        if stage == "head":
            return lax.ppermute(value, "head", [(i, (i + k) % self.nh) for i in range(self.nh)])
        low, up = self.low, self.up
        if stage == "up":
            pairs = [(i, (i // low + k) % up * low + i % low) for i in range(self.nd)]
        else:
            pairs = [(i, i // low * low + (i % low + k) % low) for i in range(self.nd)]
        return lax.ppermute(value, "dp", pairs)

    def gather(self, shard):
        for stage, size in (("head", self.nh), ("up", self.up), ("low", self.low)):
            shard = jnp.stack([shard] + [self.turn(shard, stage, k) for k in range(1, size)])
        return shard.reshape(self.nd * self.nh, *shard.shape[3:])

    def scatter_sum(self, parts):
        for stage, size in (("low", self.low), ("up", self.up), ("head", self.nh)):
            total = parts[0].astype(F32)
            for k in range(1, size):
                total = total + self.turn(parts[k], stage, k).astype(F32)
            parts = total.astype(parts.dtype) if stage != "head" else total
        return parts

    def gather_slot(self, dp, head):
        low, up, z = self.mine
        back = (low - dp % self.low) % self.low, (up - dp // self.low) % self.up
        return (back[0] * self.up + back[1]) * self.nh + (z - head) % self.nh

    def scatter_slot(self, dp, head):
        low, up, z = self.mine
        on = (dp % self.low - low) % self.low, (dp // self.low - up) % self.up
        return on[0] * self.up + on[1], (head - z) % self.nh


def per_device(
    block_input,
    out_grad,
    kernel_radius,
    qkv_weight,
    qkv_first,
    qkv_second,
    qkv_average,
    proj_weight,
    proj_first,
    proj_second,
    proj_average,
    up_weight,
    up_first,
    up_second,
    up_average,
    down_weight,
    down_first,
    down_second,
    down_average,
    head_params,
    head_first,
    head_second,
    head_average,
    rep_params,
    rep_first,
    rep_second,
    rep_average,
):
    nd, nh = lax.axis_size("dp"), lax.axis_size("head")
    imgs, _, width = block_input.shape
    rows = SEQ * imgs
    span = qkv_weight.shape[0]
    hid = up_weight.shape[1]
    ring = Ring(nd, nh)
    staged = span % 16 == 0

    pack_one = jnp.concatenate(
        [qkv_weight.astype(BF16).reshape(span, 3 * LANE), proj_weight.astype(BF16)], axis=1
    )
    pack_two = jnp.concatenate([up_weight.astype(BF16), down_weight.astype(BF16)], axis=1)
    nblk = nd if staged else 8
    size = width // nblk
    dps = jnp.arange(nblk, dtype=jnp.int32)
    heads = jnp.arange(nh, dtype=jnp.int32)
    if staged:
        gathered_one = ring.gather(pack_one)
        gathered_two = ring.gather(pack_two)
        in_slots = ring.gather_slot(dps[:, None], heads[None, :]).reshape(-1)
        out_rows, _ = ring.scatter_slot(dps, 0)
        _, out_heads = ring.scatter_slot(0, heads)
    else:

        def spread(pack):
            full = lax.all_gather(pack, ("dp", "head"), axis=0)
            full = full.reshape(nd, nh, span, -1).swapaxes(0, 1)
            full = full.reshape(nh, nblk, size, -1).swapaxes(0, 1)
            return full.reshape(nblk * nh, size, -1)

        gathered_one, gathered_two = spread(pack_one), spread(pack_two)
        in_slots = jnp.arange(nblk * nh, dtype=jnp.int32)
        out_rows, out_heads = dps, heads
    slots = jnp.concatenate([in_slots, out_rows, out_heads]).astype(jnp.int32)

    def weight_specs(cols):
        return [
            pl.BlockSpec((1, size, cols), lambda j, s, d=d: (s[d * nh + j], 0, 0))
            for d in range(nblk)
        ]

    grad_spec = lambda cols: pl.BlockSpec(
        (nblk, 1, size, cols), lambda j, s: (0, s[nblk * nh + nblk + j], 0, 0)
    )
    shape = jax.ShapeDtypeStruct
    params = pltpu.CompilerParams(
        dimension_semantics=("arbitrary",), vmem_limit_bytes=60 * 1024 * 1024
    )

    stream_zero, normed_one, pixels, cot, cot_sum = pl.pallas_call(
        pre_kernel,
        out_shape=(
            shape((rows, width), F32),
            shape((rows, width), BF16),
            shape((rows, width), BF16),
            shape((rows, width), BF16),
            shape((8, width), F32),
        ),
        scratch_shapes=[
            pltpu.VMEM((width // LANE, 9 * GRID * imgs, LANE), F32),
            pltpu.VMEM((width // LANE, rows, LANE), F32),
        ],
        compiler_params=pltpu.CompilerParams(vmem_limit_bytes=60 * 1024 * 1024),
        name="pre",
    )(block_input, out_grad, rep_params)

    mask = tap_mask(kernel_radius)
    head_rows = jnp.concatenate([head_params[:TAPS] * mask, head_params[TAPS : TAPS + 7]], axis=0)
    bias_up = head_params[TAPS + 3 :].reshape(nh, 1, hid)
    per_head = shape((nh, rows, LANE), F32)
    tile_spec = pl.BlockSpec((1, rows, LANE), lambda j, s: (j, 0, 0))
    full = whole((rows, width))
    padded = pltpu.VMEM((PAD_TOKENS * imgs, LANE), F32)
    framed = pltpu.VMEM((13 * GRID * imgs, LANE), F32)
    hp_spec = pl.BlockSpec((56, LANE), lambda j, s: (0, j))
    queries, keys_soft, values, conv_val, attended, stream_one, normed_two = pl.pallas_call(
        partial(attn_kernel, imgs=imgs, nblk=nblk),
        out_shape=(
            per_head,
            per_head,
            per_head,
            per_head,
            shape((nh, rows, LANE), BF16),
            shape((rows, width), F32),
            shape((rows, width), BF16),
        ),
        grid_spec=pltpu.PrefetchScalarGridSpec(
            num_scalar_prefetch=1,
            grid=(nh,),
            in_specs=[full, full] + weight_specs(4 * LANE) + [hp_spec, whole((16, width))],
            out_specs=[tile_spec] * 5 + [full, full],
            scratch_shapes=[padded] * 4 + [framed],
        ),
        compiler_params=params,
        name="attn",
    )(slots, normed_one, stream_zero, *[gathered_one] * nblk, head_rows, rep_params)

    output, grad_two, grad_low, grad_one, bias_grad, rep_mid = pl.pallas_call(
        partial(mlp_kernel, imgs=imgs, nblk=nblk, hid=hid),
        out_shape=(
            shape((imgs, SEQ, width), BF16),
            shape((nblk, nh, size, 2 * hid), BF16),
            shape((rows, width), BF16),
            shape((rows, width), F32),
            shape((nh, 8, hid), F32),
            shape((8, width), F32),
        ),
        grid_spec=pltpu.PrefetchScalarGridSpec(
            num_scalar_prefetch=1,
            grid=(nh,),
            in_specs=[full, full, full]
            + weight_specs(2 * hid)
            + [pl.BlockSpec((1, 1, hid), lambda j, s: (j, 0, 0)), whole((16, width))],
            out_specs=[
                whole((imgs, SEQ, width)),
                grad_spec(2 * hid),
                full,
                full,
                pl.BlockSpec((1, 8, hid), lambda j, s: (j, 0, 0)),
                whole((8, width)),
            ],
            scratch_shapes=[
                pltpu.VMEM((rows, hid), F32),
                pltpu.VMEM((rows, hid), F32),
                pltpu.VMEM((rows, hid), BF16),
                pltpu.VMEM((rows, hid), BF16),
                pltpu.VMEM((rows, width), F32),
                pltpu.VMEM((rows, width), F32),
                pltpu.VMEM((rows, LANE), F32),
            ],
        ),
        compiler_params=params,
        name="mlp",
    )(slots, normed_two, cot, stream_one, *[gathered_two] * nblk, bias_up, rep_params)

    grad_w_one, grad_norm_one, head_grad = pl.pallas_call(
        partial(attn_back_kernel, imgs=imgs, nblk=nblk),
        out_shape=(
            shape((nblk, nh, size, 4 * LANE), BF16),
            shape((rows, width), F32),
            shape((nh, 56, LANE), F32),
        ),
        grid_spec=pltpu.PrefetchScalarGridSpec(
            num_scalar_prefetch=1,
            grid=(nh,),
            in_specs=[full, full] + weight_specs(4 * LANE) + [hp_spec] + [tile_spec] * 5,
            out_specs=[
                grad_spec(4 * LANE),
                full,
                pl.BlockSpec((1, 56, LANE), lambda j, s: (j, 0, 0)),
            ],
            scratch_shapes=[padded] * 7 + [framed] * 2 + [pltpu.VMEM((rows, 3 * LANE), BF16)],
        ),
        compiler_params=params,
        name="attn_back",
    )(
        slots,
        normed_one,
        grad_low,
        *[gathered_one] * nblk,
        head_rows,
        queries,
        keys_soft,
        values,
        conv_val,
        attended,
    )

    input_grad, rep_top = pl.pallas_call(
        tail_kernel,
        out_shape=(shape((imgs, SEQ, width), BF16), shape((16, width), F32)),
        scratch_shapes=[
            pltpu.VMEM((9 * GRID * imgs, width), F32),
            pltpu.VMEM((9 * GRID * imgs, width), F32),
            pltpu.VMEM((width // LANE, rows, LANE), F32),
        ],
        compiler_params=pltpu.CompilerParams(vmem_limit_bytes=60 * 1024 * 1024),
        name="tail",
    )(stream_zero, grad_one, grad_norm_one, pixels, rep_params)

    rep_grad = jnp.concatenate([rep_top[:12], rep_mid[:3], cot_sum[:1]], axis=0)
    head_part = head_grad.transpose(1, 0, 2).reshape(56, width)
    head_part = jnp.concatenate(
        [head_part[:TAPS] * mask, head_part[TAPS : TAPS + 3], bias_grad[:, 0].reshape(-1, width)],
        axis=0,
    )
    small = jnp.concatenate([head_part, rep_grad], axis=0)
    head_count = head_part.shape[0]
    if staged:
        two = ring.scatter_sum(grad_two.reshape(ring.low, ring.up, nh, size, -1))
        one = ring.scatter_sum(grad_w_one.reshape(ring.low, ring.up, nh, size, -1))
        ndev = nd * nh
        cells = small.size // ndev
        order = jnp.arange(ndev, dtype=jnp.int32)
        low, up, z = ring.mine
        own = (
            ((order // (ring.up * nh) + low) % ring.low)
            + ((order // nh + up) % ring.up) * ring.low
        ) * nh + (order + z) % nh
        turned = jnp.take(small.reshape(ndev, cells), own, axis=0)
        share = ring.scatter_sum(turned.reshape(ring.low, ring.up, nh, cells // LANE, LANE))
        partial_sum = square_sum(one) + square_sum(two)
        tail = jnp.zeros((1, LANE), F32) + partial_sum
        everyone = ring.gather(jnp.concatenate([share, tail], axis=0))
        mat_total = jnp.sum(everyone[:, -1, 0])
        back = ring.gather_slot(order // nh, order % nh)
        small_sum = jnp.take(everyone[:, :-1].reshape(ndev, cells), back, axis=0)
        small_sum = small_sum.reshape(small.shape)
    else:

        def owned(grads):
            full = grads.swapaxes(0, 1).reshape(nh, nd, span, -1).swapaxes(0, 1)
            full = full.reshape(nd * nh, span, -1)
            return lax.psum_scatter(
                full, ("dp", "head"), scatter_dimension=0, tiled=False
            ).astype(F32)

        one, two = owned(grad_w_one), owned(grad_two)
        small_sum, mat_total = lax.psum(
            (small, square_sum(one) + square_sum(two)), ("dp", "head")
        )
    head_sum, rep_sum = small_sum[:head_count], small_sum[head_count:]
    qkv_raw = one[:, : 3 * LANE].reshape(qkv_weight.shape)
    proj_raw = one[:, 3 * LANE :]
    up_raw = two[:, :hid]
    down_raw = two[:, hid:]
    total = mat_total + square_sum(small_sum)
    grad_norm = jnp.sqrt(total)
    scale_clip = jnp.minimum(1.0, CLIP_NORM / (grad_norm + 1e-06))
    qkv_out = adam_step(
        qkv_raw, qkv_weight, qkv_first, qkv_second, qkv_average, scale_clip, WEIGHT_DECAY
    )
    proj_out = adam_step(
        proj_raw, proj_weight, proj_first, proj_second, proj_average, scale_clip, WEIGHT_DECAY
    )
    up_out = adam_step(up_raw, up_weight, up_first, up_second, up_average, scale_clip, WEIGHT_DECAY)
    down_out = adam_step(
        down_raw, down_weight, down_first, down_second, down_average, scale_clip, WEIGHT_DECAY
    )
    head_out = adam_step(
        head_sum, head_params, head_first, head_second, head_average, scale_clip, 0.0
    )
    rep_out = adam_step(rep_sum, rep_params, rep_first, rep_second, rep_average, scale_clip, 0.0)
    return (
        output,
        input_grad,
        grad_norm,
        *qkv_out,
        *proj_out,
        *up_out,
        *down_out,
        *head_out,
        *rep_out,
    )


def solution(mesh):
    tokens = P(("dp", "head"), None, None)
    qkv = P("dp", None, "head")
    mat = P("dp", "head")
    in_specs = (tokens, tokens, P()) + (qkv,) * 4 + (mat,) * 12 + (P(),) * 8
    out_specs = (tokens, tokens, P()) + (qkv,) * 6 + (mat,) * 18 + (P(),) * 12
    return jax.shard_map(
        per_device, mesh=mesh, in_specs=in_specs, out_specs=out_specs, check_vma=False
    )
```

time: 955 us -> 298 us (0.31)
  waiting for transfers between devices: 502 us -> 73.1 us
  matrix products: 143 us -> 0 us
  Pallas kernels: 0 us -> 111 us
  blocking collectives: 83.2 us -> 0 us
  local copies, waits for them, and re-layouts: 89.3 us -> 17.7 us
  other arithmetic: 89.6 us -> 30.1 us
  starting transfers between devices: 17.2 us -> 60.3 us
  between operations: 22.2 us -> 5.29 us
    reduce_scatter x4 -> x0, waiting for transfers between devices: 240 us -> none  [the longest x1 61.2 us: collect_three(): lax.psum_scatter(values.astype(jnp.bfloat16), 'head', scatter_dimension=0...]
    all_gather x4 -> x0, waiting for transfers between devices: 194 us -> none  [the longest x1 65 us: spread_four(): return lax.all_gather(values, 'head', axis=0, tiled=True)]
    dot_general x18 -> x0, matrix products: 143 us -> none  [the longest x1 19 us: block_pass(): jnp.einsum('bnd,df->bnf', rows_two, w_up, preferred_element_type=jnp.floa...]
    pallas_call x0 -> x5, Pallas kernels: none -> 111 us  [the longest x1 40.9 us: per_device(): pl.pallas_call(partial(attn_back_kernel, imgs=imgs, nblk=nblk), out_shape...]
    ppermute x0 -> x42, waiting for transfers between devices: none -> 73.1 us  [the longest x24 55.2 us: turn(): return lax.ppermute(value, 'dp', pairs)]
    ppermute x0 -> x42, starting transfers between devices: none -> 60.3 us  [the longest x18 32.1 us: turn(): lax.ppermute(value, 'head', [(i, (i + k) % self.nh) for i in range(self.n...]
    psum x1 -> x0, waiting for transfers between devices: 57.1 us -> none  [per_device(): lax.psum((rep_grad, head_full, partial_sum), ('dp', 'head'))]
    all_gather x4 -> x0, blocking collectives: 42.6 us -> none  [the longest x1 11.7 us: per_device(): lax.all_gather(up_weight.astype(jnp.bfloat16), 'dp', axis=0, tiled=True)]
  transfers between devices with their start and end apart: 13 -> 42, of which waited for: 12 -> 20; matrix products, arithmetic and copies ran while one was open for 8% -> 9% of each run, Pallas kernels for 0% -> 10%
where the time goes in v1:
time: 298 us; the launch traced here: 297 us
  Pallas kernels  111 us (37%)
  waiting for transfers between devices  73.1 us (25%)
  starting transfers between devices  60.3 us (20%)
  other arithmetic  30.1 us (10%)
  local copies, waits for them, and re-layouts  17.7 us (6%)
  between operations  5.29 us (2%)
    ppermute x24, waiting for transfers between devices, turn(): return lax.ppermute(value, 'dp', pairs)  55.2 us
    pallas_call x1, Pallas kernels, per_device(): pl.pallas_call(partial(attn_back_kernel, imgs=imgs, nblk=nblk), out_shape...  40.9 us
    ppermute x18, starting transfers between devices, turn(): lax.ppermute(value, 'head', [(i, (i + k) % self.nh) for i in range(self.n...  32.1 us
    pallas_call x1, Pallas kernels, per_device(): pl.pallas_call(partial(mlp_kernel, imgs=imgs, nblk=nblk, hid=hid), out_sh...  28.7 us
    ppermute x24, starting transfers between devices, turn(): return lax.ppermute(value, 'dp', pairs)  28.3 us
    pallas_call x1, Pallas kernels, per_device(): pl.pallas_call(partial(attn_kernel, imgs=imgs, nblk=nblk), out_shape=(per...  22.8 us
    ppermute x18, waiting for transfers between devices, turn(): lax.ppermute(value, 'head', [(i, (i + k) % self.nh) for i in range(self.n...  17.9 us
    another operation x11, other arithmetic, gather(): jnp.stack([shard] + [self.turn(shard, stage, k) for k in range(1, size)])  10.9 us
  transfers between devices with their start and end apart: 42, of which 20 were waited for; matrix products, arithmetic and copies ran while one was open for 9% of the time, Pallas kernels for 10%

profile of v1, /device:TPU:0, one launch (start us, length us, event | category | flops | bytes accessed | tf_op | source)
XLA Modules:
  0.0 297.2 jit_solution(2361401076870717940)
XLA Ops:
  2.6 4.1 %collective-permute-start.8 = (bf16[64,1024]{1,0:T(8,128)(2,1)S(1)}, bf16[64,1024]{1,0:T(8,128)(2,1)S(1)}, u32[]{:S(2)}, u32[]{:S(2)}) collective-permute-start(bf16[64,1024]{1,0:T(8,128)(2,1)S(1)} %get-tuple-element.276), channel_id=1, source_target_pairs={{0,2},{1,3},{2,0},{3,1},{4,6},{5,7},{6,4},{7,5},{8,10},{9,11},{10,... | collective-permute-start | bytes 393224 | tf_op jit(solution)/shard_map/ppermute | solution.py:509
  10.6 6.2 %collective-permute-done.8 = bf16[64,1024]{1,0:T(8,128)(2,1)S(1)} collective-permute-done((bf16[64,1024]{1,0:T(8,128)(2,1)S(1)}, bf16[64,1024]{1,0:T(8,128)(2,1)S(1)}, u32[]{:S(2)}, u32[]{:S(2)}) %collective-permute-start.8) | collective-permute-done | bytes 131104 | tf_op jit(solution)/shard_map/ppermute | solution.py:509
  22.1 3.9 %collective-permute-start.1 = (bf16[64,512]{1,0:T(8,128)(2,1)S(1)}, bf16[64,512]{1,0:T(8,128)(2,1)S(1)}, u32[]{:S(2)}, u32[]{:S(2)}) collective-permute-start(bf16[64,512]{1,0:T(8,128)(2,1)S(1)} %get-tuple-element.278), channel_id=1, source_target_pairs={{0,2},{1,3},{2,0},{3,1},{4,6},{5,7},{6,4},{7,5},{8,10},{9,11},{10,... | collective-permute-start | bytes 196616 | tf_op jit(solution)/shard_map/ppermute | solution.py:509
  26.0 15.2 %collective-permute-done.11 = bf16[4,64,1024]{2,1,0:T(8,128)(2,1)S(1)} collective-permute-done((bf16[4,64,1024]{2,1,0:T(8,128)(2,1)S(1)}, bf16[4,64,1024]{2,1,0:T(8,128)(2,1)S(1)}, u32[]{:S(2)}, u32[]{:S(2)}) %collective-permute-start.11) | collective-permute-done | bytes 524320 | tf_op jit(solution)/shard_map/ppermute | solution.py:515
  44.6 2.9 fusion.58
  49.2 2.9 collective-permute-start.5
  52.2 9.8 %collective-permute-done.4 = bf16[4,64,512]{2,1,0:T(8,128)(2,1)S(1)} collective-permute-done((bf16[4,64,512]{2,1,0:T(8,128)(2,1)S(1)}, bf16[4,64,512]{2,1,0:T(8,128)(2,1)S(1)}, u32[]{:S(2)}, u32[]{:S(2)}) %collective-permute-start.4) | collective-permute-done | bytes 262176 | tf_op jit(solution)/shard_map/ppermute | solution.py:515
  69.3 8.3 %pre.1 = (f32[800,512]{1,0:T(8,128)}, bf16[800,512]{1,0:T(8,128)(2,1)}, bf16[800,512]{1,0:T(8,128)(2,1)}, bf16[800,512]{1,0:T(8,128)(2,1)}, f32[8,512]{1,0:T(8,128)}) custom-call(bf16[16,50,512]{2,1,0:T(8,128)(2,1)} %copy.94.x_ref, bf16[16,50,512]{2,1,0:T(8,128)(2,1)} %copy.95.og_ref, f32[16,512]{1,0:T(8,128)} %rp.1), custom_call_target="tpu_custom_call" | custom-call | tf_op jit(solution)/shard_map/pre/pallas_call | solution.py:619
  80.8 2.7 pad_maximum_fusion.1
  83.6 22.8 %attn.1 = (f32[4,800,128]{2,1,0:T(8,128)}, f32[4,800,128]{2,1,0:T(8,128)}, f32[4,800,128]{2,1,0:T(8,128)}, f32[4,800,128]{2,1,0:T(8,128)}, bf16[4,800,128]{2,1,0...) custom-call(s32[44]{0:T(128)} %pad_add_fusion.refs_0_, bf16[800,512]{1,0:T(8,128)(2,1)} %get-tuple-element.63.refs_1_, ...), custom_call_target="tpu_custom_call" | custom-call | tf_op jit(solution)/shard_map/attn/pallas_call | solution.py:645
  106.3 4.0 %pad_maximum_fusion = bf16[2,4,4,64,1024]{4,3,2,1,0:T(8,128)(2,1)} fusion(bf16[1,4,4,64,1024]{4,3,2,1,0:T(8,128)(2,1)} %bitcast.20, bf16[1,4,4,64,1024]{4,3,2,1,0:T(8,128)(2,1)S(1)} %get-tuple-element.246), kind=kLoop, calls=%fused_computation.2 | loop fusion | flops 2097152 | bytes 8388608 | tf_op jit(solution)/shard_map/stack | solution.py:519
  110.3 28.7 %mlp.1 = (bf16[16,50,512]{2,1,0:T(8,128)(2,1)}, bf16[8,4,64,1024]{3,2,1,0:T(8,128)(2,1)}, bf16[800,512]{1,0:T(8,128)(2,1)}, f32[800,512]{1,0:T(8,128)}, f32[4,8,512]{2,1,0:T(8,128)}, /*index=5*/f32[8,512]{1,0:T(8,128)}) custom-call(s32[44]{0:T(128)} %pad_add_fusion.refs_0_, bf16[800,512]{1,0:T(8,128)(2,1)} %get-tuple-element.65.refs_1_, ...), custom_call_target="tpu_custom_call" | custom-call | tf_op jit(solution)/shard_map/mlp/pallas_call | solution.py:667
  139.0 40.9 %attn_back.1 = (bf16[8,4,64,512]{3,2,1,0:T(8,128)(2,1)}, f32[800,512]{1,0:T(8,128)}, f32[4,56,128]{2,1,0:T(8,128)}) custom-call(s32[44]{0:T(128)} %pad_add_fusion.refs_0_, bf16[800,512]{1,0:T(8,128)(2,1)} %get-tuple-element.63.refs_1_, bf16[800,512]{1,0:T(8,128)(2,1)} %get-tuple-element.70.refs_2_, bf16[32,64,512]{2,1,0:T(8,128)(2,1)} %bitcast.150, ...), custom_call_target="tpu_custom_call" | custom-call | tf_op jit(solution)/shard_map/attn_back/pallas_call | solution.py:705
  181.9 10.0 %tail.1 = (bf16[16,50,512]{2,1,0:T(8,128)(2,1)}, f32[16,512]{1,0:T(8,128)}) custom-call(f32[800,512]{1,0:T(8,128)} %get-tuple-element.64.refs_2_.s0, f32[800,512]{1,0:T(8,128)} %get-tuple-element.69.gs1, f32[800,512]{1,0:T(8,128)} %get-tuple-element.76.gn1, bf16[800,512]{1,0:T(8,128)(2,1)} %get-tuple-element.77.xp, f32[16,512]{1,0:T(8,128)} %rp.1), custom_call_target="tpu_custom_call" | custom-call | tf_op jit(solution)/shard_map/tail/pallas_call | solution.py:738
  194.3 3.2 %slice.185 = bf16[4,4,64,1024]{3,2,1,0:T(8,128)(2,1)} slice(bf16[8,4,64,1024]{3,2,1,0:T(8,128)(2,1)} %get-tuple-element.85), slice={[4:8], [0:4], [0:64], [0:1024]} | slice | bytes 4194304 | tf_op jit(solution)/shard_map/slice | solution.py:526
  199.0 3.2 %collective-permute-done.14 = f32[4,4,9,128]{3,2,1,0:T(8,128)} collective-permute-done((f32[4,4,9,128]{3,2,1,0:T(8,128)S(1)}, f32[4,4,9,128]{3,2,1,0:T(8,128)}, u32[]{:S(2)}, u32[]{:S(2)}) %collective-permute-start.14) | collective-permute-done | bytes 73760 | tf_op jit(solution)/shard_map/ppermute | solution.py:515
  223.6 2.9 collective-permute-start.31
  229.5 4.1 %collective-permute-done.24 = bf16[4,64,512]{2,1,0:T(8,128)(2,1)S(1)} collective-permute-done((bf16[4,64,512]{2,1,0:T(8,128)(2,1)S(1)}, bf16[4,64,512]{2,1,0:T(8,128)(2,1)S(1)}, u32[]{:S(2)}, u32[]{:S(2)}) %collective-permute-start.24) | collective-permute-done | bytes 262176 | tf_op jit(solution)/shard_map/ppermute | solution.py:515
  233.6 8.7 %collective-permute-done.23 = bf16[4,64,512]{2,1,0:T(8,128)(2,1)S(1)} collective-permute-done((bf16[4,64,512]{2,1,0:T(8,128)(2,1)S(1)}, bf16[4,64,512]{2,1,0:T(8,128)(2,1)S(1)}, u32[]{:S(2)}, u32[]{:S(2)}) %collective-permute-start.23) | collective-permute-done | bytes 262176 | tf_op jit(solution)/shard_map/ppermute | solution.py:515
  243.4 3.0 collective-permute-start.27
  246.4 6.6 %collective-permute-done.31 = bf16[4,64,1024]{2,1,0:T(8,128)(2,1)S(1)} collective-permute-done((bf16[4,64,1024]{2,1,0:T(8,128)(2,1)S(1)}, bf16[4,64,1024]{2,1,0:T(8,128)(2,1)S(1)}, u32[]{:S(2)}, u32[]{:S(2)}) %collective-permute-start.31) | collective-permute-done | bytes 524320 | tf_op jit(solution)/shard_map/ppermute | solution.py:515
  254.1 3.1 %collective-permute-start.34 = (bf16[64,1024]{1,0:T(8,128)(2,1)S(1)}, bf16[64,1024]{1,0:T(8,128)(2,1)S(1)}, u32[]{:S(2)}, u32[]{:S(2)}) collective-permute-start(bf16[64,1024]{1,0:T(8,128)(2,1)S(1)} %get-tuple-element.254), channel_id=1, source_target_pairs={{0,3},{1,0},{2,1},{3,2},{4,7},{5,4},{6,5},{7,6},{8,11},{9,8},{10,9... | collective-permute-start | bytes 393224 | tf_op jit(solution)/shard_map/ppermute | solution.py:509
  257.9 3.8 %collective-permute-done.32 = bf16[64,1024]{1,0:T(8,128)(2,1)S(1)} collective-permute-done((bf16[64,1024]{1,0:T(8,128)(2,1)S(1)}, bf16[64,1024]{1,0:T(8,128)(2,1)S(1)}, u32[]{:S(2)}, u32[]{:S(2)}) %collective-permute-start.32) | collective-permute-done | bytes 131104 | tf_op jit(solution)/shard_map/ppermute | solution.py:509
  261.7 5.1 %collective-permute-done.33 = bf16[64,1024]{1,0:T(8,128)(2,1)S(1)} collective-permute-done((bf16[64,1024]{1,0:T(8,128)(2,1)S(1)}, bf16[64,1024]{1,0:T(8,128)(2,1)S(1)}, u32[]{:S(2)}, u32[]{:S(2)}) %collective-permute-start.33) | collective-permute-done | bytes 131104 | tf_op jit(solution)/shard_map/ppermute | solution.py:509
  (247 shorter events, 85.9 us)
Async XLA Ops:
  2.6 14.1 %collective-permute-start.8 = (bf16[64,1024]{1,0:T(8,128)(2,1)S(1)}, bf16[64,1024]{1,0:T(8,128)(2,1)S(1)}, u32[]{:S(2)}, u32[]{:S(2)}) collective-permute-start(bf16[64,1024]{1,0:T(8,128)(2,1)S(1)} %get-tuple-element.276), channel_id=1, source_target_pairs={{0,2},{1,3},{2,0},{3,1},{4,6},{5,7},{6,4},{7,5},{8,10},{9,11},{10,... | collective-permute-start | bytes 393224 | tf_op jit(solution)/shard_map/ppermute | solution.py:509
  17.5 23.7 %collective-permute-start.11 = (bf16[4,64,1024]{2,1,0:T(8,128)(2,1)S(1)}, bf16[4,64,1024]{2,1,0:T(8,128)(2,1)S(1)}, u32[]{:S(2)}, u32[]{:S(2)}) collective-permute-start(bf16[4,64,1024]{2,1,0:T(8,128)(2,1)S(1)} %get-tuple-element.257), channel_id=1, source_target_pairs={{0,16},{4,20},{8,24},{12,28},{16,0},{20,4},{24,8},{28,12},{1,17},{... | collective-permute-start | bytes 1572872 | tf_op jit(solution)/shard_map/ppermute | solution.py:515
  19.2 24.4 %collective-permute-start.10 = (bf16[4,64,1024]{2,1,0:T(8,128)(2,1)S(1)}, bf16[4,64,1024]{2,1,0:T(8,128)(2,1)S(1)}, u32[]{:S(2)}, u32[]{:S(2)}) collective-permute-start(bf16[4,64,1024]{2,1,0:T(8,128)(2,1)S(1)} %get-tuple-element.257), channel_id=1, source_target_pairs={{0,8},{4,12},{8,16},{12,20},{16,24},{20,28},{24,0},{28,4},{1,9},{5... | collective-permute-start | bytes 1572872 | tf_op jit(solution)/shard_map/ppermute | solution.py:515
  20.7 22.9 %collective-permute-start.12 = (bf16[4,64,1024]{2,1,0:T(8,128)(2,1)S(1)}, bf16[4,64,1024]{2,1,0:T(8,128)(2,1)S(1)}, u32[]{:S(2)}, u32[]{:S(2)}) collective-permute-start(bf16[4,64,1024]{2,1,0:T(8,128)(2,1)S(1)} %get-tuple-element.257), channel_id=1, source_target_pairs={{0,24},{4,28},{8,0},{12,4},{16,8},{20,12},{24,16},{28,20},{1,25},{... | collective-permute-start | bytes 1572872 | tf_op jit(solution)/shard_map/ppermute | solution.py:515
  22.1 25.3 %collective-permute-start.1 = (bf16[64,512]{1,0:T(8,128)(2,1)S(1)}, bf16[64,512]{1,0:T(8,128)(2,1)S(1)}, u32[]{:S(2)}, u32[]{:S(2)}) collective-permute-start(bf16[64,512]{1,0:T(8,128)(2,1)S(1)} %get-tuple-element.278), channel_id=1, source_target_pairs={{0,2},{1,3},{2,0},{3,1},{4,6},{5,7},{6,4},{7,5},{8,10},{9,11},{10,... | collective-permute-start | bytes 196616 | tf_op jit(solution)/shard_map/ppermute | solution.py:509
  26.0 21.5 %collective-permute-start = (bf16[64,512]{1,0:T(8,128)(2,1)S(1)}, bf16[64,512]{1,0:T(8,128)(2,1)S(1)}, u32[]{:S(2)}, u32[]{:S(2)}) collective-permute-start(bf16[64,512]{1,0:T(8,128)(2,1)S(1)} %get-tuple-element.278), channel_id=1, source_target_pairs={{0,1},{1,2},{2,3},{3,0},{4,5},{5,6},{6,7},{7,4},{8,9},{9,10},{10,1... | collective-permute-start | bytes 196616 | tf_op jit(solution)/shard_map/ppermute | solution.py:509
  47.4 58.9 %collective-permute-start.13 = (bf16[4,4,64,1024]{3,2,1,0:T(8,128)(2,1)}, bf16[4,4,64,1024]{3,2,1,0:T(8,128)(2,1)}, u32[]{:S(2)}, u32[]{:S(2)}) collective-permute-start(bf16[4,4,64,1024]{3,2,1,0:T(8,128)(2,1)} %get-tuple-element.247), channel_id=1, source_target_pairs={{0,4},{4,0},{8,12},{12,8},{16,20},{20,16},{24,28},{28,24},{1,5},{5... | collective-permute-start | bytes 6291464 | tf_op jit(solution)/shard_map/ppermute | solution.py:515
  47.6 14.4 %collective-permute-start.4 = (bf16[4,64,512]{2,1,0:T(8,128)(2,1)S(1)}, bf16[4,64,512]{2,1,0:T(8,128)(2,1)S(1)}, u32[]{:S(2)}, u32[]{:S(2)}) collective-permute-start(bf16[4,64,512]{2,1,0:T(8,128)(2,1)S(1)} %get-tuple-element.267), channel_id=1, source_target_pairs={{0,16},{4,20},{8,24},{12,28},{16,0},{20,4},{24,8},{28,12},{1,17},{... | collective-permute-start | bytes 786440 | tf_op jit(solution)/shard_map/ppermute | solution.py:515
  49.1 12.8 %collective-permute-start.3 = (bf16[4,64,512]{2,1,0:T(8,128)(2,1)S(1)}, bf16[4,64,512]{2,1,0:T(8,128)(2,1)S(1)}, u32[]{:S(2)}, u32[]{:S(2)}) collective-permute-start(bf16[4,64,512]{2,1,0:T(8,128)(2,1)S(1)} %get-tuple-element.267), channel_id=1, source_target_pairs={{0,8},{4,12},{8,16},{12,20},{16,24},{20,28},{24,0},{28,4},{1,9},{5... | collective-permute-start | bytes 786440 | tf_op jit(solution)/shard_map/ppermute | solution.py:515
  49.2 14.0 %collective-permute-start.5 = (bf16[4,64,512]{2,1,0:T(8,128)(2,1)S(1)}, bf16[4,64,512]{2,1,0:T(8,128)(2,1)S(1)}, u32[]{:S(2)}, u32[]{:S(2)}) collective-permute-start(bf16[4,64,512]{2,1,0:T(8,128)(2,1)S(1)} %get-tuple-element.267), channel_id=1, source_target_pairs={{0,24},{4,28},{8,0},{12,4},{16,8},{20,12},{24,16},{28,20},{1,25},{... | collective-permute-start | bytes 786440 | tf_op jit(solution)/shard_map/ppermute | solution.py:515
  64.3 16.5 %collective-permute-start.6 = (bf16[4,4,64,512]{3,2,1,0:T(8,128)(2,1)}, bf16[4,4,64,512]{3,2,1,0:T(8,128)(2,1)}, u32[]{:S(2)}, u32[]{:S(2)}) collective-permute-start(bf16[4,4,64,512]{3,2,1,0:T(8,128)(2,1)} %get-tuple-element.252), channel_id=1, source_target_pairs={{0,4},{4,0},{8,12},{12,8},{16,20},{20,16},{24,28},{28,24},{1,5},{5... | collective-permute-start | bytes 3145736 | tf_op jit(solution)/shard_map/ppermute | solution.py:515
  193.8 22.4 %collective-permute-start.21 = (bf16[4,4,64,512]{3,2,1,0:T(8,128)(2,1)}, bf16[4,4,64,512]{3,2,1,0:T(8,128)(2,1)S(1)}, u32[]{:S(2)}, u32[]{:S(2)}) collective-permute-start(bf16[4,4,64,512]{3,2,1,0:T(8,128)(2,1)} %slice.175), channel_id=1, source_target_pairs={{0,4},{4,0},{8,12},{12,8},{16,20},{20,16},{24,28},{28,24},{1,5},{5... | collective-permute-start | bytes 3145736 | tf_op jit(solution)/shard_map/ppermute | solution.py:515
  197.5 21.3 %collective-permute-start.28 = (bf16[4,4,64,1024]{3,2,1,0:T(8,128)(2,1)}, bf16[4,4,64,1024]{3,2,1,0:T(8,128)(2,1)S(1)}, u32[]{:S(2)}, u32[]{:S(2)}) collective-permute-start(bf16[4,4,64,1024]{3,2,1,0:T(8,128)(2,1)} %slice.185), channel_id=1, source_target_pairs={{0,4},{4,0},{8,12},{12,8},{16,20},{20,16},{24,28},{28,24},{1,5},{5... | collective-permute-start | bytes 6291464 | tf_op jit(solution)/shard_map/ppermute | solution.py:515
  210.1 11.8 %collective-permute-start.18 = (f32[9,128]{1,0:T(8,128)S(1)}, f32[9,128]{1,0:T(8,128)S(1)}, u32[]{:S(2)}, u32[]{:S(2)}) collective-permute-start(f32[9,128]{1,0:T(8,128)S(1)} %get-tuple-element.281), channel_id=1, source_target_pairs={{0,1},{1,2},{2,3},{3,0},{4,5},{5,6},{6,7},{7,4},{8,9},{9,10},{10,1... | collective-permute-start | bytes 13832 | tf_op jit(solution)/shard_map/ppermute | solution.py:509
  212.2 11.4 %collective-permute-start.20 = (f32[9,128]{1,0:T(8,128)S(1)}, f32[9,128]{1,0:T(8,128)S(1)}, u32[]{:S(2)}, u32[]{:S(2)}) collective-permute-start(f32[9,128]{1,0:T(8,128)S(1)} %get-tuple-element.282), channel_id=1, source_target_pairs={{0,3},{1,0},{2,1},{3,2},{4,7},{5,4},{6,5},{7,6},{8,11},{9,8},{10,9... | collective-permute-start | bytes 13832 | tf_op jit(solution)/shard_map/ppermute | solution.py:509
  217.8 10.1 %collective-permute-start.22 = (bf16[4,64,512]{2,1,0:T(8,128)(2,1)S(1)}, bf16[4,64,512]{2,1,0:T(8,128)(2,1)S(1)}, u32[]{:S(2)}, u32[]{:S(2)}) collective-permute-start(bf16[4,64,512]{2,1,0:T(8,128)(2,1)S(1)} %get-tuple-element.248), channel_id=1, source_target_pairs={{0,8},{4,12},{8,16},{12,20},{16,24},{20,28},{24,0},{28,4},{1,9},{5... | collective-permute-start | bytes 786440 | tf_op jit(solution)/shard_map/ppermute | solution.py:515
  218.8 14.8 %collective-permute-start.24 = (bf16[4,64,512]{2,1,0:T(8,128)(2,1)S(1)}, bf16[4,64,512]{2,1,0:T(8,128)(2,1)S(1)}, u32[]{:S(2)}, u32[]{:S(2)}) collective-permute-start(bf16[4,64,512]{2,1,0:T(8,128)(2,1)S(1)} %get-tuple-element.249), channel_id=1, source_target_pairs={{0,24},{4,28},{8,0},{12,4},{16,8},{20,12},{24,16},{28,20},{1,25},{... | collective-permute-start | bytes 786440 | tf_op jit(solution)/shard_map/ppermute | solution.py:515
  221.8 20.5 %collective-permute-start.23 = (bf16[4,64,512]{2,1,0:T(8,128)(2,1)S(1)}, bf16[4,64,512]{2,1,0:T(8,128)(2,1)S(1)}, u32[]{:S(2)}, u32[]{:S(2)}) collective-permute-start(bf16[4,64,512]{2,1,0:T(8,128)(2,1)S(1)} %get-tuple-element.250), channel_id=1, source_target_pairs={{0,16},{4,20},{8,24},{12,28},{16,0},{20,4},{24,8},{28,12},{1,17},{... | collective-permute-start | bytes 786440 | tf_op jit(solution)/shard_map/ppermute | solution.py:515
  223.5 22.8 %collective-permute-start.29 = (bf16[4,64,1024]{2,1,0:T(8,128)(2,1)S(1)}, bf16[4,64,1024]{2,1,0:T(8,128)(2,1)S(1)}, u32[]{:S(2)}, u32[]{:S(2)}) collective-permute-start(bf16[4,64,1024]{2,1,0:T(8,128)(2,1)S(1)} %get-tuple-element.243), channel_id=1, source_target_pairs={{0,8},{4,12},{8,16},{12,20},{16,24},{20,28},{24,0},{28,4},{1,9},{5... | collective-permute-start | bytes 1572872 | tf_op jit(solution)/shard_map/ppermute | solution.py:515
  223.6 29.3 %collective-permute-start.31 = (bf16[4,64,1024]{2,1,0:T(8,128)(2,1)S(1)}, bf16[4,64,1024]{2,1,0:T(8,128)(2,1)S(1)}, u32[]{:S(2)}, u32[]{:S(2)}) collective-permute-start(bf16[4,64,1024]{2,1,0:T(8,128)(2,1)S(1)} %get-tuple-element.244), channel_id=1, source_target_pairs={{0,24},{4,28},{8,0},{12,4},{16,8},{20,12},{24,16},{28,20},{1,25},{... | collective-permute-start | bytes 1572872 | tf_op jit(solution)/shard_map/ppermute | solution.py:515
  228.0 25.0 %collective-permute-start.30 = (bf16[4,64,1024]{2,1,0:T(8,128)(2,1)S(1)}, bf16[4,64,1024]{2,1,0:T(8,128)(2,1)S(1)}, u32[]{:S(2)}, u32[]{:S(2)}) collective-permute-start(bf16[4,64,1024]{2,1,0:T(8,128)(2,1)S(1)} %get-tuple-element.245), channel_id=1, source_target_pairs={{0,16},{4,20},{8,24},{12,28},{16,0},{20,4},{24,8},{28,12},{1,17},{... | collective-permute-start | bytes 1572872 | tf_op jit(solution)/shard_map/ppermute | solution.py:515
  242.5 14.8 %collective-permute-start.25 = (bf16[64,512]{1,0:T(8,128)(2,1)S(1)}, bf16[64,512]{1,0:T(8,128)(2,1)S(1)}, u32[]{:S(2)}, u32[]{:S(2)}) collective-permute-start(bf16[64,512]{1,0:T(8,128)(2,1)S(1)} %get-tuple-element.263), channel_id=1, source_target_pairs={{0,1},{1,2},{2,3},{3,0},{4,5},{5,6},{6,7},{7,4},{8,9},{9,10},{10,1... | collective-permute-start | bytes 196616 | tf_op jit(solution)/shard_map/ppermute | solution.py:509
  243.4 13.8 %collective-permute-start.27 = (bf16[64,512]{1,0:T(8,128)(2,1)S(1)}, bf16[64,512]{1,0:T(8,128)(2,1)S(1)}, u32[]{:S(2)}, u32[]{:S(2)}) collective-permute-start(bf16[64,512]{1,0:T(8,128)(2,1)S(1)} %get-tuple-element.264), channel_id=1, source_target_pairs={{0,3},{1,0},{2,1},{3,2},{4,7},{5,4},{6,5},{7,6},{8,11},{9,8},{10,9... | collective-permute-start | bytes 196616 | tf_op jit(solution)/shard_map/ppermute | solution.py:509
  246.4 10.9 %collective-permute-start.26 = (bf16[64,512]{1,0:T(8,128)(2,1)S(1)}, bf16[64,512]{1,0:T(8,128)(2,1)S(1)}, u32[]{:S(2)}, u32[]{:S(2)}) collective-permute-start(bf16[64,512]{1,0:T(8,128)(2,1)S(1)} %get-tuple-element.265), channel_id=1, source_target_pairs={{0,2},{1,3},{2,0},{3,1},{4,6},{5,7},{6,4},{7,5},{8,10},{9,11},{10,... | collective-permute-start | bytes 196616 | tf_op jit(solution)/shard_map/ppermute | solution.py:509
  (64 other events, 576.3 us)

commit v2 on v1

v2 whole, which is shorter than its diff:
```python
from functools import partial

import jax
import jax.numpy as jnp
from jax import lax
from jax.experimental import pallas as pl
from jax.experimental.pallas import tpu as pltpu
from jax.sharding import PartitionSpec as P


HD = 64
GRID = 7
TAPS = 49
STEP = 5
SEQ = 50
LANE = 128
PAD_TOKENS = 64

NORM_EPS = 1e-06
BETA_FIRST = 0.9
BETA_SECOND = 0.999
ADAM_EPS = 1e-08
LEARN_RATE = 0.1
WEIGHT_DECAY = 0.05
CLIP_NORM = 1.0
AVG_KEEP = 0.9

F32 = jnp.float32
BF16 = jnp.bfloat16

NN = (((1,), (0,)), ((), ()))
NT = (((1,), (1,)), ((), ()))
TN = (((0,), (0,)), ((), ()))


def dot(left, right, dims=NN):
    return lax.dot_general(left, right, dims, preferred_element_type=F32)


def rows_at(start, size):
    return pl.ds(pl.multiple_of(start, 16), size)


def norm_parts(values):
    center = values - jnp.mean(values, axis=-1, keepdims=True)
    inv = lax.rsqrt(jnp.mean(center * center, axis=-1, keepdims=True) + NORM_EPS)
    return center * inv, inv


def norm_back(grad, gain, unit, inv):
    scaled = grad * gain
    mean_one = jnp.mean(scaled, axis=-1, keepdims=True)
    mean_two = jnp.mean(scaled * unit, axis=-1, keepdims=True)
    return inv * (scaled - mean_one - unit * mean_two)


def conv_row(src, taps, reach, y, cols, imgs, flip):
    side = 2 * reach + 1
    acc = [None] * GRID
    for a in range(side):
        start = (y + a) * (GRID * imgs)
        vals = [src[rows_at(start + x * imgs, imgs), cols] for x in range(GRID)]
        for b in range(side):
            t = a * side + b
            tap = taps[side * side - 1 - t if flip else t]
            for x in range(GRID):
                other = x + b - reach
                if 0 <= other < GRID:
                    term = tap * vals[other]
                    acc[x] = term if acc[x] is None else acc[x] + term
    return acc


def tap_products(src, grad_row, y, reach, cols, imgs, a, accs):
    side = 2 * reach + 1
    start = (y + a) * (GRID * imgs)
    vals = [src[rows_at(start + x * imgs, imgs), cols] for x in range(GRID)]
    out = []
    for b in range(side):
        acc = accs[b]
        for x in range(GRID):
            other = x + b - reach
            if 0 <= other < GRID:
                acc = acc + grad_row[x] * vals[other]
        out.append(acc)
    return tuple(out)


def transposed(out, src, rows):
    for r in range(0, rows, LANE):
        stop = min(r + LANE, rows)
        out[:, r:stop] = src[r:stop].T


def pre_kernel(x_ref, og_ref, rp_ref, s0_ref, n1_ref, n1t_ref, ogt_ref, ogsum_ref, xs, *, imgs):
    rows, width = x_ref.shape
    row = GRID * imgs
    base = row - imgs
    xs[0:base] = jnp.zeros((base, width), F32)
    xs[8 * row : 9 * row] = jnp.zeros((row, width), F32)
    xs[base : base + rows] = x_ref[...].astype(F32)
    s0_ref[0:imgs] = xs[base:row]
    xs[base:row] = jnp.zeros((imgs, width), F32)

    def conv_body(y, carry):
        for c in range(0, width, LANE):
            cols = slice(c, c + LANE)
            taps = [rp_ref[t : t + 1, cols] for t in range(9)]
            acc = conv_row(xs, taps, 1, y, cols, imgs, False)
            for x in range(GRID):
                here = xs[rows_at((y + 1) * row + x * imgs, imgs), cols]
                s0_ref[rows_at(imgs + y * row + x * imgs, imgs), cols] = (
                    here + acc[x] + rp_ref[9:10, cols]
                )
        return carry

    lax.fori_loop(0, GRID, conv_body, 0)
    step = 5 * imgs

    def norm_body(r, total):
        at = rows_at(r * step, step)
        unit, _ = norm_parts(s0_ref[at, :])
        n1_ref[at, :] = (unit * rp_ref[10:11] + rp_ref[11:12]).astype(BF16)
        wide = og_ref[at, :].astype(F32).reshape(step // 8, 8, width)
        return total + jnp.sum(wide, axis=0)

    total = lax.fori_loop(0, rows // step, norm_body, jnp.zeros((8, width), F32))
    ogsum_ref[...] = jnp.broadcast_to(jnp.sum(total, axis=0, keepdims=True), (8, width))
    transposed(n1t_ref, n1_ref, rows)
    transposed(ogt_ref, og_ref, rows)


def head_block_mask(scale):
    row = lax.broadcasted_iota(jnp.int32, (LANE, LANE), 0) // HD
    col = lax.broadcasted_iota(jnp.int32, (LANE, LANE), 1) // HD
    return jnp.where(row == col, F32(scale), F32(0.0))


class Slots:
    def __init__(self, up, nh):
        self.up_in, self.up_out = 0, up
        self.head_in = 2 * up
        self.head_col = 2 * up + nh
        self.head_out = 2 * up + 2 * nh
        self.head_abs = 2 * up + 3 * nh
        self.low = 2 * up + 4 * nh
        self.up, self.nh = up, nh


def gather_weights(table, slots, own, recv, to, kinds, width):
    size = own.shape[3]
    for u in range(slots.up):
        at = table[slots.up_in + u]
        for low, src in ((table[slots.low], own), (1 - table[slots.low], recv)):
            rows = rows_at((2 * u + low) * size, size)
            for k in range(kinds):
                to[rows, k * width : (k + 1) * width] = src[at, 0, k]


def scatter_grads(table, slots, left, right, keep, send, kinds, width):
    size = keep.shape[3]
    for low, to in ((table[slots.low], keep), (1 - table[slots.low], send)):
        lhs = [left[rows_at((2 * u + low) * size, size), :] for u in range(slots.up)]
        value = dot(jnp.concatenate(lhs, axis=0), right).astype(BF16)
        for u in range(slots.up):
            at = table[slots.up_out + u]
            for i, k in enumerate(kinds):
                to[at, 0, k] = value[u * size : (u + 1) * size, i * width : (i + 1) * width]


def attn_kernel(
    table, n1, s0, own, recv, hp, rp,
    q_o, k_o, v_o, cv_o, at_o, s1_o, n2_o, n2t_o,
    wbuf, qs, ks, vs, fs, vp,
    *, imgs, slots,
):
    j = pl.program_id(0)
    rows = SEQ * imgs
    grid_row = GRID * imgs
    first = (3 * GRID - 1) * imgs

    @pl.when(j == 0)
    def _():
        for ref in (qs, ks, vs):
            ref[rows:] = jnp.zeros((ref.shape[0] - rows, LANE), F32)
        vp[0:first] = jnp.zeros((first, LANE), F32)
        vp[first + rows :] = jnp.zeros((vp.shape[0] - first - rows, LANE), F32)
        s1_o[...] = s0[...] + rp[14:15]

    gather_weights(table, slots, own, recv, wbuf, 4, LANE)
    chunk = 10 * imgs
    for r in range(0, rows, chunk):
        qkv = dot(n1[r : r + chunk], wbuf[:, 0 : 3 * LANE])
        q = qkv[:, 0:LANE] + hp[50:51]
        qs[r : r + chunk] = q
        q_o[0, r : r + chunk] = q
        ks[r : r + chunk] = qkv[:, LANE : 2 * LANE]
        v = qkv[:, 2 * LANE :] + hp[51:52]
        vs[r : r + chunk] = v
        v_o[0, r : r + chunk] = v
        vp[first + r : first + r + chunk] = v
    vp[first : first + imgs] = jnp.zeros((imgs, LANE), F32)
    keys = ks[0:rows].reshape(SEQ, imgs, LANE)
    expo = jnp.exp(keys - jnp.max(keys, axis=0, keepdims=True))
    soft = (expo / jnp.sum(expo, axis=0, keepdims=True)).reshape(rows, LANE)
    ks[0:rows] = soft
    k_o[0] = soft
    scale = head_block_mask(HD**-0.5)

    def image_body(i, carry):
        at = pl.ds(i, PAD_TOKENS, stride=imgs)
        ctx = dot(ks[at, :].astype(BF16), vs[at, :].astype(BF16), TN) * scale
        fs[at, :] = dot(qs[at, :].astype(BF16), ctx.astype(BF16))
        return carry

    lax.fori_loop(0, imgs, image_body, 0, unroll=4)
    at_o[0, 0:imgs] = fs[0:imgs].astype(BF16)
    cv_o[0, 0:imgs] = jnp.zeros((imgs, LANE), F32)
    everything = slice(0, LANE)

    def conv_body(y, carry):
        taps = [hp[t : t + 1] for t in range(TAPS)]
        acc = conv_row(vp, taps, 3, y, everything, imgs, False)
        for x in range(GRID):
            at = rows_at(imgs + y * grid_row + x * imgs, imgs)
            value = acc[x] + hp[49:50]
            cv_o[0, at] = value
            at_o[0, at] = (fs[at] + qs[at] * value).astype(BF16)
        return carry

    lax.fori_loop(0, GRID, conv_body, 0)
    s1_o[...] += dot(at_o[0], wbuf[:, 3 * LANE :], NT)

    @pl.when(j == pl.num_programs(0) - 1)
    def _():
        step = 5 * imgs

        def norm_body(r, carry):
            at = rows_at(r * step, step)
            unit, _ = norm_parts(s1_o[at, :])
            n2_o[at, :] = (unit * rp[12:13] + rp[13:14]).astype(BF16)
            return carry

        lax.fori_loop(0, rows // step, norm_body, 0)
        transposed(n2t_o, n2_o, rows)


def mlp_kernel(
    table, n2, n2t, og, ogt, s1, own, recv, ub, rp,
    out_o, gn2_o, keep_o, send_o, ubg_o,
    wbuf, hs, ds, hb, gb, oacc,
    *, imgs, slots, hid,
):
    j = pl.program_id(0)
    rows = SEQ * imgs
    gather_weights(table, slots, own, recv, wbuf, 2, hid)
    hs[...] = dot(n2[...], wbuf[:, 0:hid]) + ub[0]
    ds[...] = dot(og[...], wbuf[:, hid:])
    step = 2 * imgs

    def gelu_body(r, total):
        at = rows_at(r * step, step)
        pre = hs[at, :]
        cdf = 0.5 * (1.0 + lax.erf(pre * F32(0.5**0.5)))
        pdf = jnp.exp(-0.5 * pre * pre) * F32(0.3989422804014327)
        hb[at, :] = (pre * cdf).astype(BF16)
        grad = (ds[at, :] * (cdf + pre * pdf)).astype(BF16)
        gb[at, :] = grad
        wide = grad.astype(F32).reshape(step // 8, 8, hid)
        return total + jnp.sum(wide, axis=0)

    total = lax.fori_loop(0, rows // step, gelu_body, jnp.zeros((8, hid), F32))
    ubg_o[0] = jnp.broadcast_to(jnp.sum(total, axis=0, keepdims=True), (8, hid))

    @pl.when(j == 0)
    def _():
        oacc[...] = s1[...] + rp[15:16]
        gn2_o[...] = jnp.zeros(gn2_o.shape, F32)

    chunk = 10 * imgs
    for r in range(0, rows, chunk):
        at = slice(r, r + chunk)
        oacc[at] += dot(hb[at], wbuf[:, hid:], NT)
        gn2_o[at] += dot(gb[at], wbuf[:, 0:hid], NT)
    scatter_grads(table, slots, n2t, gb[...], keep_o, send_o, (0,), hid)
    scatter_grads(table, slots, ogt, hb[...], keep_o, send_o, (1,), hid)

    @pl.when(j == pl.num_programs(0) - 1)
    def _():
        out_o[...] = oacc[...].astype(BF16)


def mid_kernel(gn2, s1, og, rp, gs1_o, gal_o, galt_o, rep_o, *, imgs):
    rows, width = s1.shape
    part = 5 * imgs

    def fold(v):
        return jnp.sum(v.reshape(part // 8, 8, width), axis=0)

    def back_body(r, sums):
        at = rows_at(r * part, part)
        grad = gn2[at, :]
        unit, inv = norm_parts(s1[at, :])
        one = og[at, :].astype(F32) + norm_back(grad, rp[12:13], unit, inv)
        gs1_o[at, :] = one
        low = one.astype(BF16)
        gal_o[at, :] = low
        return (
            sums[0] + fold(grad * unit),
            sums[1] + fold(grad),
            sums[2] + fold(low.astype(F32)),
        )

    zero = jnp.zeros((8, width), F32)
    sums = lax.fori_loop(0, rows // part, back_body, (zero, zero, zero))
    rep_o[...] = jnp.concatenate(
        [jnp.sum(s, axis=0, keepdims=True) for s in sums] + [jnp.zeros((5, width), F32)], axis=0
    )
    transposed(galt_o, gal_o, rows)


def attn_back_kernel(*refs, imgs, slots, begin):
    table, n1t, gal, galt, own, recv, hp, q_i, k_i, v_i, cv, at_i = refs[:12]
    refs = refs[12:]
    if begin:
        gn1_i, refs = refs[0], refs[1:]
    keep_o, send_o, gn1_o, hg_o, wbuf, qs, ks, vs, gs, fq, fk, fv, vp, gp, gqkv = refs
    j = pl.program_id(0)
    rows = SEQ * imgs
    grid_row = GRID * imgs
    first = (3 * GRID - 1) * imgs

    @pl.when(j == 0)
    def _():
        for ref in (qs, ks, vs, gs):
            ref[rows:] = jnp.zeros((ref.shape[0] - rows, LANE), F32)
        for ref in (vp, gp):
            ref[0:first] = jnp.zeros((first, LANE), F32)
            ref[first + rows :] = jnp.zeros((ref.shape[0] - first - rows, LANE), F32)
        gn1_o[...] = gn1_i[...] if begin else jnp.zeros(gn1_o.shape, F32)

    gather_weights(table, slots, own, recv, wbuf, 4, LANE)
    chunk = 10 * imgs
    for r in range(0, rows, chunk):
        at = slice(r, r + chunk)
        grad = dot(gal[at], wbuf[:, 3 * LANE :])
        gs[at] = grad
        q = q_i[0, at]
        v = v_i[0, at]
        qs[at] = q
        ks[at] = k_i[0, at]
        vs[at] = v
        vp[first + r : first + r + chunk] = v
        gp[first + r : first + r + chunk] = grad * q
    vp[first : first + imgs] = jnp.zeros((imgs, LANE), F32)
    gp[first : first + imgs] = jnp.zeros((imgs, LANE), F32)
    scale = head_block_mask(HD**-0.5)

    def image_body(i, carry):
        at = pl.ds(i, PAD_TOKENS, stride=imgs)
        q = qs[at, :].astype(BF16)
        k = ks[at, :].astype(BF16)
        v = vs[at, :].astype(BF16)
        g = gs[at, :].astype(BF16)
        ctx = (dot(k, v, TN) * scale).astype(BF16)
        gctx = (dot(q, g, TN) * scale).astype(BF16)
        fq[at, :] = dot(g, ctx, NT)
        fk[at, :] = dot(v, gctx, NT)
        fv[at, :] = dot(k, gctx)
        return carry

    lax.fori_loop(0, imgs, image_body, 0, unroll=4)
    soft = ks[0:rows].reshape(SEQ, imgs, LANE)
    gsoft = fk[0:rows].reshape(SEQ, imgs, LANE)
    total = jnp.sum(soft * gsoft, axis=0, keepdims=True)
    gqkv[:, LANE : 2 * LANE] = (soft * (gsoft - total)).reshape(rows, LANE).astype(BF16)
    gquery = (fq[0:rows] + gs[0:rows] * cv[0]).astype(BF16)
    gqkv[:, 0:LANE] = gquery
    everything = slice(0, LANE)
    low = fv[0:imgs].astype(BF16)
    gqkv[0:imgs, 2 * LANE :] = low

    def conv_body(y, carry):
        taps = [hp[t : t + 1] for t in range(TAPS)]
        acc = conv_row(gp, taps, 3, y, everything, imgs, True)
        for x in range(GRID):
            at = rows_at(imgs + y * grid_row + x * imgs, imgs)
            value = (fv[at] + acc[x]).astype(BF16)
            gqkv[at, 2 * LANE :] = value
            carry = carry + value.astype(F32)
        return carry

    value_sum = lax.fori_loop(0, GRID, conv_body, low.astype(F32))
    side = GRID
    zero = jnp.zeros((imgs, LANE), F32)
    for a in range(side):

        def tap_body(y, accs, a=a):
            start = (y + 3) * grid_row
            grad_row = [gp[rows_at(start + x * imgs, imgs)] for x in range(GRID)]
            return tap_products(vp, grad_row, y, 3, everything, imgs, a, accs)

        accs = lax.fori_loop(max(0, 3 - a), GRID - max(0, a - 3), tap_body, (zero,) * side)
        hg_o[0, a * side : (a + 1) * side] = jnp.concatenate(
            [jnp.sum(acc, axis=0, keepdims=True) for acc in accs], axis=0
        )
    conv_sum = jnp.sum(gp[first : first + rows], axis=0, keepdims=True)
    query_sum = jnp.sum(gquery.astype(F32), axis=0, keepdims=True)
    hg_o[0, 49:50] = conv_sum
    hg_o[0, 50:51] = query_sum
    hg_o[0, 51:52] = jnp.sum(value_sum, axis=0, keepdims=True)
    hg_o[0, 52:56] = jnp.zeros((4, LANE), F32)
    for r in range(0, rows, chunk):
        gn1_o[r : r + chunk] += dot(gqkv[r : r + chunk], wbuf[:, 0 : 3 * LANE], NT)
    scatter_grads(table, slots, n1t, gqkv[...], keep_o, send_o, (0, 1, 2), LANE)
    scatter_grads(table, slots, galt, at_i[0], keep_o, send_o, (3,), LANE)


def tail_kernel(
    table, s0, gs1, gn1, xp, rp, hg_one, hg_two, ubg, rep_mid, cot, mask,
    ig_o, small_o, gz, xs, res, sm, rep,
    *, imgs, slots,
):
    rows, width = s0.shape
    row = GRID * imgs
    base = row - imgs
    part = 5 * imgs
    for ref in (gz, xs):
        ref[0:row] = jnp.zeros((row, width), F32)
        ref[8 * row : 9 * row] = jnp.zeros((row, width), F32)

    def fold(v):
        return jnp.sum(v.reshape(-1, 8, width), axis=0)

    def back_body(r, sums):
        at = rows_at(r * part, part)
        grad = gn1[at, :]
        unit, inv = norm_parts(s0[at, :])
        to = rows_at(base + r * part, part)
        gz[to, :] = gs1[at, :] + norm_back(grad, rp[10:11], unit, inv)
        xs[to, :] = xp[at, :].astype(F32)
        return (sums[0] + fold(grad * unit), sums[1] + fold(grad))

    zero = jnp.zeros((8, width), F32)
    sums = lax.fori_loop(0, rows // part, back_body, (zero, zero))
    res[0:imgs] = gz[base : base + imgs]
    gz[base : base + imgs] = jnp.zeros((imgs, width), F32)
    xs[base : base + imgs] = jnp.zeros((imgs, width), F32)
    rep[9:10] = jnp.sum(gz[row : 8 * row], axis=0, keepdims=True)
    rep[10:11] = jnp.sum(sums[0], axis=0, keepdims=True)
    rep[11:12] = jnp.sum(sums[1], axis=0, keepdims=True)
    rep[12:15] = rep_mid[0:3]
    rep[15:16] = cot[0:1]

    def conv_body(y, carry):
        for c in range(0, width, LANE):
            cols = slice(c, c + LANE)
            taps = [rp[t : t + 1, cols] for t in range(9)]
            acc = conv_row(gz, taps, 1, y, cols, imgs, True)
            for x in range(GRID):
                here = gz[rows_at((y + 1) * row + x * imgs, imgs), cols]
                res[rows_at(imgs + y * row + x * imgs, imgs), cols] = here + acc[x]
        return carry

    lax.fori_loop(0, GRID, conv_body, 0)
    nothing = jnp.zeros((imgs, LANE), F32)
    for c in range(0, width, LANE):
        cols = slice(c, c + LANE)

        def tap_body(y, accs, cols=cols):
            start = (y + 1) * row
            grad_row = [gz[rows_at(start + x * imgs, imgs), cols] for x in range(GRID)]
            out = []
            for a in range(3):
                out.extend(tap_products(xs, grad_row, y, 1, cols, imgs, a, accs[3 * a : 3 * a + 3]))
            return tuple(out)

        accs = lax.fori_loop(0, GRID, tap_body, (nothing,) * 9)
        rep[0:9, cols] = jnp.concatenate(
            [jnp.sum(acc, axis=0, keepdims=True) for acc in accs], axis=0
        )
    ig_o[...] = res[...].astype(BF16)

    sm[:, 72:] = jnp.zeros((sm.shape[0], sm.shape[1] - 72, LANE), F32)
    half = slots.nh // 2
    for k in range(slots.nh):
        at = table[slots.head_col + k]
        sm[at, 0:56] = hg_one[k] if k < half else hg_two[k - half]
    for t in range(width // LANE):
        cols = slice(t * LANE, (t + 1) * LANE)
        sm[t, 0:TAPS] = sm[t, 0:TAPS] * mask[:, cols]
        for r in range(ubg.shape[0]):
            sm[t, 52 + r : 53 + r] = ubg[r, 0:1, cols]
        sm[t, 56:72] = rep[:, cols]
    span = small_o.shape[2]
    for u in range(small_o.shape[0]):
        for t in range(width // LANE):
            at = table[slots.up_out + u]
            to = table[slots.head_out + t]
            small_o[at, to] = sm[t, u * span : (u + 1) * span]


def whole(shape):
    return pl.BlockSpec(shape, lambda *_: (0,) * len(shape))


def tap_mask(radius):
    reach = jnp.repeat(radius, HD)
    taps = lax.broadcasted_iota(jnp.int32, (TAPS, reach.shape[0]), 0)
    vertical = jnp.abs(taps // 7 - 3)
    horizontal = jnp.abs(taps % 7 - 3)
    inside = (vertical <= reach[None, :]) & (horizontal <= reach[None, :])
    return inside.astype(F32)


def adam_store(outs, raw, weight, first, second, average, clip, decay):
    grad = raw * clip
    first_new = BETA_FIRST * first + (1.0 - BETA_FIRST) * grad
    second_new = BETA_SECOND * second + (1.0 - BETA_SECOND) * grad * grad
    moment_hat = first_new / (1.0 - BETA_FIRST**STEP)
    second_hat = second_new / (1.0 - BETA_SECOND**STEP)
    weight_new = weight - LEARN_RATE * (
        moment_hat / (jnp.sqrt(second_hat) + ADAM_EPS) + decay * weight
    )
    outs[0][...] = grad
    outs[1][...] = first_new
    outs[2][...] = second_new
    outs[3][...] = weight_new
    outs[4][...] = weight_new.astype(BF16)
    outs[5][...] = AVG_KEEP * average + (1.0 - AVG_KEEP) * weight_new


def adam_kernel(table, shares, one, two, *refs, slots, span):
    ins, norm_o, outs, sm = refs[:24], refs[24], refs[25:61], refs[61]
    tiles = sm.shape[0]
    total = jnp.zeros((1, 1), F32)
    for u in range(slots.up):
        for t in range(tiles):
            share = shares[table[slots.up_in + u], table[slots.head_abs + t]]
            sm[t, u * span : (u + 1) * span] = share[0:span]
            total = total + jnp.sum(share[0:span] * share[0:span], keepdims=True)
            total = total + share[span : span + 1, 0:1]
    norm = jnp.sqrt(total)
    clip = jnp.minimum(1.0, CLIP_NORM / (norm + 1e-06))
    norm_o[...] = jnp.broadcast_to(norm, norm_o.shape)
    raws = (one[0:3], one[3], two[0], two[1])
    for p, raw in enumerate(raws):
        state = [ref[...] for ref in ins[4 * p : 4 * p + 4]]
        adam_store(outs[6 * p : 6 * p + 6], raw, *state, clip, WEIGHT_DECAY)
    for p, (begin, end) in ((4, (0, 56)), (5, (56, 72))):
        for t in range(tiles):
            cols = slice(t * LANE, (t + 1) * LANE)
            state = [ref[:, cols] for ref in ins[4 * p : 4 * p + 4]]
            to = [ref.at[:, cols] for ref in outs[6 * p : 6 * p + 6]]
            adam_store(to, sm[t, begin:end], *state, clip, 0.0)


def square_sum(values):
    return jnp.sum(values * values)


class Ring:
    def __init__(self, nd, nh):
        self.low = 2 if nd % 2 == 0 else 1
        self.nd, self.nh, self.up = nd, nh, nd // self.low
        dp = lax.axis_index("dp")
        self.mine = (dp % self.low, dp // self.low, lax.axis_index("head"))

    def turn(self, value, stage, k=1):
        axis = "head" if stage == "head" else "dp"
        low, up = self.low, self.up
        if stage == "head":
            pairs = [(i, (i + k) % self.nh) for i in range(self.nh)]
        elif stage == "up":
            pairs = [(i, (i // low + k) % up * low + i % low) for i in range(self.nd)]
        else:
            pairs = [(i, i // low * low + (i % low + k) % low) for i in range(self.nd)]
        return lax.ppermute(value, axis, pairs)

    def gather(self, shard, stage):
        size = self.nh if stage == "head" else self.up
        return jnp.stack([shard] + [self.turn(shard, stage, k) for k in range(1, size)])

    def scatter(self, parts, stage):
        total = parts[0].astype(F32)
        for k in range(1, len(parts)):
            total = total + self.turn(parts[k], stage, k).astype(F32)
        return total

    def swap_sum(self, keep, send):
        return keep.astype(F32) + self.turn(send, "low").astype(F32)


def per_device(
    block_input,
    out_grad,
    kernel_radius,
    qkv_weight,
    qkv_first,
    qkv_second,
    qkv_average,
    proj_weight,
    proj_first,
    proj_second,
    proj_average,
    up_weight,
    up_first,
    up_second,
    up_average,
    down_weight,
    down_first,
    down_second,
    down_average,
    head_params,
    head_first,
    head_second,
    head_average,
    rep_params,
    rep_first,
    rep_second,
    rep_average,
):
    nd, nh = lax.axis_size("dp"), lax.axis_size("head")
    imgs, _, width = block_input.shape
    rows = SEQ * imgs
    span = qkv_weight.shape[0]
    hid = up_weight.shape[1]
    ring = Ring(nd, nh)
    staged = span % 16 == 0 and ring.low == 2
    tiles = width // LANE

    x = block_input.transpose(1, 0, 2).reshape(rows, width)
    cot = out_grad.transpose(1, 0, 2).reshape(rows, width)
    kinds_first = lambda v: v.transpose(1, 0, 2)
    pack_one = jnp.concatenate(
        [kinds_first(qkv_weight).astype(BF16), proj_weight.astype(BF16)[None]], axis=0
    )
    pack_two = jnp.stack([up_weight.astype(BF16), down_weight.astype(BF16)])
    up = ring.up if staged else 4
    slots = Slots(up, nh)
    ups = jnp.arange(up, dtype=jnp.int32)
    heads = jnp.arange(nh, dtype=jnp.int32)
    if staged:
        size = span
        my_low, my_up, z = ring.mine
        parts = [
            (my_up - ups) % up,
            (ups - my_up) % up,
            (nh - heads) % nh,
            (z + heads) % nh,
            (heads - z) % nh,
            (z - heads) % nh,
            my_low[None],
        ]
        gathered_one = ring.gather(ring.gather(pack_one, "head"), "up")
        other_one = ring.turn(gathered_one, "low")
        gathered_two = ring.gather(ring.gather(pack_two, "head"), "up")
        other_two = ring.turn(gathered_two, "low")
    else:
        size = width // (2 * up)
        parts = [ups, ups, heads, heads, heads, heads, jnp.zeros((1,), jnp.int32)]

        def spread(pack):
            kinds = pack.shape[0]
            full = lax.all_gather(pack, ("dp", "head"), axis=0)
            full = full.reshape(nd, nh, kinds, span, -1).transpose(1, 2, 0, 3, 4)
            full = full.reshape(nh, kinds, up, 2, size, -1).transpose(3, 2, 0, 1, 4, 5)
            return full[0], full[1]

        gathered_one, other_one = spread(pack_one)
        gathered_two, other_two = spread(pack_two)
    table = jnp.concatenate([p.astype(jnp.int32) for p in parts])

    shape = jax.ShapeDtypeStruct

    def params(*semantics):
        return pltpu.CompilerParams(
            dimension_semantics=semantics or None, vmem_limit_bytes=60 * 1024 * 1024
        )

    def cost(us):
        return pl.CostEstimate(flops=0, transcendentals=0, bytes_accessed=int(us * 3.0e6))

    def weight_spec(kinds, cols):
        return pl.BlockSpec(
            (up, 1, kinds, size, cols), lambda j, s: (0, s[slots.head_in + j], 0, 0, 0)
        )

    full = whole((rows, width))
    turned = whole((width, rows))
    rp_spec = whole((16, width))
    wide = shape((rows, width), F32)
    low = shape((rows, width), BF16)
    low_turned = shape((width, rows), BF16)

    stream_zero, normed_one, normed_one_t, cot_t, cot_sum = pl.pallas_call(
        partial(pre_kernel, imgs=imgs),
        out_shape=(wide, low, low_turned, low_turned, shape((8, width), F32)),
        scratch_shapes=[pltpu.VMEM((9 * GRID * imgs, width), F32)],
        compiler_params=params(),
        cost_estimate=cost(9),
        name="pre",
    )(x, cot, rep_params)

    mask = tap_mask(kernel_radius)
    head_rows = jnp.concatenate([head_params[:TAPS] * mask, head_params[TAPS : TAPS + 7]], axis=0)
    bias_up = head_params[TAPS + 3 :].reshape(nh, 1, hid)
    per_head = shape((nh, rows, LANE), F32)
    tile_spec = pl.BlockSpec((1, rows, LANE), lambda j, s: (j, 0, 0))
    padded = pltpu.VMEM((PAD_TOKENS * imgs, LANE), F32)
    framed = pltpu.VMEM((13 * GRID * imgs, LANE), F32)
    w_one = pltpu.VMEM((width, 4 * LANE), BF16)
    hp_spec = pl.BlockSpec((56, LANE), lambda j, s: (0, s[slots.head_col + j]))
    queries, keys_soft, values, conv_val, attended, stream_one, normed_two, normed_two_t = (
        pl.pallas_call(
            partial(attn_kernel, imgs=imgs, slots=slots),
            out_shape=(
                per_head,
                per_head,
                per_head,
                per_head,
                shape((nh, rows, LANE), BF16),
                wide,
                low,
                low_turned,
            ),
            grid_spec=pltpu.PrefetchScalarGridSpec(
                num_scalar_prefetch=1,
                grid=(nh,),
                in_specs=[full, full] + [weight_spec(4, LANE)] * 2 + [hp_spec, rp_spec],
                out_specs=[tile_spec] * 5 + [full, full, turned],
                scratch_shapes=[w_one] + [padded] * 4 + [framed],
            ),
            compiler_params=params("arbitrary"),
            cost_estimate=cost(21),
            name="attn",
        )(table, normed_one, stream_zero, gathered_one, other_one, head_rows, rep_params)
    )

    two_grads = shape((up, nh, 2, size, hid), BF16)
    two_spec = pl.BlockSpec((up, 1, 2, size, hid), lambda j, s: (0, j, 0, 0, 0))
    output, grad_norm_two, keep_two, send_two, bias_grad = pl.pallas_call(
        partial(mlp_kernel, imgs=imgs, slots=slots, hid=hid),
        out_shape=(low, wide, two_grads, two_grads, shape((nh, 8, hid), F32)),
        grid_spec=pltpu.PrefetchScalarGridSpec(
            num_scalar_prefetch=1,
            grid=(nh,),
            in_specs=[full, turned, full, turned, full]
            + [weight_spec(2, hid)] * 2
            + [pl.BlockSpec((1, 1, hid), lambda j, s: (s[slots.head_col + j], 0, 0)), rp_spec],
            out_specs=[
                full,
                full,
                two_spec,
                two_spec,
                pl.BlockSpec((1, 8, hid), lambda j, s: (s[slots.head_col + j], 0, 0)),
            ],
            scratch_shapes=[
                pltpu.VMEM((width, 2 * hid), BF16),
                pltpu.VMEM((rows, hid), F32),
                pltpu.VMEM((rows, hid), F32),
                pltpu.VMEM((rows, hid), BF16),
                pltpu.VMEM((rows, hid), BF16),
                pltpu.VMEM((rows, width), F32),
            ],
        ),
        compiler_params=params("arbitrary"),
        cost_estimate=cost(26),
        name="mlp",
    )(
        table,
        normed_two,
        normed_two_t,
        cot,
        cot_t,
        stream_one,
        gathered_two,
        other_two,
        bias_up,
        rep_params,
    )

    grad_one, grad_low, grad_low_t, rep_mid = pl.pallas_call(
        partial(mid_kernel, imgs=imgs),
        out_shape=(wide, low, low_turned, shape((8, width), F32)),
        compiler_params=params(),
        cost_estimate=cost(4),
        name="mid",
    )(grad_norm_two, stream_one, cot, rep_params)

    half = nh // 2
    one_grads = shape((up, half, 4, size, LANE), BF16)
    one_spec = pl.BlockSpec((up, 1, 4, size, LANE), lambda j, s: (0, j, 0, 0, 0))

    def attn_back(begin, so_far):
        def at_head(j, s):
            return (0, s[slots.head_in + begin + j], 0, 0, 0)

        weights = pl.BlockSpec((up, 1, 4, size, LANE), at_head)
        tile = pl.BlockSpec((1, rows, LANE), lambda j, s: (begin + j, 0, 0))
        taps = pl.BlockSpec((56, LANE), lambda j, s: (0, s[slots.head_col + begin + j]))
        return pl.pallas_call(
            partial(attn_back_kernel, imgs=imgs, slots=slots, begin=begin),
            out_shape=(one_grads, one_grads, wide, shape((half, 56, LANE), F32)),
            grid_spec=pltpu.PrefetchScalarGridSpec(
                num_scalar_prefetch=1,
                grid=(half,),
                in_specs=[turned, full, turned, weights, weights, taps]
                + [tile] * 5
                + [full] * len(so_far),
                out_specs=[
                    one_spec,
                    one_spec,
                    full,
                    pl.BlockSpec((1, 56, LANE), lambda j, s: (j, 0, 0)),
                ],
                scratch_shapes=[w_one]
                + [padded] * 7
                + [framed] * 2
                + [pltpu.VMEM((rows, 3 * LANE), BF16)],
            ),
            compiler_params=params("arbitrary"),
            cost_estimate=cost(19),
            name="attn_back_b" if begin else "attn_back_a",
        )(
            table,
            normed_one_t,
            grad_low,
            grad_low_t,
            gathered_one,
            other_one,
            head_rows,
            queries,
            keys_soft,
            values,
            conv_val,
            attended,
            *so_far,
        )

    keep_a, send_a, grad_half, head_a = attn_back(0, ())
    keep_b, send_b, grad_norm_one, head_b = attn_back(half, (grad_half,))

    small_rows = 8 * pl.cdiv(72, 8 * up)
    smem = pl.BlockSpec(memory_space=pltpu.SMEM)
    vmem = pl.BlockSpec(memory_space=pltpu.VMEM)
    input_grad, small = pl.pallas_call(
        partial(tail_kernel, imgs=imgs, slots=slots),
        out_shape=(low, shape((up, tiles, small_rows, LANE), F32)),
        in_specs=[smem] + [vmem] * 11,
        scratch_shapes=[
            pltpu.VMEM((9 * GRID * imgs, width), F32),
            pltpu.VMEM((9 * GRID * imgs, width), F32),
            pltpu.VMEM((rows, width), F32),
            pltpu.VMEM((tiles, up * small_rows, LANE), F32),
            pltpu.VMEM((16, width), F32),
        ],
        compiler_params=params(),
        cost_estimate=cost(9),
        name="tail",
    )(
        table,
        stream_zero,
        grad_one,
        grad_norm_one,
        x,
        rep_params,
        head_a,
        head_b,
        bias_grad,
        rep_mid,
        cot_sum,
        mask,
    )

    if staged:
        two = ring.swap_sum(keep_two, send_two).astype(BF16)
        two = ring.scatter(two, "up").astype(BF16)
        two = ring.scatter(two, "head")
        one_a = ring.swap_sum(keep_a, send_a).astype(BF16)
        one_b = ring.swap_sum(keep_b, send_b).astype(BF16)
        one = ring.scatter(jnp.concatenate([one_a, one_b], axis=1), "up").astype(BF16)
        one = ring.scatter(one, "head")
        share = ring.swap_sum(small, small)
        share = ring.scatter(share, "up")
        share = ring.scatter(share, "head")
        mine = jnp.zeros((8, LANE), F32) + (square_sum(one) + square_sum(two))
        mine = ring.swap_sum(mine, mine)
        shares = jnp.concatenate([share, mine], axis=0)
        shares = ring.gather(ring.gather(shares, "head"), "up")
    else:

        def owned(even, odd):
            full = jnp.stack([even, odd], axis=1)
            kinds = full.shape[3]
            full = full.transpose(2, 3, 0, 1, 4, 5).reshape(nh, kinds, nd, span, -1)
            full = full.transpose(2, 0, 1, 3, 4).reshape(nd * nh, kinds, span, -1)
            return lax.psum_scatter(full, ("dp", "head"), scatter_dimension=0).astype(F32)

        two = owned(keep_two, send_two)
        one = owned(
            jnp.concatenate([keep_a, keep_b], axis=1), jnp.concatenate([send_a, send_b], axis=1)
        )
        small_sum, mat_total = lax.psum(
            (small, square_sum(one) + square_sum(two)), ("dp", "head")
        )
        first_cell = (lax.broadcasted_iota(jnp.int32, (up, tiles, 8, LANE), 0) == 0) & (
            lax.broadcasted_iota(jnp.int32, (up, tiles, 8, LANE), 1) == 0
        )
        mine = jnp.where(first_cell, mat_total, F32(0.0))
        shares = jnp.concatenate([small_sum, mine], axis=2)

    states = (
        *(kinds_first(v) for v in (qkv_weight, qkv_first, qkv_second, qkv_average)),
        *(proj_weight, proj_first, proj_second, proj_average),
        *(up_weight, up_first, up_second, up_average),
        *(down_weight, down_first, down_second, down_average),
        *(head_params, head_first, head_second, head_average),
        *(rep_params, rep_first, rep_second, rep_average),
    )
    results = []
    for p in range(6):
        like = states[4 * p].shape
        results += [shape(like, BF16 if k == 4 else F32) for k in range(6)]
    norm, *outs = pl.pallas_call(
        partial(adam_kernel, slots=slots, span=small_rows),
        out_shape=(shape((8, LANE), F32), *results),
        in_specs=[smem] + [vmem] * 27,
        scratch_shapes=[pltpu.VMEM((tiles, up * small_rows, LANE), F32)],
        compiler_params=params(),
        cost_estimate=cost(4),
        name="adam",
    )(table, shares, one, two, *states)
    outs[0:6] = [kinds_first(v) for v in outs[0:6]]

    def by_image(v):
        return v.reshape(SEQ, imgs, width).transpose(1, 0, 2)

    return (by_image(output), by_image(input_grad), norm[0, 0], *outs)


def solution(mesh):
    tokens = P(("dp", "head"), None, None)
    qkv = P("dp", None, "head")
    mat = P("dp", "head")
    in_specs = (tokens, tokens, P()) + (qkv,) * 4 + (mat,) * 12 + (P(),) * 8
    out_specs = (tokens, tokens, P()) + (qkv,) * 6 + (mat,) * 18 + (P(),) * 12

    return jax.shard_map(
        per_device, mesh=mesh, in_specs=in_specs, out_specs=out_specs, check_vma=False
    )
```

time: 298 us -> 280 us (0.940)
  other arithmetic: 30.1 us -> 10.6 us
  local copies, waits for them, and re-layouts: 17.7 us -> 3.84 us
  Pallas kernels: 111 us -> 121 us
  waiting for transfers between devices: 73.1 us -> 77.5 us
  starting transfers between devices: 60.3 us -> 64.3 us
    pallas_call x5 -> x8, Pallas kernels: 111 us -> 121 us  [the longest x2 43.6 us: attn_back(): pl.pallas_call(partial(attn_back_kernel, imgs=imgs, slots=slots, begin=be...]
    another operation x11 -> x9, other arithmetic: 10.9 us -> 2.64 us  [gather(): jnp.stack([shard] + [self.turn(shard, stage, k) for k in range(1, size)])]
    unnamed x99 -> x22, local copies, waits for them, and re-layouts: 7.56 us -> 1.03 us
    convert_element_type x13 -> x7, other arithmetic: 8.79 us -> 2.38 us  [the longest x1 0.76 us: tap_mask(): return inside.astype(F32)]
    slice x7 -> x1, local copies, waits for them, and re-layouts: 6.66 us -> 1.19 us  [per_device(): return (by_image(output), by_image(input_grad), norm[0, 0], *outs)]
    ppermute x42 -> x43, waiting for transfers between devices: 73.1 us -> 77.5 us  [turn(): return lax.ppermute(value, axis, pairs)]
    add x10 -> x4, other arithmetic: 4.96 us -> 0.98 us  [the longest x2 0.96 us: swap_sum(): return keep.astype(F32) + self.turn(send, 'low').astype(F32)]
    ppermute x42 -> x43, starting transfers between devices: 60.3 us -> 64.3 us  [turn(): return lax.ppermute(value, axis, pairs)]
  transfers between devices with their start and end apart: 42 -> 43, of which waited for: 20 -> 30; matrix products, arithmetic and copies ran while one was open for 9% -> 3% of each run, Pallas kernels for 10% -> 32%
where the time goes in v2:
time: 280 us; the launch traced here: 279 us
  Pallas kernels  121 us (43%)
  waiting for transfers between devices  77.5 us (28%)
  starting transfers between devices  64.3 us (23%)
  other arithmetic  10.6 us (4%)
  local copies, waits for them, and re-layouts  3.84 us (1%)
    ppermute x43, waiting for transfers between devices, turn(): return lax.ppermute(value, axis, pairs)  77.5 us
    ppermute x43, starting transfers between devices, turn(): return lax.ppermute(value, axis, pairs)  64.3 us
    pallas_call x2, Pallas kernels, attn_back(): pl.pallas_call(partial(attn_back_kernel, imgs=imgs, slots=slots, begin=be...  43.6 us
    pallas_call x1, Pallas kernels, per_device(): pl.pallas_call(partial(mlp_kernel, imgs=imgs, slots=slots, hid=hid), out_...  26.8 us
    pallas_call x1, Pallas kernels, per_device(): pl.pallas_call(partial(attn_kernel, imgs=imgs, slots=slots), out_shape=(p...  23.3 us
    pallas_call x1, Pallas kernels, per_device(): pl.pallas_call(partial(tail_kernel, imgs=imgs, slots=slots), out_shape=(l...  9.53 us
    pallas_call x1, Pallas kernels, per_device(): pl.pallas_call(partial(mid_kernel, imgs=imgs), out_shape=(wide, low, low_...  6.98 us
    pallas_call x1, Pallas kernels, per_device(): pl.pallas_call(partial(pre_kernel, imgs=imgs), out_shape=(wide, low, low_...  6.75 us
  transfers between devices with their start and end apart: 43, of which 30 were waited for; matrix products, arithmetic and copies ran while one was open for 3% of the time, Pallas kernels for 32%

profile of v2, /device:TPU:0, one launch (start us, length us, event | category | flops | bytes accessed | tf_op | source)
XLA Modules:
  0.0 279.3 jit_solution(759706373690504426)
XLA Ops:
  1.7 3.1 %collective-permute-start.7 = (bf16[2,64,512]{2,1,0:T(8,128)(2,1)S(1)}, bf16[2,64,512]{2,1,0:T(8,128)(2,1)S(1)}, u32[]{:S(2)}, u32[]{:S(2)}) collective-permute-start(bf16[2,64,512]{2,1,0:T(8,128)(2,1)S(1)} %get-tuple-element.201), channel_id=1, source_target_pairs={{0,1},{1,2},{2,3},{3,0},{4,5},{5,6},{6,7},{7,4},{8,9},{9,10},{10,1... | collective-permute-start | bytes 393224 | tf_op jit(solution)/shard_map/ppermute | solution.py:578
  11.3 4.8 %collective-permute-done.8 = bf16[2,64,512]{2,1,0:T(8,128)(2,1)S(1)} collective-permute-done((bf16[2,64,512]{2,1,0:T(8,128)(2,1)S(1)}, bf16[2,64,512]{2,1,0:T(8,128)(2,1)S(1)}, u32[]{:S(2)}, u32[]{:S(2)}) %collective-permute-start.8) | collective-permute-done | bytes 131104 | tf_op jit(solution)/shard_map/ppermute | solution.py:578
  20.6 11.3 %collective-permute-done.10 = bf16[4,2,64,512]{3,2,1,0:T(8,128)(2,1)S(1)} collective-permute-done((bf16[4,2,64,512]{3,2,1,0:T(8,128)(2,1)S(1)}, bf16[4,2,64,512]{3,2,1,0:T(8,128)(2,1)S(1)}, u32[]{:S(2)}, u32[]{:S(2)}) %collective-permute-start.10) | collective-permute-done | bytes 524320 | tf_op jit(solution)/shard_map/ppermute | solution.py:578
  31.9 10.1 %collective-permute-done.11 = bf16[4,2,64,512]{3,2,1,0:T(8,128)(2,1)S(1)} collective-permute-done((bf16[4,2,64,512]{3,2,1,0:T(8,128)(2,1)S(1)}, bf16[4,2,64,512]{3,2,1,0:T(8,128)(2,1)S(1)}, u32[]{:S(2)}, u32[]{:S(2)}) %collective-permute-start.11) | collective-permute-done | bytes 524320 | tf_op jit(solution)/shard_map/ppermute | solution.py:578
  43.9 3.5 %collective-permute-start.2 = (bf16[4,64,128]{2,1,0:T(8,128)(2,1)S(1)}, bf16[4,64,128]{2,1,0:T(8,128)(2,1)S(1)}, u32[]{:S(2)}, u32[]{:S(2)}) collective-permute-start(bf16[4,64,128]{2,1,0:T(8,128)(2,1)S(1)} %get-tuple-element.205), channel_id=1, source_target_pairs={{0,3},{1,0},{2,1},{3,2},{4,7},{5,4},{6,5},{7,6},{8,11},{9,8},{10,9... | collective-permute-start | bytes 196616 | tf_op jit(solution)/shard_map/ppermute | solution.py:578
  50.0 4.1 %collective-permute-done = bf16[4,64,128]{2,1,0:T(8,128)(2,1)S(1)} collective-permute-done((bf16[4,64,128]{2,1,0:T(8,128)(2,1)S(1)}, bf16[4,64,128]{2,1,0:T(8,128)(2,1)S(1)}, u32[]{:S(2)}, u32[]{:S(2)}) %collective-permute-start) | collective-permute-done | bytes 65568 | tf_op jit(solution)/shard_map/ppermute | solution.py:578
  59.9 4.8 %collective-permute-done.3 = bf16[4,4,64,128]{3,2,1,0:T(8,128)(2,1)S(1)} collective-permute-done((bf16[4,4,64,128]{3,2,1,0:T(8,128)(2,1)S(1)}, bf16[4,4,64,128]{3,2,1,0:T(8,128)(2,1)S(1)}, u32[]{:S(2)}, u32[]{:S(2)}) %collective-permute-start.3) | collective-permute-done | bytes 262176 | tf_op jit(solution)/shard_map/ppermute | solution.py:578
  64.7 2.7 collective-permute-done.4
  68.5 6.7 %pre.1 = (f32[800,512]{1,0:T(8,128)}, bf16[800,512]{1,0:T(8,128)(2,1)}, bf16[512,800]{1,0:T(8,128)(2,1)}, bf16[512,800]{1,0:T(8,128)(2,1)}, f32[8,512]{1,0:T(8,128)}) custom-call(bf16[800,512]{1,0:T(8,128)(2,1)} %bitcast.138, bf16[800,512]{1,0:T(8,128)(2,1)} %bitcast.135, f32[16,512]{1,0:T(8,128)} %refs_20_.1), custom_call_target="tpu_custom_call" | custom-call | bytes 27000000 | tf_op jit(solution)/shard_map/pre/pallas_call | solution.py:696
  77.8 23.3 %attn.1 = (f32[4,800,128]{2,1,0:T(8,128)}, f32[4,800,128]{2,1,0:T(8,128)}, f32[4,800,128]{2,1,0:T(8,128)}, f32[4,800,128]{2,1,0:T(8,128)}, bf16[4,800,128]{2,1,0...) custom-call(s32[25]{0:T(128)} %concatenate.15.table.refs_0_, ...), custom_call_target="tpu_custom_call" | custom-call | bytes 63000000 | tf_op jit(solution)/shard_map/attn/pallas_call | solution.py:715
  101.1 26.8 %mlp.1 = (bf16[800,512]{1,0:T(8,128)(2,1)}, f32[800,512]{1,0:T(8,128)}, bf16[4,4,2,64,512]{4,3,2,1,0:T(8,128)(2,1)}, bf16[4,4,2,64,512]{4,3,2,1,0:T(8,128)(2,1)}, f32[4,8,512]{2,1,0:T(8,128)}) custom-call(s32[25]{0:T(128)} %concatenate.15.table.refs_0_, bf16[800,512]{1,0:T(8,128)(2,1)} %get-tuple-element.110.n2, bf16[512,800]{1,0:T(8,128)(2,1)} %get-tuple-element.111.n2t, ...), custom_call_target="tpu_custom_call" | custom-call | bytes 78000000 | tf_op jit(solution)/shard_map/mlp/pallas_call | solution.py:742
  129.1 7.0 %mid.1 = (f32[800,512]{1,0:T(8,128)}, bf16[800,512]{1,0:T(8,128)(2,1)}, bf16[512,800]{1,0:T(8,128)(2,1)}, f32[8,512]{1,0:T(8,128)}) custom-call(f32[800,512]{1,0:T(8,128)} %get-tuple-element.115.gn2, f32[800,512]{1,0:T(8,128)} %get-tuple-element.113.s1, bf16[800,512]{1,0:T(8,128)(2,1)} %bitcast.137, f32[16,512]{1,0:T(8,128)} %refs_20_.1), custom_call_target="tpu_custom_call" | custom-call | bytes 12000000 | tf_op jit(solution)/shard_map/mid/pallas_call | solution.py:783
  136.1 21.4 %attn_back_a.1 = (bf16[4,2,4,64,128]{4,3,2,1,0:T(8,128)(2,1)}, bf16[4,2,4,64,128]{4,3,2,1,0:T(8,128)(2,1)}, f32[800,512]{1,0:T(8,128)}, f32[2,56,128]{2,1,0:T(8,128)}) custom-call(s32[25]{0:T(128)} %concatenate.15.table.refs_0_, bf16[512,800]{1,0:T(8,128)(2,1)} %get-tuple-element.117.refs_1_, bf16[800,512]{1,0:T(8,128)(2,1)} %get-tuple-element.118.refs_2_, ...), custom_call_target="tpu_custom_call" | custom-call | bytes 57000000 | tf_op jit(solution)/shard_map/attn_back_a/pallas_call | solution.py:802
  157.5 22.2 %attn_back_b.1 = (bf16[4,2,4,64,128]{4,3,2,1,0:T(8,128)(2,1)}, bf16[4,2,4,64,128]{4,3,2,1,0:T(8,128)(2,1)}, f32[800,512]{1,0:T(8,128)}, f32[2,56,128]{2,1,0:T(8,128)}) custom-call(s32[25]{0:T(128)} %concatenate.15.table.refs_0_, bf16[512,800]{1,0:T(8,128)(2,1)} %get-tuple-element.117.refs_1_, bf16[800,512]{1,0:T(8,128)(2,1)} %get-tuple-element.118.refs_2_, ...), custom_call_target="tpu_custom_call" | custom-call | bytes 57000000 | tf_op jit(solution)/shard_map/attn_back_b/pallas_call | solution.py:802
  179.8 9.5 %tail.1 = (bf16[800,512]{1,0:T(8,128)(2,1)}, f32[4,4,24,128]{3,2,1,0:T(8,128)}) custom-call(s32[25]{0:T(128)} %concatenate.15.table.refs_0_, f32[800,512]{1,0:T(8,128)} %get-tuple-element.109.s0, f32[800,512]{1,0:T(8,128)} %get-tuple-element.116.gs1, f32[800,512]{1,0:T(8,128)} %get-tuple-element.126.gn1, bf16[800,512]{1,0:T(8,128)(2,1)} %bitcast.139, ...), custom_call_target="tpu_custom_call" | custom-call | bytes 27000000 | tf_op jit(solution)/shard_map/tail/pallas_call | solution.py:847
  206.0 3.3 %collective-permute-done.23 = bf16[4,4,64,128]{3,2,1,0:T(8,128)(2,1)S(1)} collective-permute-done((bf16[4,4,64,128]{3,2,1,0:T(8,128)(2,1)S(1)}, bf16[4,4,64,128]{3,2,1,0:T(8,128)(2,1)S(1)}, u32[]{:S(2)}, u32[]{:S(2)}) %collective-permute-start.23) | collective-permute-done | bytes 262176 | tf_op jit(solution)/shard_map/ppermute | solution.py:578
  210.7 4.3 %collective-permute-done.24 = bf16[4,4,64,128]{3,2,1,0:T(8,128)(2,1)S(1)} collective-permute-done((bf16[4,4,64,128]{3,2,1,0:T(8,128)(2,1)S(1)}, bf16[4,4,64,128]{3,2,1,0:T(8,128)(2,1)S(1)}, u32[]{:S(2)}, u32[]{:S(2)}) %collective-permute-start.24) | collective-permute-done | bytes 262176 | tf_op jit(solution)/shard_map/ppermute | solution.py:578
  217.5 3.4 %collective-permute-start.19 = (f32[24,128]{1,0:T(8,128)S(1)}, f32[24,128]{1,0:T(8,128)S(1)}, u32[]{:S(2)}, u32[]{:S(2)}) collective-permute-start(f32[24,128]{1,0:T(8,128)S(1)} %get-tuple-element.208), channel_id=1, source_target_pairs={{0,2},{1,3},{2,0},{3,1},{4,6},{5,7},{6,4},{7,5},{8,10},{9,11},{10,... | collective-permute-start | bytes 36872 | tf_op jit(solution)/shard_map/ppermute | solution.py:578
  221.1 5.1 %collective-permute-done.30 = bf16[4,2,64,512]{3,2,1,0:T(8,128)(2,1)S(1)} collective-permute-done((bf16[4,2,64,512]{3,2,1,0:T(8,128)(2,1)S(1)}, bf16[4,2,64,512]{3,2,1,0:T(8,128)(2,1)S(1)}, u32[]{:S(2)}, u32[]{:S(2)}) %collective-permute-start.30) | collective-permute-done | bytes 524320 | tf_op jit(solution)/shard_map/ppermute | solution.py:578
  228.7 7.4 %collective-permute-done.31 = bf16[4,2,64,512]{3,2,1,0:T(8,128)(2,1)S(1)} collective-permute-done((bf16[4,2,64,512]{3,2,1,0:T(8,128)(2,1)S(1)}, bf16[4,2,64,512]{3,2,1,0:T(8,128)(2,1)S(1)}, u32[]{:S(2)}, u32[]{:S(2)}) %collective-permute-start.31) | collective-permute-done | bytes 524320 | tf_op jit(solution)/shard_map/ppermute | solution.py:578
  238.7 2.8 %collective-permute-start.28 = (bf16[4,64,128]{2,1,0:T(8,128)(2,1)S(1)}, bf16[4,64,128]{2,1,0:T(8,128)(2,1)S(1)}, u32[]{:S(2)}, u32[]{:S(2)}) collective-permute-start(bf16[4,64,128]{2,1,0:T(8,128)(2,1)S(1)} %get-tuple-element.193), channel_id=1, source_target_pairs={{0,3},{1,0},{2,1},{3,2},{4,7},{5,4},{6,5},{7,6},{8,11},{9,8},{10,9... | collective-permute-start | bytes 196616 | tf_op jit(solution)/shard_map/ppermute | solution.py:578
  244.2 4.2 %collective-permute-start.35 = (bf16[2,64,512]{2,1,0:T(8,128)(2,1)S(1)}, bf16[2,64,512]{2,1,0:T(8,128)(2,1)S(1)}, u32[]{:S(2)}, u32[]{:S(2)}) collective-permute-start(bf16[2,64,512]{2,1,0:T(8,128)(2,1)S(1)} %get-tuple-element.188), channel_id=1, source_target_pairs={{0,3},{1,0},{2,1},{3,2},{4,7},{5,4},{6,5},{7,6},{8,11},{9,8},{10,9... | collective-permute-start | bytes 393224 | tf_op jit(solution)/shard_map/ppermute | solution.py:578
  250.1 2.7 collective-permute-start.20
  274.4 3.8 %adam.1 = (f32[8,128]{1,0:T(8,128)}, f32[3,64,128]{2,1,0:T(8,128)}, f32[3,64,128]{2,1,0:T(8,128)}, f32[3,64,128]{2,1,0:T(8,128)}, f32[3,64,128]{2,1,0:T(8,128)},...) custom-call(s32[25]{0:T(128)} %concatenate.15.table.refs_0_, ...), custom_call_target="tpu_custom_call" | custom-call | bytes 12000000 | tf_op jit(solution)/shard_map/adam/pallas_call | solution.py:925
  (138 shorter events, 78.7 us)
Async XLA Ops:
  1.7 9.6 %collective-permute-start.7 = (bf16[2,64,512]{2,1,0:T(8,128)(2,1)S(1)}, bf16[2,64,512]{2,1,0:T(8,128)(2,1)S(1)}, u32[]{:S(2)}, u32[]{:S(2)}) collective-permute-start(bf16[2,64,512]{2,1,0:T(8,128)(2,1)S(1)} %get-tuple-element.201), channel_id=1, source_target_pairs={{0,1},{1,2},{2,3},{3,0},{4,5},{5,6},{6,7},{7,4},{8,9},{9,10},{10,1... | collective-permute-start | bytes 393224 | tf_op jit(solution)/shard_map/ppermute | solution.py:578
  4.8 11.2 %collective-permute-start.8 = (bf16[2,64,512]{2,1,0:T(8,128)(2,1)S(1)}, bf16[2,64,512]{2,1,0:T(8,128)(2,1)S(1)}, u32[]{:S(2)}, u32[]{:S(2)}) collective-permute-start(bf16[2,64,512]{2,1,0:T(8,128)(2,1)S(1)} %get-tuple-element.201), channel_id=1, source_target_pairs={{0,2},{1,3},{2,0},{3,1},{4,6},{5,7},{6,4},{7,5},{8,10},{9,11},{10,... | collective-permute-start | bytes 393224 | tf_op jit(solution)/shard_map/ppermute | solution.py:578
  7.4 8.6 %collective-permute-start.9 = (bf16[2,64,512]{2,1,0:T(8,128)(2,1)S(1)}, bf16[2,64,512]{2,1,0:T(8,128)(2,1)S(1)}, u32[]{:S(2)}, u32[]{:S(2)}) collective-permute-start(bf16[2,64,512]{2,1,0:T(8,128)(2,1)S(1)} %get-tuple-element.201), channel_id=1, source_target_pairs={{0,3},{1,0},{2,1},{3,2},{4,7},{5,4},{6,5},{7,6},{8,11},{9,8},{10,9... | collective-permute-start | bytes 393224 | tf_op jit(solution)/shard_map/ppermute | solution.py:578
  16.1 15.8 %collective-permute-start.10 = (bf16[4,2,64,512]{3,2,1,0:T(8,128)(2,1)S(1)}, bf16[4,2,64,512]{3,2,1,0:T(8,128)(2,1)S(1)}, u32[]{:S(2)}, u32[]{:S(2)}) collective-permute-start(bf16[4,2,64,512]{3,2,1,0:T(8,128)(2,1)S(1)} %get-tuple-element.191), channel_id=1, source_target_pairs={{0,8},{4,12},{8,16},{12,20},{16,24},{20,28},{24,0},{28,4},{1,9},{5... | collective-permute-start | bytes 1572872 | tf_op jit(solution)/shard_map/ppermute | solution.py:578
  17.7 24.4 %collective-permute-start.11 = (bf16[4,2,64,512]{3,2,1,0:T(8,128)(2,1)S(1)}, bf16[4,2,64,512]{3,2,1,0:T(8,128)(2,1)S(1)}, u32[]{:S(2)}, u32[]{:S(2)}) collective-permute-start(bf16[4,2,64,512]{3,2,1,0:T(8,128)(2,1)S(1)} %get-tuple-element.191), channel_id=1, source_target_pairs={{0,16},{4,20},{8,24},{12,28},{16,0},{20,4},{24,8},{28,12},{1,17},{... | collective-permute-start | bytes 1572872 | tf_op jit(solution)/shard_map/ppermute | solution.py:578
  19.2 23.0 %collective-permute-start.12 = (bf16[4,2,64,512]{3,2,1,0:T(8,128)(2,1)S(1)}, bf16[4,2,64,512]{3,2,1,0:T(8,128)(2,1)S(1)}, u32[]{:S(2)}, u32[]{:S(2)}) collective-permute-start(bf16[4,2,64,512]{3,2,1,0:T(8,128)(2,1)S(1)} %get-tuple-element.191), channel_id=1, source_target_pairs={{0,24},{4,28},{8,0},{12,4},{16,8},{20,12},{24,16},{28,20},{1,25},{... | collective-permute-start | bytes 1572872 | tf_op jit(solution)/shard_map/ppermute | solution.py:578
  43.8 57.3 %collective-permute-start.13 = (bf16[4,4,2,64,512]{4,3,2,1,0:T(8,128)(2,1)}, bf16[4,4,2,64,512]{4,3,2,1,0:T(8,128)(2,1)}, u32[]{:S(2)}, u32[]{:S(2)}) collective-permute-start(bf16[4,4,2,64,512]{4,3,2,1,0:T(8,128)(2,1)} %pad_maximum_fusion.own), channel_id=1, source_target_pairs={{0,4},{4,0},{8,12},{12,8},{16,20},{20,16},{24,28},{28,24},{1,5},{5... | collective-permute-start | bytes 6291464 | tf_op jit(solution)/shard_map/ppermute | solution.py:578
  55.5 9.2 %collective-permute-start.3 = (bf16[4,4,64,128]{3,2,1,0:T(8,128)(2,1)S(1)}, bf16[4,4,64,128]{3,2,1,0:T(8,128)(2,1)S(1)}, u32[]{:S(2)}, u32[]{:S(2)}) collective-permute-start(bf16[4,4,64,128]{3,2,1,0:T(8,128)(2,1)S(1)} %get-tuple-element.196), channel_id=1, source_target_pairs={{0,8},{4,12},{8,16},{12,20},{16,24},{20,28},{24,0},{28,4},{1,9},{5... | collective-permute-start | bytes 786440 | tf_op jit(solution)/shard_map/ppermute | solution.py:578
  57.2 10.1 %collective-permute-start.4 = (bf16[4,4,64,128]{3,2,1,0:T(8,128)(2,1)S(1)}, bf16[4,4,64,128]{3,2,1,0:T(8,128)(2,1)S(1)}, u32[]{:S(2)}, u32[]{:S(2)}) collective-permute-start(bf16[4,4,64,128]{3,2,1,0:T(8,128)(2,1)S(1)} %get-tuple-element.196), channel_id=1, source_target_pairs={{0,16},{4,20},{8,24},{12,28},{16,0},{20,4},{24,8},{28,12},{1,17},{... | collective-permute-start | bytes 786440 | tf_op jit(solution)/shard_map/ppermute | solution.py:578
  57.7 9.7 %collective-permute-start.5 = (bf16[4,4,64,128]{3,2,1,0:T(8,128)(2,1)S(1)}, bf16[4,4,64,128]{3,2,1,0:T(8,128)(2,1)S(1)}, u32[]{:S(2)}, u32[]{:S(2)}) collective-permute-start(bf16[4,4,64,128]{3,2,1,0:T(8,128)(2,1)S(1)} %get-tuple-element.196), channel_id=1, source_target_pairs={{0,24},{4,28},{8,0},{12,4},{16,8},{20,12},{24,16},{28,20},{1,25},{... | collective-permute-start | bytes 786440 | tf_op jit(solution)/shard_map/ppermute | solution.py:578
  67.6 9.2 %collective-permute-start.6 = (bf16[4,4,4,64,128]{4,3,2,1,0:T(8,128)(2,1)S(1)}, bf16[4,4,4,64,128]{4,3,2,1,0:T(8,128)(2,1)S(1)}, u32[]{:S(2)}, u32[]{:S(2)}) collective-permute-start(bf16[4,4,4,64,128]{4,3,2,1,0:T(8,128)(2,1)S(1)} %pad_maximum_fusion.1.own.refs_4_), channel_id=1, source_target_pairs={{0,4},{4,0},{8,12},{12,8},{16,20},{20,16},{24,28},{28,24},{1,5},{5... | collective-permute-start | bytes 3145736 | tf_op jit(solution)/shard_map/ppermute | solution.py:578
  127.9 75.4 %collective-permute-start.29 = (bf16[4,4,2,64,512]{4,3,2,1,0:T(8,128)(2,1)}, bf16[4,4,2,64,512]{4,3,2,1,0:T(8,128)(2,1)S(1)}, u32[]{:S(2)}, u32[]{:S(2)}) collective-permute-start(bf16[4,4,2,64,512]{4,3,2,1,0:T(8,128)(2,1)} %get-tuple-element.139), channel_id=1, source_target_pairs={{0,4},{4,0},{8,12},{12,8},{16,20},{20,16},{24,28},{28,24},{1,5},{5... | collective-permute-start | bytes 6291464 | tf_op jit(solution)/shard_map/ppermute | solution.py:578
  189.4 9.1 %collective-permute-start.22 = (bf16[4,2,4,64,128]{4,3,2,1,0:T(8,128)(2,1)S(1)}, bf16[4,2,4,64,128]{4,3,2,1,0:T(8,128)(2,1)S(1)}, u32[]{:S(2)}, u32[]{:S(2)}) collective-permute-start(bf16[4,2,4,64,128]{4,3,2,1,0:T(8,128)(2,1)S(1)} %copy-done.10), channel_id=1, source_target_pairs={{0,4},{4,0},{8,12},{12,8},{16,20},{20,16},{24,28},{28,24},{1,5},{5... | collective-permute-start | bytes 1572872 | tf_op jit(solution)/shard_map/ppermute | solution.py:578
  199.1 10.2 %collective-permute-start.23 = (bf16[4,4,64,128]{3,2,1,0:T(8,128)(2,1)S(1)}, bf16[4,4,64,128]{3,2,1,0:T(8,128)(2,1)S(1)}, u32[]{:S(2)}, u32[]{:S(2)}) collective-permute-start(bf16[4,4,64,128]{3,2,1,0:T(8,128)(2,1)S(1)} %get-tuple-element.184), channel_id=1, source_target_pairs={{0,8},{4,12},{8,16},{12,20},{16,24},{20,28},{24,0},{28,4},{1,9},{5... | collective-permute-start | bytes 786440 | tf_op jit(solution)/shard_map/ppermute | solution.py:578
  201.0 14.0 %collective-permute-start.24 = (bf16[4,4,64,128]{3,2,1,0:T(8,128)(2,1)S(1)}, bf16[4,4,64,128]{3,2,1,0:T(8,128)(2,1)S(1)}, u32[]{:S(2)}, u32[]{:S(2)}) collective-permute-start(bf16[4,4,64,128]{3,2,1,0:T(8,128)(2,1)S(1)} %get-tuple-element.186), channel_id=1, source_target_pairs={{0,16},{4,20},{8,24},{12,28},{16,0},{20,4},{24,8},{28,12},{1,17},{... | collective-permute-start | bytes 786440 | tf_op jit(solution)/shard_map/ppermute | solution.py:578
  202.0 15.5 %collective-permute-start.25 = (bf16[4,4,64,128]{3,2,1,0:T(8,128)(2,1)S(1)}, bf16[4,4,64,128]{3,2,1,0:T(8,128)(2,1)S(1)}, u32[]{:S(2)}, u32[]{:S(2)}) collective-permute-start(bf16[4,4,64,128]{3,2,1,0:T(8,128)(2,1)S(1)} %get-tuple-element.185), channel_id=1, source_target_pairs={{0,24},{4,28},{8,0},{12,4},{16,8},{20,12},{24,16},{28,20},{1,25},{... | collective-permute-start | bytes 786440 | tf_op jit(solution)/shard_map/ppermute | solution.py:578
  204.2 22.1 %collective-permute-start.30 = (bf16[4,2,64,512]{3,2,1,0:T(8,128)(2,1)S(1)}, bf16[4,2,64,512]{3,2,1,0:T(8,128)(2,1)S(1)}, u32[]{:S(2)}, u32[]{:S(2)}) collective-permute-start(bf16[4,2,64,512]{3,2,1,0:T(8,128)(2,1)S(1)} %get-tuple-element.181), channel_id=1, source_target_pairs={{0,8},{4,12},{8,16},{12,20},{16,24},{20,28},{24,0},{28,4},{1,9},{5... | collective-permute-start | bytes 1572872 | tf_op jit(solution)/shard_map/ppermute | solution.py:578
  205.0 31.1 %collective-permute-start.31 = (bf16[4,2,64,512]{3,2,1,0:T(8,128)(2,1)S(1)}, bf16[4,2,64,512]{3,2,1,0:T(8,128)(2,1)S(1)}, u32[]{:S(2)}, u32[]{:S(2)}) collective-permute-start(bf16[4,2,64,512]{3,2,1,0:T(8,128)(2,1)S(1)} %get-tuple-element.183), channel_id=1, source_target_pairs={{0,16},{4,20},{8,24},{12,28},{16,0},{20,4},{24,8},{28,12},{1,17},{... | collective-permute-start | bytes 1572872 | tf_op jit(solution)/shard_map/ppermute | solution.py:578
  209.3 29.4 %collective-permute-start.32 = (bf16[4,2,64,512]{3,2,1,0:T(8,128)(2,1)S(1)}, bf16[4,2,64,512]{3,2,1,0:T(8,128)(2,1)S(1)}, u32[]{:S(2)}, u32[]{:S(2)}) collective-permute-start(bf16[4,2,64,512]{3,2,1,0:T(8,128)(2,1)S(1)} %get-tuple-element.182), channel_id=1, source_target_pairs={{0,24},{4,28},{8,0},{12,4},{16,8},{20,12},{24,16},{28,20},{1,25},{... | collective-permute-start | bytes 1572872 | tf_op jit(solution)/shard_map/ppermute | solution.py:578
  215.0 43.2 %collective-permute-start.18 = (f32[24,128]{1,0:T(8,128)S(1)}, f32[24,128]{1,0:T(8,128)S(1)}, u32[]{:S(2)}, u32[]{:S(2)}) collective-permute-start(f32[24,128]{1,0:T(8,128)S(1)} %get-tuple-element.206), channel_id=1, source_target_pairs={{0,1},{1,2},{2,3},{3,0},{4,5},{5,6},{6,7},{7,4},{8,9},{9,10},{10,1... | collective-permute-start | bytes 36872 | tf_op jit(solution)/shard_map/ppermute | solution.py:578
  217.5 40.7 %collective-permute-start.19 = (f32[24,128]{1,0:T(8,128)S(1)}, f32[24,128]{1,0:T(8,128)S(1)}, u32[]{:S(2)}, u32[]{:S(2)}) collective-permute-start(f32[24,128]{1,0:T(8,128)S(1)} %get-tuple-element.208), channel_id=1, source_target_pairs={{0,2},{1,3},{2,0},{3,1},{4,6},{5,7},{6,4},{7,5},{8,10},{9,11},{10,... | collective-permute-start | bytes 36872 | tf_op jit(solution)/shard_map/ppermute | solution.py:578
  226.2 15.6 %collective-permute-start.26 = (bf16[4,64,128]{2,1,0:T(8,128)(2,1)S(1)}, bf16[4,64,128]{2,1,0:T(8,128)(2,1)S(1)}, u32[]{:S(2)}, u32[]{:S(2)}) collective-permute-start(bf16[4,64,128]{2,1,0:T(8,128)(2,1)S(1)} %get-tuple-element.192), channel_id=1, source_target_pairs={{0,1},{1,2},{2,3},{3,0},{4,5},{5,6},{6,7},{7,4},{8,9},{9,10},{10,1... | collective-permute-start | bytes 196616 | tf_op jit(solution)/shard_map/ppermute | solution.py:578
  242.4 12.4 %collective-permute-start.34 = (bf16[2,64,512]{2,1,0:T(8,128)(2,1)S(1)}, bf16[2,64,512]{2,1,0:T(8,128)(2,1)S(1)}, u32[]{:S(2)}, u32[]{:S(2)}) collective-permute-start(bf16[2,64,512]{2,1,0:T(8,128)(2,1)S(1)} %get-tuple-element.189), channel_id=1, source_target_pairs={{0,2},{1,3},{2,0},{3,1},{4,6},{5,7},{6,4},{7,5},{8,10},{9,11},{10,... | collective-permute-start | bytes 393224 | tf_op jit(solution)/shard_map/ppermute | solution.py:578
  244.2 11.2 %collective-permute-start.35 = (bf16[2,64,512]{2,1,0:T(8,128)(2,1)S(1)}, bf16[2,64,512]{2,1,0:T(8,128)(2,1)S(1)}, u32[]{:S(2)}, u32[]{:S(2)}) collective-permute-start(bf16[2,64,512]{2,1,0:T(8,128)(2,1)S(1)} %get-tuple-element.188), channel_id=1, source_target_pairs={{0,3},{1,0},{2,1},{3,2},{4,7},{5,4},{6,5},{7,6},{8,11},{9,8},{10,9... | collective-permute-start | bytes 393224 | tf_op jit(solution)/shard_map/ppermute | solution.py:578
  (30 other events, 216.1 us)

commit v3 on v2

--- a/solution.py
+++ b/solution.py
@@ -15,6 +15,7 @@
 SEQ = 50
 LANE = 128
 PAD_TOKENS = 64
+COLS = 256
 
 NORM_EPS = 1e-06
 BETA_FIRST = 0.9
@@ -38,6 +39,8 @@
 
 
 def rows_at(start, size):
+    if isinstance(start, int):
+        return pl.ds(start, size)
     return pl.ds(pl.multiple_of(start, 16), size)
 
 
@@ -57,7 +60,10 @@
 def conv_row(src, taps, reach, y, cols, imgs, flip):
     side = 2 * reach + 1
     acc = [None] * GRID
-    for a in range(side):
+    inside = range(side)
+    if isinstance(y, int):
+        inside = range(max(0, reach - y), min(side, GRID + reach - y))
+    for a in inside:
         start = (y + a) * (GRID * imgs)
         vals = [src[rows_at(start + x * imgs, imgs), cols] for x in range(GRID)]
         for b in range(side):
@@ -92,7 +98,7 @@
         out[:, r:stop] = src[r:stop].T
 
 
-def pre_kernel(x_ref, og_ref, rp_ref, s0_ref, n1_ref, n1t_ref, ogt_ref, ogsum_ref, xs, *, imgs):
+def pre_kernel(x_ref, rp_ref, s0_ref, n1_ref, n1t_ref, xs, *, imgs):
     rows, width = x_ref.shape
     row = GRID * imgs
     base = row - imgs
@@ -117,16 +123,21 @@
     lax.fori_loop(0, GRID, conv_body, 0)
     step = 5 * imgs
 
-    def norm_body(r, total):
+    def norm_body(r, carry):
         at = rows_at(r * step, step)
         unit, _ = norm_parts(s0_ref[at, :])
         n1_ref[at, :] = (unit * rp_ref[10:11] + rp_ref[11:12]).astype(BF16)
-        wide = og_ref[at, :].astype(F32).reshape(step // 8, 8, width)
-        return total + jnp.sum(wide, axis=0)
-
-    total = lax.fori_loop(0, rows // step, norm_body, jnp.zeros((8, width), F32))
-    ogsum_ref[...] = jnp.broadcast_to(jnp.sum(total, axis=0, keepdims=True), (8, width))
+        return carry
+
+    lax.fori_loop(0, rows // step, norm_body, 0)
     transposed(n1t_ref, n1_ref, rows)
+
+
+def cot_kernel(og_ref, ogt_ref, ogsum_ref):
+    rows, width = og_ref.shape
+    wide = og_ref[...].astype(F32).reshape(rows // 8, 8, width)
+    total = jnp.sum(jnp.sum(wide, axis=0), axis=0, keepdims=True)
+    ogsum_ref[...] = jnp.broadcast_to(total, (8, width))
     transposed(ogt_ref, og_ref, rows)
 
 
@@ -159,13 +170,18 @@
 
 def scatter_grads(table, slots, left, right, keep, send, kinds, width):
     size = keep.shape[3]
-    for low, to in ((table[slots.low], keep), (1 - table[slots.low], send)):
-        lhs = [left[rows_at((2 * u + low) * size, size), :] for u in range(slots.up)]
-        value = dot(jnp.concatenate(lhs, axis=0), right).astype(BF16)
-        for u in range(slots.up):
-            at = table[slots.up_out + u]
-            for i, k in enumerate(kinds):
-                to[at, 0, k] = value[u * size : (u + 1) * size, i * width : (i + 1) * width]
+    lows = (table[slots.low], 1 - table[slots.low])
+    starts = [(2 * u + low) * size for low in lows for u in range(slots.up)]
+    lhs = jnp.concatenate([left[rows_at(start, size), :] for start in starts], axis=0)
+    step = max(1, COLS // width)
+    for n in range(0, len(kinds), step):
+        some = kinds[n : n + step]
+        value = dot(lhs, right[:, n * width : (n + len(some)) * width]).astype(BF16)
+        for b in range(2 * slots.up):
+            to = (keep, send)[b // slots.up]
+            at = table[slots.up_out + b % slots.up]
+            for i, k in enumerate(some):
+                to[at, 0, k] = value[b * size : (b + 1) * size, i * width : (i + 1) * width]
 
 
 def attn_kernel(
@@ -188,17 +204,15 @@
         s1_o[...] = s0[...] + rp[14:15]
 
     gather_weights(table, slots, own, recv, wbuf, 4, LANE)
-    chunk = 10 * imgs
-    for r in range(0, rows, chunk):
-        qkv = dot(n1[r : r + chunk], wbuf[:, 0 : 3 * LANE])
-        q = qkv[:, 0:LANE] + hp[50:51]
-        qs[r : r + chunk] = q
-        q_o[0, r : r + chunk] = q
-        ks[r : r + chunk] = qkv[:, LANE : 2 * LANE]
-        v = qkv[:, 2 * LANE :] + hp[51:52]
-        vs[r : r + chunk] = v
-        v_o[0, r : r + chunk] = v
-        vp[first + r : first + r + chunk] = v
+    qk = dot(n1[...], wbuf[:, 0 : 2 * LANE])
+    q = qk[:, 0:LANE] + hp[50:51]
+    qs[0:rows] = q
+    q_o[0] = q
+    ks[0:rows] = qk[:, LANE:]
+    v = dot(n1[...], wbuf[:, 2 * LANE : 3 * LANE]) + hp[51:52]
+    vs[0:rows] = v
+    v_o[0] = v
+    vp[first : first + rows] = v
     vp[first : first + imgs] = jnp.zeros((imgs, LANE), F32)
     keys = ks[0:rows].reshape(SEQ, imgs, LANE)
     expo = jnp.exp(keys - jnp.max(keys, axis=0, keepdims=True))
@@ -228,8 +242,10 @@
             at_o[0, at] = (fs[at] + qs[at] * value).astype(BF16)
         return carry
 
-    lax.fori_loop(0, GRID, conv_body, 0)
-    s1_o[...] += dot(at_o[0], wbuf[:, 3 * LANE :], NT)
+    for y in range(GRID):
+        conv_body(y, 0)
+    for c in range(0, s1_o.shape[1], COLS):
+        s1_o[:, c : c + COLS] += dot(at_o[0], wbuf[c : c + COLS, 3 * LANE :], NT)
 
     @pl.when(j == pl.num_programs(0) - 1)
     def _():
@@ -254,8 +270,9 @@
     j = pl.program_id(0)
     rows = SEQ * imgs
     gather_weights(table, slots, own, recv, wbuf, 2, hid)
-    hs[...] = dot(n2[...], wbuf[:, 0:hid]) + ub[0]
-    ds[...] = dot(og[...], wbuf[:, hid:])
+    for c in range(0, hid, COLS):
+        hs[:, c : c + COLS] = dot(n2[...], wbuf[:, c : c + COLS]) + ub[0, :, c : c + COLS]
+        ds[:, c : c + COLS] = dot(og[...], wbuf[:, hid + c : hid + c + COLS])
     step = 2 * imgs
 
     def gelu_body(r, total):
@@ -277,13 +294,12 @@
         oacc[...] = s1[...] + rp[15:16]
         gn2_o[...] = jnp.zeros(gn2_o.shape, F32)
 
-    chunk = 10 * imgs
-    for r in range(0, rows, chunk):
-        at = slice(r, r + chunk)
-        oacc[at] += dot(hb[at], wbuf[:, hid:], NT)
-        gn2_o[at] += dot(gb[at], wbuf[:, 0:hid], NT)
-    scatter_grads(table, slots, n2t, gb[...], keep_o, send_o, (0,), hid)
-    scatter_grads(table, slots, ogt, hb[...], keep_o, send_o, (1,), hid)
+    for c in range(0, oacc.shape[1], COLS):
+        cols = slice(c, c + COLS)
+        oacc[:, cols] += dot(hb[...], wbuf[cols, hid:], NT)
+        gn2_o[:, cols] += dot(gb[...], wbuf[cols, 0:hid], NT)
+    scatter_grads(table, slots, n2t, gb, keep_o, send_o, (0,), hid)
+    scatter_grads(table, slots, ogt, hb, keep_o, send_o, (1,), hid)
 
     @pl.when(j == pl.num_programs(0) - 1)
     def _():
@@ -340,18 +356,15 @@
         gn1_o[...] = gn1_i[...] if begin else jnp.zeros(gn1_o.shape, F32)
 
     gather_weights(table, slots, own, recv, wbuf, 4, LANE)
-    chunk = 10 * imgs
-    for r in range(0, rows, chunk):
-        at = slice(r, r + chunk)
-        grad = dot(gal[at], wbuf[:, 3 * LANE :])
-        gs[at] = grad
-        q = q_i[0, at]
-        v = v_i[0, at]
-        qs[at] = q
-        ks[at] = k_i[0, at]
-        vs[at] = v
-        vp[first + r : first + r + chunk] = v
-        gp[first + r : first + r + chunk] = grad * q
+    grad = dot(gal[...], wbuf[:, 3 * LANE :])
+    gs[0:rows] = grad
+    q = q_i[0]
+    v = v_i[0]
+    qs[0:rows] = q
+    ks[0:rows] = k_i[0]
+    vs[0:rows] = v
+    vp[first : first + rows] = v
+    gp[first : first + rows] = grad * q
     vp[first : first + imgs] = jnp.zeros((imgs, LANE), F32)
     gp[first : first + imgs] = jnp.zeros((imgs, LANE), F32)
     scale = head_block_mask(HD**-0.5)
@@ -390,7 +403,9 @@
             carry = carry + value.astype(F32)
         return carry
 
-    value_sum = lax.fori_loop(0, GRID, conv_body, low.astype(F32))
+    value_sum = low.astype(F32)
+    for y in range(GRID):
+        value_sum = conv_body(y, value_sum)
     side = GRID
     zero = jnp.zeros((imgs, LANE), F32)
     for a in range(side):
@@ -410,10 +425,11 @@
     hg_o[0, 50:51] = query_sum
     hg_o[0, 51:52] = jnp.sum(value_sum, axis=0, keepdims=True)
     hg_o[0, 52:56] = jnp.zeros((4, LANE), F32)
-    for r in range(0, rows, chunk):
-        gn1_o[r : r + chunk] += dot(gqkv[r : r + chunk], wbuf[:, 0 : 3 * LANE], NT)
-    scatter_grads(table, slots, n1t, gqkv[...], keep_o, send_o, (0, 1, 2), LANE)
-    scatter_grads(table, slots, galt, at_i[0], keep_o, send_o, (3,), LANE)
+    for c in range(0, gn1_o.shape[1], COLS):
+        cols = slice(c, c + COLS)
+        gn1_o[:, cols] += dot(gqkv[...], wbuf[cols, 0 : 3 * LANE], NT)
+    scatter_grads(table, slots, n1t, gqkv, keep_o, send_o, (0, 1, 2), LANE)
+    scatter_grads(table, slots, galt, at_i.at[0], keep_o, send_o, (3,), LANE)
 
 
 def tail_kernel(
@@ -482,7 +498,7 @@
     ig_o[...] = res[...].astype(BF16)
 
     sm[:, 72:] = jnp.zeros((sm.shape[0], sm.shape[1] - 72, LANE), F32)
-    half = slots.nh // 2
+    half = hg_one.shape[0]
     for k in range(slots.nh):
         at = table[slots.head_col + k]
         sm[at, 0:56] = hg_one[k] if k < half else hg_two[k - half]
@@ -542,7 +558,7 @@
             total = total + share[span : span + 1, 0:1]
     norm = jnp.sqrt(total)
     clip = jnp.minimum(1.0, CLIP_NORM / (norm + 1e-06))
-    norm_o[...] = jnp.broadcast_to(norm, norm_o.shape)
+    norm_o[...] = norm
     raws = (one[0:3], one[3], two[0], two[1])
     for p, raw in enumerate(raws):
         state = [ref[...] for ref in ins[4 * p : 4 * p + 4]]
@@ -673,9 +689,9 @@
 
     shape = jax.ShapeDtypeStruct
 
-    def params(*semantics):
+    def params(mebibytes, *semantics):
         return pltpu.CompilerParams(
-            dimension_semantics=semantics or None, vmem_limit_bytes=60 * 1024 * 1024
+            dimension_semantics=semantics or None, vmem_limit_bytes=mebibytes * 1024 * 1024
         )
 
     def cost(us):
@@ -693,14 +709,21 @@
     low = shape((rows, width), BF16)
     low_turned = shape((width, rows), BF16)
 
-    stream_zero, normed_one, normed_one_t, cot_t, cot_sum = pl.pallas_call(
+    stream_zero, normed_one, normed_one_t = pl.pallas_call(
         partial(pre_kernel, imgs=imgs),
-        out_shape=(wide, low, low_turned, low_turned, shape((8, width), F32)),
+        out_shape=(wide, low, low_turned),
         scratch_shapes=[pltpu.VMEM((9 * GRID * imgs, width), F32)],
-        compiler_params=params(),
+        compiler_params=params(10),
         cost_estimate=cost(9),
         name="pre",
-    )(x, cot, rep_params)
+    )(x, rep_params)
+    cot_t, cot_sum = pl.pallas_call(
+        cot_kernel,
+        out_shape=(low_turned, shape((8, width), F32)),
+        compiler_params=params(6),
+        cost_estimate=cost(2),
+        name="cot",
+    )(cot)
 
     mask = tap_mask(kernel_radius)
     head_rows = jnp.concatenate([head_params[:TAPS] * mask, head_params[TAPS : TAPS + 7]], axis=0)
@@ -731,7 +754,7 @@
                 out_specs=[tile_spec] * 5 + [full, full, turned],
                 scratch_shapes=[w_one] + [padded] * 4 + [framed],
             ),
-            compiler_params=params("arbitrary"),
+            compiler_params=params(19, "arbitrary"),
             cost_estimate=cost(21),
             name="attn",
         )(table, normed_one, stream_zero, gathered_one, other_one, head_rows, rep_params)
@@ -764,7 +787,7 @@
                 pltpu.VMEM((rows, width), F32),
             ],
         ),
-        compiler_params=params("arbitrary"),
+        compiler_params=params(26, "arbitrary"),
         cost_estimate=cost(26),
         name="mlp",
     )(
@@ -783,16 +806,17 @@
     grad_one, grad_low, grad_low_t, rep_mid = pl.pallas_call(
         partial(mid_kernel, imgs=imgs),
         out_shape=(wide, low, low_turned, shape((8, width), F32)),
-        compiler_params=params(),
+        compiler_params=params(9),
         cost_estimate=cost(4),
         name="mid",
     )(grad_norm_two, stream_one, cot, rep_params)
 
-    half = nh // 2
-    one_grads = shape((up, half, 4, size, LANE), BF16)
+    cut = nh - 1
     one_spec = pl.BlockSpec((up, 1, 4, size, LANE), lambda j, s: (0, j, 0, 0, 0))
 
-    def attn_back(begin, so_far):
+    def attn_back(begin, count, so_far):
+        one_grads = shape((up, count, 4, size, LANE), BF16)
+
         def at_head(j, s):
             return (0, s[slots.head_in + begin + j], 0, 0, 0)
 
@@ -801,10 +825,10 @@
         taps = pl.BlockSpec((56, LANE), lambda j, s: (0, s[slots.head_col + begin + j]))
         return pl.pallas_call(
             partial(attn_back_kernel, imgs=imgs, slots=slots, begin=begin),
-            out_shape=(one_grads, one_grads, wide, shape((half, 56, LANE), F32)),
+            out_shape=(one_grads, one_grads, wide, shape((count, 56, LANE), F32)),
             grid_spec=pltpu.PrefetchScalarGridSpec(
                 num_scalar_prefetch=1,
-                grid=(half,),
+                grid=(count,),
                 in_specs=[turned, full, turned, weights, weights, taps]
                 + [tile] * 5
                 + [full] * len(so_far),
@@ -819,8 +843,8 @@
                 + [framed] * 2
                 + [pltpu.VMEM((rows, 3 * LANE), BF16)],
             ),
-            compiler_params=params("arbitrary"),
-            cost_estimate=cost(19),
+            compiler_params=params(21, "arbitrary"),
+            cost_estimate=cost(7 * count),
             name="attn_back_b" if begin else "attn_back_a",
         )(
             table,
@@ -838,8 +862,8 @@
             *so_far,
         )
 
-    keep_a, send_a, grad_half, head_a = attn_back(0, ())
-    keep_b, send_b, grad_norm_one, head_b = attn_back(half, (grad_half,))
+    keep_a, send_a, grad_part, head_a = attn_back(0, cut, ())
+    keep_b, send_b, grad_norm_one, head_b = attn_back(cut, nh - cut, (grad_part,))
 
     small_rows = 8 * pl.cdiv(72, 8 * up)
     smem = pl.BlockSpec(memory_space=pltpu.SMEM)
@@ -855,7 +879,7 @@
             pltpu.VMEM((tiles, up * small_rows, LANE), F32),
             pltpu.VMEM((16, width), F32),
         ],
-        compiler_params=params(),
+        compiler_params=params(16),
         cost_estimate=cost(9),
         name="tail",
     )(
@@ -880,13 +904,17 @@
         one_a = ring.swap_sum(keep_a, send_a).astype(BF16)
         one_b = ring.swap_sum(keep_b, send_b).astype(BF16)
         one = ring.scatter(jnp.concatenate([one_a, one_b], axis=1), "up").astype(BF16)
-        one = ring.scatter(one, "head")
-        share = ring.swap_sum(small, small)
-        share = ring.scatter(share, "up")
-        share = ring.scatter(share, "head")
+        share = ring.scatter(small, "up").astype(BF16)
+        pad = -small_rows % 16
+        rider = jnp.concatenate(
+            [one.reshape(nh, 4 * size, LANE), jnp.pad(share, ((0, 0), (0, pad), (0, 0)))], axis=1
+        )
+        rider = ring.scatter(rider, "head")
+        one = rider[: 4 * size].reshape(4, size, LANE)
+        share = rider[4 * size : 4 * size + small_rows]
         mine = jnp.zeros((8, LANE), F32) + (square_sum(one) + square_sum(two))
-        mine = ring.swap_sum(mine, mine)
         shares = jnp.concatenate([share, mine], axis=0)
+        shares = ring.swap_sum(shares, shares)
         shares = ring.gather(ring.gather(shares, "head"), "up")
     else:
 
@@ -924,10 +952,10 @@
         results += [shape(like, BF16 if k == 4 else F32) for k in range(6)]
     norm, *outs = pl.pallas_call(
         partial(adam_kernel, slots=slots, span=small_rows),
-        out_shape=(shape((8, LANE), F32), *results),
+        out_shape=(shape((1, 1), F32), *results),
         in_specs=[smem] + [vmem] * 27,
         scratch_shapes=[pltpu.VMEM((tiles, up * small_rows, LANE), F32)],
-        compiler_params=params(),
+        compiler_params=params(10),
         cost_estimate=cost(4),
         name="adam",
     )(table, shares, one, two, *states)
@@ -936,7 +964,7 @@
     def by_image(v):
         return v.reshape(SEQ, imgs, width).transpose(1, 0, 2)
 
-    return (by_image(output), by_image(input_grad), norm[0, 0], *outs)
+    return (by_image(output), by_image(input_grad), norm.reshape(()), *outs)
 
 
 def solution(mesh):

time: 280 us -> 243 us (0.87)
  Pallas kernels: 121 us -> 89.1 us
  starting transfers between devices: 64.3 us -> 51.6 us
  waiting for transfers between devices: 77.5 us -> 84 us
  local copies, waits for them, and re-layouts: 3.84 us -> 8.32 us
  other arithmetic: 10.6 us -> 6.29 us
    ppermute x43 -> x39, starting transfers between devices: 64.3 us -> 51.6 us  [turn(): return lax.ppermute(value, axis, pairs)]
    pallas_call x2, Pallas kernels: 43.6 us -> 33.6 us  [attn_back(): pl.pallas_call(partial(attn_back_kernel, imgs=imgs, slots=slots, begin=be...]
    unnamed x22 -> x74, local copies, waits for them, and re-layouts: 1.03 us -> 7.88 us
    ppermute x43 -> x39, waiting for transfers between devices: 77.5 us -> 84 us  [turn(): return lax.ppermute(value, axis, pairs)]
    pallas_call x1, Pallas kernels: 26.8 us -> 21.1 us  [per_device(): pl.pallas_call(partial(mlp_kernel, imgs=imgs, slots=slots, hid=hid), out_...]
    pallas_call x1, Pallas kernels: 23.3 us -> 17.6 us  [per_device(): pl.pallas_call(partial(attn_kernel, imgs=imgs, slots=slots), out_shape=(p...]
    pallas_call x1, Pallas kernels: 6.98 us -> 3.29 us  [per_device(): pl.pallas_call(partial(mid_kernel, imgs=imgs), out_shape=(wide, low, low_...]
    pallas_call x1, Pallas kernels: 6.75 us -> 3.42 us  [per_device(): pl.pallas_call(partial(pre_kernel, imgs=imgs), out_shape=(wide, low, low_...]
  transfers between devices with their start and end apart: 43 -> 39, of which waited for: 30 -> 25; matrix products, arithmetic and copies ran while one was open for 3% -> 1% of each run, Pallas kernels for 32% -> 27%
where the time goes in v3:
time: 243 us; the launch traced here: 242 us
  Pallas kernels  89.1 us (37%)
  waiting for transfers between devices  84 us (35%)
  starting transfers between devices  51.6 us (21%)
  local copies, waits for them, and re-layouts  8.32 us (3%)
  other arithmetic  6.29 us (3%)
  between operations  2.92 us (1%)
    ppermute x39, waiting for transfers between devices, turn(): return lax.ppermute(value, axis, pairs)  84 us
    ppermute x39, starting transfers between devices, turn(): return lax.ppermute(value, axis, pairs)  51.6 us
    pallas_call x2, Pallas kernels, attn_back(): pl.pallas_call(partial(attn_back_kernel, imgs=imgs, slots=slots, begin=be...  33.6 us
    pallas_call x1, Pallas kernels, per_device(): pl.pallas_call(partial(mlp_kernel, imgs=imgs, slots=slots, hid=hid), out_...  21.1 us
    pallas_call x1, Pallas kernels, per_device(): pl.pallas_call(partial(attn_kernel, imgs=imgs, slots=slots), out_shape=(p...  17.6 us
    unnamed x74, local copies, waits for them, and re-layouts  7.88 us
    pallas_call x1, Pallas kernels, per_device(): pl.pallas_call(partial(tail_kernel, imgs=imgs, slots=slots), out_shape=(l...  7 us
  transfers between devices with their start and end apart: 39, of which 25 were waited for; matrix products, arithmetic and copies ran while one was open for 1% of the time, Pallas kernels for 27%

profile of v3, /device:TPU:0, one launch (start us, length us, event | category | flops | bytes accessed | tf_op | source)
XLA Modules:
  0.0 242.3 jit_solution(16222686309634508569)
XLA Ops:
  1.7 3.1 %collective-permute-start.7 = (bf16[2,64,512]{2,1,0:T(8,128)(2,1)S(1)}, bf16[2,64,512]{2,1,0:T(8,128)(2,1)S(1)}, u32[]{:S(2)}, u32[]{:S(2)}) collective-permute-start(bf16[2,64,512]{2,1,0:T(8,128)(2,1)S(1)} %get-tuple-element.201), channel_id=1, source_target_pairs={{0,1},{1,2},{2,3},{3,0},{4,5},{5,6},{6,7},{7,4},{8,9},{9,10},{10,1... | collective-permute-start | bytes 393224 | tf_op jit(solution)/shard_map/ppermute | solution.py:594
  11.3 4.8 %collective-permute-done.8 = bf16[2,64,512]{2,1,0:T(8,128)(2,1)S(1)} collective-permute-done((bf16[2,64,512]{2,1,0:T(8,128)(2,1)S(1)}, bf16[2,64,512]{2,1,0:T(8,128)(2,1)S(1)}, u32[]{:S(2)}, u32[]{:S(2)}) %collective-permute-start.8) | collective-permute-done | bytes 131104 | tf_op jit(solution)/shard_map/ppermute | solution.py:594
  20.6 11.3 %collective-permute-done.10 = bf16[4,2,64,512]{3,2,1,0:T(8,128)(2,1)S(1)} collective-permute-done((bf16[4,2,64,512]{3,2,1,0:T(8,128)(2,1)S(1)}, bf16[4,2,64,512]{3,2,1,0:T(8,128)(2,1)S(1)}, u32[]{:S(2)}, u32[]{:S(2)}) %collective-permute-start.10) | collective-permute-done | bytes 524320 | tf_op jit(solution)/shard_map/ppermute | solution.py:594
  31.9 10.1 %collective-permute-done.11 = bf16[4,2,64,512]{3,2,1,0:T(8,128)(2,1)S(1)} collective-permute-done((bf16[4,2,64,512]{3,2,1,0:T(8,128)(2,1)S(1)}, bf16[4,2,64,512]{3,2,1,0:T(8,128)(2,1)S(1)}, u32[]{:S(2)}, u32[]{:S(2)}) %collective-permute-start.11) | collective-permute-done | bytes 524320 | tf_op jit(solution)/shard_map/ppermute | solution.py:594
  43.9 3.4 %collective-permute-start = (bf16[4,64,128]{2,1,0:T(8,128)(2,1)S(1)}, bf16[4,64,128]{2,1,0:T(8,128)(2,1)S(1)}, u32[]{:S(2)}, u32[]{:S(2)}) collective-permute-start(bf16[4,64,128]{2,1,0:T(8,128)(2,1)S(1)} %get-tuple-element.205), channel_id=1, source_target_pairs={{0,1},{1,2},{2,3},{3,0},{4,5},{5,6},{6,7},{7,4},{8,9},{9,10},{10,1... | collective-permute-start | bytes 196616 | tf_op jit(solution)/shard_map/ppermute | solution.py:594
  50.2 3.5 %collective-permute-done.1 = bf16[4,64,128]{2,1,0:T(8,128)(2,1)S(1)} collective-permute-done((bf16[4,64,128]{2,1,0:T(8,128)(2,1)S(1)}, bf16[4,64,128]{2,1,0:T(8,128)(2,1)S(1)}, u32[]{:S(2)}, u32[]{:S(2)}) %collective-permute-start.1) | collective-permute-done | bytes 65568 | tf_op jit(solution)/shard_map/ppermute | solution.py:594
  58.1 5.8 %collective-permute-done.3 = bf16[4,4,64,128]{3,2,1,0:T(8,128)(2,1)S(1)} collective-permute-done((bf16[4,4,64,128]{3,2,1,0:T(8,128)(2,1)S(1)}, bf16[4,4,64,128]{3,2,1,0:T(8,128)(2,1)S(1)}, u32[]{:S(2)}, u32[]{:S(2)}) %collective-permute-start.3) | collective-permute-done | bytes 262176 | tf_op jit(solution)/shard_map/ppermute | solution.py:594
  63.9 4.6 %collective-permute-done.4 = bf16[4,4,64,128]{3,2,1,0:T(8,128)(2,1)S(1)} collective-permute-done((bf16[4,4,64,128]{3,2,1,0:T(8,128)(2,1)S(1)}, bf16[4,4,64,128]{3,2,1,0:T(8,128)(2,1)S(1)}, u32[]{:S(2)}, u32[]{:S(2)}) %collective-permute-start.4) | collective-permute-done | bytes 262176 | tf_op jit(solution)/shard_map/ppermute | solution.py:594
  71.4 3.4 %pre.1 = (f32[800,512]{1,0:T(8,128)S(1)}, bf16[800,512]{1,0:T(8,128)(2,1)S(1)}, bf16[512,800]{1,0:T(8,128)(2,1)S(1)}) custom-call(bf16[800,512]{1,0:T(8,128)(2,1)S(1)} %bitcast.124, f32[16,512]{1,0:T(8,128)S(1)} %copy-done.8), custom_call_target="tpu_custom_call" | custom-call | bytes 27000000 | tf_op jit(solution)/shard_map/pre/pallas_call | solution.py:712
  80.7 17.6 %attn.1 = (f32[4,800,128]{2,1,0:T(8,128)S(1)}, f32[4,800,128]{2,1,0:T(8,128)S(1)}, f32[4,800,128]{2,1,0:T(8,128)S(1)}, f32[4,800,128]{2,1,0:T(8,128)S(1)}, bf16[...) custom-call(s32[25]{0:T(128)S(1)} %concatenate.18.table.refs_0_, ...), custom_call_target="tpu_custom_call" | custom-call | bytes 63000000 | tf_op jit(solution)/shard_map/attn/pallas_call | solution.py:738
  98.4 21.1 %mlp.1 = (bf16[800,512]{1,0:T(8,128)(2,1)}, f32[800,512]{1,0:T(8,128)S(1)}, bf16[4,4,2,64,512]{4,3,2,1,0:T(8,128)(2,1)S(1)}, bf16[4,4,2,64,512]{4,3,2,1,0:T(8,128)(2,1)S(1)}, f32[4,8,512]{2,1,0:T(8,128)S(1)}) custom-call(s32[25]{0:T(128)S(1)} %concatenate.18.table.refs_0_, bf16[800,512]{1,0:T(8,128)(2,1)S(1)} %get-tuple-element.110.n2, ...), custom_call_target="tpu_custom_call" | custom-call | bytes 78000000 | tf_op jit(solution)/shard_map/mlp/pallas_call | solution.py:765
  119.9 3.3 %mid.1 = (f32[800,512]{1,0:T(8,128)S(1)}, bf16[800,512]{1,0:T(8,128)(2,1)S(1)}, bf16[512,800]{1,0:T(8,128)(2,1)S(1)}, f32[8,512]{1,0:T(8,128)S(1)}) custom-call(f32[800,512]{1,0:T(8,128)S(1)} %get-tuple-element.115.gn2, f32[800,512]{1,0:T(8,128)S(1)} %get-tuple-element.113.s1, bf16[800,512]{1,0:T(8,128)(2,1)S(1)} %bitcast.123, f32[16,512]{1,0:T(8,128)S(1)} %copy-done.8), custom_call_target="tpu_custom_call" | custom-call | bytes 12000000 | tf_op jit(solution)/shard_map/mid/pallas_call | solution.py:806
  123.2 24.9 %attn_back_a.1 = (bf16[4,3,4,64,128]{4,3,2,1,0:T(8,128)(2,1)S(1)}, bf16[4,3,4,64,128]{4,3,2,1,0:T(8,128)(2,1)S(1)}, f32[800,512]{1,0:T(8,128)S(1)}, f32[3,56,128]{2,1,0:T(8,128)S(1)}) custom-call(s32[25]{0:T(128)S(1)} %concatenate.18.table.refs_0_, bf16[512,800]{1,0:T(8,128)(2,1)S(1)} %copy-done.5, bf16[800,512]{1,0:T(8,128)(2,1)S(1)} %get-tuple-element.118.refs_2_, ...), custom_call_target="tpu_custom_call" | custom-call | bytes 63000000 | tf_op jit(solution)/shard_map/attn_back_a/pallas_call | solution.py:826
  148.3 8.8 %attn_back_b.1 = (bf16[4,1,4,64,128]{4,3,2,1,0:T(8,128)(2,1)S(1)}, bf16[4,1,4,64,128]{4,3,2,1,0:T(8,128)(2,1)S(1)}, f32[800,512]{1,0:T(8,128)S(1)}, f32[1,56,128]{2,1,0:T(8,128)S(1)}) custom-call(s32[25]{0:T(128)S(1)} %concatenate.18.table.refs_0_, bf16[512,800]{1,0:T(8,128)(2,1)S(1)} %copy-done.5, bf16[800,512]{1,0:T(8,128)(2,1)S(1)} %get-tuple-element.118.refs_2_, ...), custom_call_target="tpu_custom_call" | custom-call | bytes 21000000 | tf_op jit(solution)/shard_map/attn_back_b/pallas_call | solution.py:826
  157.7 7.0 %tail.1 = (bf16[800,512]{1,0:T(8,128)(2,1)}, f32[4,4,24,128]{3,2,1,0:T(8,128)S(1)}) custom-call(s32[25]{0:T(128)S(1)} %concatenate.18.table.refs_0_, f32[800,512]{1,0:T(8,128)S(1)} %copy-done.3, f32[800,512]{1,0:T(8,128)S(1)} %get-tuple-element.116.gs1, f32[800,512]{1,0:T(8,128)S(1)} %get-tuple-element.126.gn1, bf16[800,512]{1,0:T(8,128)(2,1)S(1)} %bitcast.125, ...), custom_call_target="tpu_custom_call" | custom-call | bytes 27000000 | tf_op jit(solution)/shard_map/tail/pallas_call | solution.py:871
  173.2 6.1 %collective-permute-done.16 = bf16[4,4,64,128]{3,2,1,0:T(8,128)(2,1)S(1)} collective-permute-done((bf16[4,4,64,128]{3,2,1,0:T(8,128)(2,1)S(1)}, bf16[4,4,64,128]{3,2,1,0:T(8,128)(2,1)S(1)}, u32[]{:S(2)}, u32[]{:S(2)}) %collective-permute-start.16) | collective-permute-done | bytes 262176 | tf_op jit(solution)/shard_map/ppermute | solution.py:594
  179.3 3.2 %collective-permute-done.17 = bf16[4,4,64,128]{3,2,1,0:T(8,128)(2,1)S(1)} collective-permute-done((bf16[4,4,64,128]{3,2,1,0:T(8,128)(2,1)S(1)}, bf16[4,4,64,128]{3,2,1,0:T(8,128)(2,1)S(1)}, u32[]{:S(2)}, u32[]{:S(2)}) %collective-permute-start.17) | collective-permute-done | bytes 262176 | tf_op jit(solution)/shard_map/ppermute | solution.py:594
  191.0 3.4 %collective-permute-done.22 = bf16[288,128]{1,0:T(8,128)(2,1)S(1)} collective-permute-done((bf16[288,128]{1,0:T(8,128)(2,1)S(1)}, bf16[288,128]{1,0:T(8,128)(2,1)S(1)}, u32[]{:S(2)}, u32[]{:S(2)}) %collective-permute-start.22) | collective-permute-done | bytes 73760 | tf_op jit(solution)/shard_map/ppermute | solution.py:594
  199.6 9.2 %collective-permute-done.27 = bf16[4,2,64,512]{3,2,1,0:T(8,128)(2,1)S(1)} collective-permute-done((bf16[4,2,64,512]{3,2,1,0:T(8,128)(2,1)S(1)}, bf16[4,2,64,512]{3,2,1,0:T(8,128)(2,1)S(1)}, u32[]{:S(2)}, u32[]{:S(2)}) %collective-permute-start.27) | collective-permute-done | bytes 524320 | tf_op jit(solution)/shard_map/ppermute | solution.py:594
  214.6 3.2 %collective-permute-done.29 = bf16[2,64,512]{2,1,0:T(8,128)(2,1)S(1)} collective-permute-done((bf16[2,64,512]{2,1,0:T(8,128)(2,1)S(1)}, bf16[2,64,512]{2,1,0:T(8,128)(2,1)S(1)}, u32[]{:S(2)}, u32[]{:S(2)}) %collective-permute-start.29) | collective-permute-done | bytes 131104 | tf_op jit(solution)/shard_map/ppermute | solution.py:594
  217.8 4.4 %collective-permute-done.30 = bf16[2,64,512]{2,1,0:T(8,128)(2,1)S(1)} collective-permute-done((bf16[2,64,512]{2,1,0:T(8,128)(2,1)S(1)}, bf16[2,64,512]{2,1,0:T(8,128)(2,1)S(1)}, u32[]{:S(2)}, u32[]{:S(2)}) %collective-permute-start.30) | collective-permute-done | bytes 131104 | tf_op jit(solution)/shard_map/ppermute | solution.py:594
  225.5 3.3 %collective-permute-start.33 = (f32[32,128]{1,0:T(8,128)S(1)}, f32[32,128]{1,0:T(8,128)S(1)}, u32[]{:S(2)}, u32[]{:S(2)}) collective-permute-start(f32[32,128]{1,0:T(8,128)S(1)} %pad_add_fusion), channel_id=1, source_target_pairs={{0,1},{1,2},{2,3},{3,0},{4,5},{5,6},{6,7},{7,4},{8,9},{9,10},{10,1... | collective-permute-start | bytes 49160 | tf_op jit(solution)/shard_map/ppermute | solution.py:594
  233.7 2.8 %collective-permute-start.38 = (f32[4,32,128]{2,1,0:T(8,128)S(1)}, f32[4,32,128]{2,1,0:T(8,128)S(1)}, u32[]{:S(2)}, u32[]{:S(2)}) collective-permute-start(f32[4,32,128]{2,1,0:T(8,128)S(1)} %get-tuple-element.203), channel_id=1, source_target_pairs={{0,24},{4,28},{8,0},{12,4},{16,8},{20,12},{24,16},{28,20},{1,25},{... | collective-permute-start | bytes 196616 | tf_op jit(solution)/shard_map/ppermute | solution.py:594
  239.4 2.7 %adam.1 = (f32[1,1]{1,0:T(1,128)}, f32[3,64,128]{2,1,0:T(8,128)}, f32[3,64,128]{2,1,0:T(8,128)}, f32[3,64,128]{2,1,0:T(8,128)}, f32[3,64,128]{2,1,0:T(8,128)}, /...) custom-call(s32[25]{0:T(128)S(1)} %concatenate.18.table.refs_0_, ...), custom_call_target="tpu_custom_call" | custom-call | bytes 12000000 | tf_op jit(solution)/shard_map/adam/pallas_call | solution.py:953
  (181 shorter events, 68.5 us)
Async XLA Ops:
  1.7 9.6 %collective-permute-start.7 = (bf16[2,64,512]{2,1,0:T(8,128)(2,1)S(1)}, bf16[2,64,512]{2,1,0:T(8,128)(2,1)S(1)}, u32[]{:S(2)}, u32[]{:S(2)}) collective-permute-start(bf16[2,64,512]{2,1,0:T(8,128)(2,1)S(1)} %get-tuple-element.201), channel_id=1, source_target_pairs={{0,1},{1,2},{2,3},{3,0},{4,5},{5,6},{6,7},{7,4},{8,9},{9,10},{10,1... | collective-permute-start | bytes 393224 | tf_op jit(solution)/shard_map/ppermute | solution.py:594
  4.8 11.2 %collective-permute-start.8 = (bf16[2,64,512]{2,1,0:T(8,128)(2,1)S(1)}, bf16[2,64,512]{2,1,0:T(8,128)(2,1)S(1)}, u32[]{:S(2)}, u32[]{:S(2)}) collective-permute-start(bf16[2,64,512]{2,1,0:T(8,128)(2,1)S(1)} %get-tuple-element.201), channel_id=1, source_target_pairs={{0,2},{1,3},{2,0},{3,1},{4,6},{5,7},{6,4},{7,5},{8,10},{9,11},{10,... | collective-permute-start | bytes 393224 | tf_op jit(solution)/shard_map/ppermute | solution.py:594
  7.4 8.6 %collective-permute-start.9 = (bf16[2,64,512]{2,1,0:T(8,128)(2,1)S(1)}, bf16[2,64,512]{2,1,0:T(8,128)(2,1)S(1)}, u32[]{:S(2)}, u32[]{:S(2)}) collective-permute-start(bf16[2,64,512]{2,1,0:T(8,128)(2,1)S(1)} %get-tuple-element.201), channel_id=1, source_target_pairs={{0,3},{1,0},{2,1},{3,2},{4,7},{5,4},{6,5},{7,6},{8,11},{9,8},{10,9... | collective-permute-start | bytes 393224 | tf_op jit(solution)/shard_map/ppermute | solution.py:594
  16.1 15.8 %collective-permute-start.10 = (bf16[4,2,64,512]{3,2,1,0:T(8,128)(2,1)S(1)}, bf16[4,2,64,512]{3,2,1,0:T(8,128)(2,1)S(1)}, u32[]{:S(2)}, u32[]{:S(2)}) collective-permute-start(bf16[4,2,64,512]{3,2,1,0:T(8,128)(2,1)S(1)} %get-tuple-element.189), channel_id=1, source_target_pairs={{0,8},{4,12},{8,16},{12,20},{16,24},{20,28},{24,0},{28,4},{1,9},{5... | collective-permute-start | bytes 1572872 | tf_op jit(solution)/shard_map/ppermute | solution.py:594
  17.7 24.4 %collective-permute-start.11 = (bf16[4,2,64,512]{3,2,1,0:T(8,128)(2,1)S(1)}, bf16[4,2,64,512]{3,2,1,0:T(8,128)(2,1)S(1)}, u32[]{:S(2)}, u32[]{:S(2)}) collective-permute-start(bf16[4,2,64,512]{3,2,1,0:T(8,128)(2,1)S(1)} %get-tuple-element.189), channel_id=1, source_target_pairs={{0,16},{4,20},{8,24},{12,28},{16,0},{20,4},{24,8},{28,12},{1,17},{... | collective-permute-start | bytes 1572872 | tf_op jit(solution)/shard_map/ppermute | solution.py:594
  19.2 23.0 %collective-permute-start.12 = (bf16[4,2,64,512]{3,2,1,0:T(8,128)(2,1)S(1)}, bf16[4,2,64,512]{3,2,1,0:T(8,128)(2,1)S(1)}, u32[]{:S(2)}, u32[]{:S(2)}) collective-permute-start(bf16[4,2,64,512]{3,2,1,0:T(8,128)(2,1)S(1)} %get-tuple-element.189), channel_id=1, source_target_pairs={{0,24},{4,28},{8,0},{12,4},{16,8},{20,12},{24,16},{28,20},{1,25},{... | collective-permute-start | bytes 1572872 | tf_op jit(solution)/shard_map/ppermute | solution.py:594
  43.8 54.6 %collective-permute-start.13 = (bf16[4,4,2,64,512]{4,3,2,1,0:T(8,128)(2,1)}, bf16[4,4,2,64,512]{4,3,2,1,0:T(8,128)(2,1)}, u32[]{:S(2)}, u32[]{:S(2)}) collective-permute-start(bf16[4,4,2,64,512]{4,3,2,1,0:T(8,128)(2,1)} %pad_maximum_fusion.own), channel_id=1, source_target_pairs={{0,4},{4,0},{8,12},{12,8},{16,20},{20,16},{24,28},{28,24},{1,5},{5... | collective-permute-start | bytes 6291464 | tf_op jit(solution)/shard_map/ppermute | solution.py:594
  53.7 10.2 %collective-permute-start.3 = (bf16[4,4,64,128]{3,2,1,0:T(8,128)(2,1)S(1)}, bf16[4,4,64,128]{3,2,1,0:T(8,128)(2,1)S(1)}, u32[]{:S(2)}, u32[]{:S(2)}) collective-permute-start(bf16[4,4,64,128]{3,2,1,0:T(8,128)(2,1)S(1)} %get-tuple-element.194), channel_id=1, source_target_pairs={{0,8},{4,12},{8,16},{12,20},{16,24},{20,28},{24,0},{28,4},{1,9},{5... | collective-permute-start | bytes 786440 | tf_op jit(solution)/shard_map/ppermute | solution.py:594
  55.4 13.0 %collective-permute-start.4 = (bf16[4,4,64,128]{3,2,1,0:T(8,128)(2,1)S(1)}, bf16[4,4,64,128]{3,2,1,0:T(8,128)(2,1)S(1)}, u32[]{:S(2)}, u32[]{:S(2)}) collective-permute-start(bf16[4,4,64,128]{3,2,1,0:T(8,128)(2,1)S(1)} %get-tuple-element.194), channel_id=1, source_target_pairs={{0,16},{4,20},{8,24},{12,28},{16,0},{20,4},{24,8},{28,12},{1,17},{... | collective-permute-start | bytes 786440 | tf_op jit(solution)/shard_map/ppermute | solution.py:594
  56.0 12.5 %collective-permute-start.5 = (bf16[4,4,64,128]{3,2,1,0:T(8,128)(2,1)S(1)}, bf16[4,4,64,128]{3,2,1,0:T(8,128)(2,1)S(1)}, u32[]{:S(2)}, u32[]{:S(2)}) collective-permute-start(bf16[4,4,64,128]{3,2,1,0:T(8,128)(2,1)S(1)} %get-tuple-element.194), channel_id=1, source_target_pairs={{0,24},{4,28},{8,0},{12,4},{16,8},{20,12},{24,16},{28,20},{1,25},{... | collective-permute-start | bytes 786440 | tf_op jit(solution)/shard_map/ppermute | solution.py:594
  68.6 9.6 %collective-permute-start.6 = (bf16[4,4,4,64,128]{4,3,2,1,0:T(8,128)(2,1)S(1)}, bf16[4,4,4,64,128]{4,3,2,1,0:T(8,128)(2,1)S(1)}, u32[]{:S(2)}, u32[]{:S(2)}) collective-permute-start(bf16[4,4,4,64,128]{4,3,2,1,0:T(8,128)(2,1)S(1)} %pad_maximum_fusion.1.own.refs_4_), channel_id=1, source_target_pairs={{0,4},{4,0},{8,12},{12,8},{16,20},{20,16},{24,28},{28,24},{1,5},{5... | collective-permute-start | bytes 3145736 | tf_op jit(solution)/shard_map/ppermute | solution.py:594
  119.5 63.5 %collective-permute-start.25 = (bf16[4,4,2,64,512]{4,3,2,1,0:T(8,128)(2,1)S(1)}, bf16[4,4,2,64,512]{4,3,2,1,0:T(8,128)(2,1)S(1)}, u32[]{:S(2)}, u32[]{:S(2)}) collective-permute-start(bf16[4,4,2,64,512]{4,3,2,1,0:T(8,128)(2,1)S(1)} %get-tuple-element.139), channel_id=1, source_target_pairs={{0,4},{4,0},{8,12},{12,8},{16,20},{20,16},{24,28},{28,24},{1,5},{5... | collective-permute-start | bytes 6291464 | tf_op jit(solution)/shard_map/ppermute | solution.py:594
  148.1 20.7 %collective-permute-start.14 = (bf16[4,3,4,64,128]{4,3,2,1,0:T(8,128)(2,1)S(1)}, bf16[4,3,4,64,128]{4,3,2,1,0:T(8,128)(2,1)S(1)}, u32[]{:S(2)}, u32[]{:S(2)}) collective-permute-start(bf16[4,3,4,64,128]{4,3,2,1,0:T(8,128)(2,1)S(1)} %get-tuple-element.134), channel_id=1, source_target_pairs={{0,4},{4,0},{8,12},{12,8},{16,20},{20,16},{24,28},{28,24},{1,5},{5... | collective-permute-start | bytes 2359304 | tf_op jit(solution)/shard_map/ppermute | solution.py:594
  157.0 10.0 %collective-permute-start.15 = (bf16[4,1,4,64,128]{4,3,2,1,0:T(8,128)(2,1)S(1)}, bf16[4,1,4,64,128]{4,3,2,1,0:T(8,128)(2,1)S(1)}, u32[]{:S(2)}, u32[]{:S(2)}) collective-permute-start(bf16[4,1,4,64,128]{4,3,2,1,0:T(8,128)(2,1)S(1)} %get-tuple-element.136), channel_id=1, source_target_pairs={{0,4},{4,0},{8,12},{12,8},{16,20},{20,16},{24,28},{28,24},{1,5},{5... | collective-permute-start | bytes 786440 | tf_op jit(solution)/shard_map/ppermute | solution.py:594
  169.2 10.1 %collective-permute-start.16 = (bf16[4,4,64,128]{3,2,1,0:T(8,128)(2,1)S(1)}, bf16[4,4,64,128]{3,2,1,0:T(8,128)(2,1)S(1)}, u32[]{:S(2)}, u32[]{:S(2)}) collective-permute-start(bf16[4,4,64,128]{3,2,1,0:T(8,128)(2,1)S(1)} %get-tuple-element.182), channel_id=1, source_target_pairs={{0,8},{4,12},{8,16},{12,20},{16,24},{20,28},{24,0},{28,4},{1,9},{5... | collective-permute-start | bytes 786440 | tf_op jit(solution)/shard_map/ppermute | solution.py:594
  169.8 12.6 %collective-permute-start.17 = (bf16[4,4,64,128]{3,2,1,0:T(8,128)(2,1)S(1)}, bf16[4,4,64,128]{3,2,1,0:T(8,128)(2,1)S(1)}, u32[]{:S(2)}, u32[]{:S(2)}) collective-permute-start(bf16[4,4,64,128]{3,2,1,0:T(8,128)(2,1)S(1)} %get-tuple-element.184), channel_id=1, source_target_pairs={{0,16},{4,20},{8,24},{12,28},{16,0},{20,4},{24,8},{28,12},{1,17},{... | collective-permute-start | bytes 786440 | tf_op jit(solution)/shard_map/ppermute | solution.py:594
  171.0 11.7 %collective-permute-start.18 = (bf16[4,4,64,128]{3,2,1,0:T(8,128)(2,1)S(1)}, bf16[4,4,64,128]{3,2,1,0:T(8,128)(2,1)S(1)}, u32[]{:S(2)}, u32[]{:S(2)}) collective-permute-start(bf16[4,4,64,128]{3,2,1,0:T(8,128)(2,1)S(1)} %get-tuple-element.183), channel_id=1, source_target_pairs={{0,24},{4,28},{8,0},{12,4},{16,8},{20,12},{24,16},{28,20},{1,25},{... | collective-permute-start | bytes 786440 | tf_op jit(solution)/shard_map/ppermute | solution.py:594
  183.9 15.7 %collective-permute-start.26 = (bf16[4,2,64,512]{3,2,1,0:T(8,128)(2,1)S(1)}, bf16[4,2,64,512]{3,2,1,0:T(8,128)(2,1)S(1)}, u32[]{:S(2)}, u32[]{:S(2)}) collective-permute-start(bf16[4,2,64,512]{3,2,1,0:T(8,128)(2,1)S(1)} %get-tuple-element.179), channel_id=1, source_target_pairs={{0,8},{4,12},{8,16},{12,20},{16,24},{20,28},{24,0},{28,4},{1,9},{5... | collective-permute-start | bytes 1572872 | tf_op jit(solution)/shard_map/ppermute | solution.py:594
  185.9 23.0 %collective-permute-start.27 = (bf16[4,2,64,512]{3,2,1,0:T(8,128)(2,1)S(1)}, bf16[4,2,64,512]{3,2,1,0:T(8,128)(2,1)S(1)}, u32[]{:S(2)}, u32[]{:S(2)}) collective-permute-start(bf16[4,2,64,512]{3,2,1,0:T(8,128)(2,1)S(1)} %get-tuple-element.181), channel_id=1, source_target_pairs={{0,16},{4,20},{8,24},{12,28},{16,0},{20,4},{24,8},{28,12},{1,17},{... | collective-permute-start | bytes 1572872 | tf_op jit(solution)/shard_map/ppermute | solution.py:594
  187.0 22.2 %collective-permute-start.28 = (bf16[4,2,64,512]{3,2,1,0:T(8,128)(2,1)S(1)}, bf16[4,2,64,512]{3,2,1,0:T(8,128)(2,1)S(1)}, u32[]{:S(2)}, u32[]{:S(2)}) collective-permute-start(bf16[4,2,64,512]{3,2,1,0:T(8,128)(2,1)S(1)} %get-tuple-element.180), channel_id=1, source_target_pairs={{0,24},{4,28},{8,0},{12,4},{16,8},{20,12},{24,16},{28,20},{1,25},{... | collective-permute-start | bytes 1572872 | tf_op jit(solution)/shard_map/ppermute | solution.py:594
  190.0 6.7 %collective-permute-start.23 = (bf16[288,128]{1,0:T(8,128)(2,1)S(1)}, bf16[288,128]{1,0:T(8,128)(2,1)S(1)}, u32[]{:S(2)}, u32[]{:S(2)}) collective-permute-start(bf16[288,128]{1,0:T(8,128)(2,1)S(1)} %get-tuple-element.192), channel_id=1, source_target_pairs={{0,2},{1,3},{2,0},{3,1},{4,6},{5,7},{6,4},{7,5},{8,10},{9,11},{10,... | collective-permute-start | bytes 221192 | tf_op jit(solution)/shard_map/ppermute | solution.py:594
  209.5 8.3 %collective-permute-start.29 = (bf16[2,64,512]{2,1,0:T(8,128)(2,1)S(1)}, bf16[2,64,512]{2,1,0:T(8,128)(2,1)S(1)}, u32[]{:S(2)}, u32[]{:S(2)}) collective-permute-start(bf16[2,64,512]{2,1,0:T(8,128)(2,1)S(1)} %get-tuple-element.185), channel_id=1, source_target_pairs={{0,1},{1,2},{2,3},{3,0},{4,5},{5,6},{6,7},{7,4},{8,9},{9,10},{10,1... | collective-permute-start | bytes 393224 | tf_op jit(solution)/shard_map/ppermute | solution.py:594
  211.5 10.7 %collective-permute-start.30 = (bf16[2,64,512]{2,1,0:T(8,128)(2,1)S(1)}, bf16[2,64,512]{2,1,0:T(8,128)(2,1)S(1)}, u32[]{:S(2)}, u32[]{:S(2)}) collective-permute-start(bf16[2,64,512]{2,1,0:T(8,128)(2,1)S(1)} %get-tuple-element.187), channel_id=1, source_target_pairs={{0,2},{1,3},{2,0},{3,1},{4,6},{5,7},{6,4},{7,5},{8,10},{9,11},{10,... | collective-permute-start | bytes 393224 | tf_op jit(solution)/shard_map/ppermute | solution.py:594
  212.6 9.7 %collective-permute-start.31 = (bf16[2,64,512]{2,1,0:T(8,128)(2,1)S(1)}, bf16[2,64,512]{2,1,0:T(8,128)(2,1)S(1)}, u32[]{:S(2)}, u32[]{:S(2)}) collective-permute-start(bf16[2,64,512]{2,1,0:T(8,128)(2,1)S(1)} %get-tuple-element.186), channel_id=1, source_target_pairs={{0,3},{1,0},{2,1},{3,2},{4,7},{5,4},{6,5},{7,6},{8,11},{9,8},{10,9... | collective-permute-start | bytes 393224 | tf_op jit(solution)/shard_map/ppermute | solution.py:594
  (52 other events, 1037.4 us)

commit v4 on v3

--- a/solution.py
+++ b/solution.py
@@ -1,3 +1,4 @@
+import math
 from functools import partial
 
 import jax
@@ -133,6 +134,20 @@
     transposed(n1t_ref, n1_ref, rows)
 
 
+def taps_kernel(radius, hp, rows_o, mask_o):
+    lane = lax.broadcasted_iota(jnp.int32, (1, hp.shape[1]), 1)
+    reach = jnp.zeros((1, hp.shape[1]), jnp.int32)
+    for h in range(hp.shape[1] // HD):
+        inside = (lane >= h * HD) & (lane < (h + 1) * HD)
+        reach = reach + jnp.where(inside, radius[h], 0)
+    keep = [jnp.where(reach >= m, F32(1.0), F32(0.0)) for m in range(4)]
+    for t in range(TAPS):
+        row = keep[max(abs(t // GRID - 3), abs(t % GRID - 3))]
+        mask_o[t : t + 1] = row
+        rows_o[t : t + 1] = hp[t : t + 1] * row
+    rows_o[TAPS:] = hp[TAPS:]
+
+
 def cot_kernel(og_ref, ogt_ref, ogsum_ref):
     rows, width = og_ref.shape
     wide = og_ref[...].astype(F32).reshape(rows // 8, 8, width)
@@ -158,30 +173,36 @@
         self.up, self.nh = up, nh
 
 
-def gather_weights(table, slots, own, recv, to, kinds, width):
+def gather_weights(table, slots, own, recv, to, starts, width):
     size = own.shape[3]
     for u in range(slots.up):
         at = table[slots.up_in + u]
         for low, src in ((table[slots.low], own), (1 - table[slots.low], recv)):
             rows = rows_at((2 * u + low) * size, size)
-            for k in range(kinds):
-                to[rows, k * width : (k + 1) * width] = src[at, 0, k]
-
-
-def scatter_grads(table, slots, left, right, keep, send, kinds, width):
+            for k, start in enumerate(starts):
+                to[rows, start : start + width] = src[at, 0, k]
+
+
+def scatter_grads(table, slots, left, right, keep, send, kinds, width, head=0, sums=None):
     size = keep.shape[3]
     lows = (table[slots.low], 1 - table[slots.low])
     starts = [(2 * u + low) * size for low in lows for u in range(slots.up)]
-    lhs = jnp.concatenate([left[rows_at(start, size), :] for start in starts], axis=0)
+    lhs = [left[rows_at(start, size), :] for start in starts]
+    if sums is not None:
+        lhs.append(jnp.ones((16, left.shape[1]), BF16))
+    lhs = jnp.concatenate(lhs, axis=0)
     step = max(1, COLS // width)
     for n in range(0, len(kinds), step):
         some = kinds[n : n + step]
-        value = dot(lhs, right[:, n * width : (n + len(some)) * width]).astype(BF16)
+        full = dot(lhs, right[:, n * width : (n + len(some)) * width])
+        if sums is not None:
+            sums[...] = full[2 * slots.up * size : 2 * slots.up * size + 8]
+        value = full[: 2 * slots.up * size].astype(BF16)
         for b in range(2 * slots.up):
             to = (keep, send)[b // slots.up]
             at = table[slots.up_out + b % slots.up]
             for i, k in enumerate(some):
-                to[at, 0, k] = value[b * size : (b + 1) * size, i * width : (i + 1) * width]
+                to[at, head, k] = value[b * size : (b + 1) * size, i * width : (i + 1) * width]
 
 
 def attn_kernel(
@@ -203,7 +224,7 @@
         vp[first + rows :] = jnp.zeros((vp.shape[0] - first - rows, LANE), F32)
         s1_o[...] = s0[...] + rp[14:15]
 
-    gather_weights(table, slots, own, recv, wbuf, 4, LANE)
+    gather_weights(table, slots, own, recv, wbuf, range(0, 4 * LANE, LANE), LANE)
     qk = dot(n1[...], wbuf[:, 0 : 2 * LANE])
     q = qk[:, 0:LANE] + hp[50:51]
     qs[0:rows] = q
@@ -227,7 +248,7 @@
         fs[at, :] = dot(qs[at, :].astype(BF16), ctx.astype(BF16))
         return carry
 
-    lax.fori_loop(0, imgs, image_body, 0, unroll=4)
+    lax.fori_loop(0, imgs, image_body, 0, unroll=8)
     at_o[0, 0:imgs] = fs[0:imgs].astype(BF16)
     cv_o[0, 0:imgs] = jnp.zeros((imgs, LANE), F32)
     everything = slice(0, LANE)
@@ -261,33 +282,33 @@
         transposed(n2t_o, n2_o, rows)
 
 
-def mlp_kernel(
-    table, n2, n2t, og, ogt, s1, own, recv, ub, rp,
-    out_o, gn2_o, keep_o, send_o, ubg_o,
-    wbuf, hs, ds, hb, gb, oacc,
-    *, imgs, slots, hid,
-):
+def mlp_kernel(table, n2, n2t, og, ogt, s1, *refs, imgs, slots, hid, heads):
+    weights, (ub, rp) = refs[: 2 * heads], refs[2 * heads : 2 * heads + 2]
+    out_o, gn2_o, keep_o, send_o, ubg_o, wbuf, hs, ds, hb, gb, oacc = refs[2 * heads + 2 :]
     j = pl.program_id(0)
     rows = SEQ * imgs
-    gather_weights(table, slots, own, recv, wbuf, 2, hid)
-    for c in range(0, hid, COLS):
-        hs[:, c : c + COLS] = dot(n2[...], wbuf[:, c : c + COLS]) + ub[0, :, c : c + COLS]
-        ds[:, c : c + COLS] = dot(og[...], wbuf[:, hid + c : hid + c + COLS])
+    span = heads * hid
+    for h in range(heads):
+        starts = (h * hid, span + h * hid)
+        gather_weights(table, slots, weights[h], weights[heads + h], wbuf, starts, hid)
+    for h in range(heads):
+        bias = ub[table[slots.head_col + j * heads + h]]
+        for c in range(0, hid, COLS):
+            at = slice(h * hid + c, h * hid + c + COLS)
+            hs[:, at] = dot(n2[...], wbuf[:, at]) + bias[:, c : c + COLS]
+            ds[:, at] = dot(og[...], wbuf[:, span + at.start : span + at.stop])
     step = 2 * imgs
 
-    def gelu_body(r, total):
+    def gelu_body(r, carry):
         at = rows_at(r * step, step)
         pre = hs[at, :]
-        cdf = 0.5 * (1.0 + lax.erf(pre * F32(0.5**0.5)))
-        pdf = jnp.exp(-0.5 * pre * pre) * F32(0.3989422804014327)
+        cdf = 0.5 + 0.5 * lax.erf(pre * F32(0.5**0.5))
+        pdf = jnp.exp2(pre * pre * F32(-0.5 * math.log2(math.e)) + F32(-0.5 * math.log2(2 * math.pi)))
         hb[at, :] = (pre * cdf).astype(BF16)
-        grad = (ds[at, :] * (cdf + pre * pdf)).astype(BF16)
-        gb[at, :] = grad
-        wide = grad.astype(F32).reshape(step // 8, 8, hid)
-        return total + jnp.sum(wide, axis=0)
-
-    total = lax.fori_loop(0, rows // step, gelu_body, jnp.zeros((8, hid), F32))
-    ubg_o[0] = jnp.broadcast_to(jnp.sum(total, axis=0, keepdims=True), (8, hid))
+        gb[at, :] = (ds[at, :] * (cdf + pre * pdf)).astype(BF16)
+        return carry
+
+    lax.fori_loop(0, rows // step, gelu_body, 0)
 
     @pl.when(j == 0)
     def _():
@@ -296,10 +317,13 @@
 
     for c in range(0, oacc.shape[1], COLS):
         cols = slice(c, c + COLS)
-        oacc[:, cols] += dot(hb[...], wbuf[cols, hid:], NT)
-        gn2_o[:, cols] += dot(gb[...], wbuf[cols, 0:hid], NT)
-    scatter_grads(table, slots, n2t, gb, keep_o, send_o, (0,), hid)
-    scatter_grads(table, slots, ogt, hb, keep_o, send_o, (1,), hid)
+        oacc[:, cols] += dot(hb[...], wbuf[cols, span:], NT)
+        gn2_o[:, cols] += dot(gb[...], wbuf[cols, 0:span], NT)
+    for h in range(heads):
+        cols = slice(h * hid, (h + 1) * hid)
+        sums = ubg_o.at[table[slots.head_col + j * heads + h]]
+        scatter_grads(table, slots, n2t, gb.at[:, cols], keep_o, send_o, (0,), hid, h, sums)
+        scatter_grads(table, slots, ogt, hb.at[:, cols], keep_o, send_o, (1,), hid, h)
 
     @pl.when(j == pl.num_programs(0) - 1)
     def _():
@@ -355,7 +379,7 @@
             ref[first + rows :] = jnp.zeros((ref.shape[0] - first - rows, LANE), F32)
         gn1_o[...] = gn1_i[...] if begin else jnp.zeros(gn1_o.shape, F32)
 
-    gather_weights(table, slots, own, recv, wbuf, 4, LANE)
+    gather_weights(table, slots, own, recv, wbuf, range(0, 4 * LANE, LANE), LANE)
     grad = dot(gal[...], wbuf[:, 3 * LANE :])
     gs[0:rows] = grad
     q = q_i[0]
@@ -382,7 +406,7 @@
         fv[at, :] = dot(k, gctx)
         return carry
 
-    lax.fori_loop(0, imgs, image_body, 0, unroll=4)
+    lax.fori_loop(0, imgs, image_body, 0, unroll=8)
     soft = ks[0:rows].reshape(SEQ, imgs, LANE)
     gsoft = fk[0:rows].reshape(SEQ, imgs, LANE)
     total = jnp.sum(soft * gsoft, axis=0, keepdims=True)
@@ -518,15 +542,6 @@
 
 def whole(shape):
     return pl.BlockSpec(shape, lambda *_: (0,) * len(shape))
-
-
-def tap_mask(radius):
-    reach = jnp.repeat(radius, HD)
-    taps = lax.broadcasted_iota(jnp.int32, (TAPS, reach.shape[0]), 0)
-    vertical = jnp.abs(taps // 7 - 3)
-    horizontal = jnp.abs(taps % 7 - 3)
-    inside = (vertical <= reach[None, :]) & (horizontal <= reach[None, :])
-    return inside.astype(F32)
 
 
 def adam_store(outs, raw, weight, first, second, average, clip, decay):
@@ -725,8 +740,17 @@
         name="cot",
     )(cot)
 
-    mask = tap_mask(kernel_radius)
-    head_rows = jnp.concatenate([head_params[:TAPS] * mask, head_params[TAPS : TAPS + 7]], axis=0)
+    head_rows, mask = pl.pallas_call(
+        taps_kernel,
+        out_shape=(shape(head_params.shape, F32), shape((TAPS, width), F32)),
+        in_specs=[
+            pl.BlockSpec(memory_space=pltpu.SMEM),
+            pl.BlockSpec(memory_space=pltpu.VMEM),
+        ],
+        compiler_params=params(2),
+        cost_estimate=cost(1),
+        name="taps",
+    )(kernel_radius, head_params)
     bias_up = head_params[TAPS + 3 :].reshape(nh, 1, hid)
     per_head = shape((nh, rows, LANE), F32)
     tile_spec = pl.BlockSpec((1, rows, LANE), lambda j, s: (j, 0, 0))
@@ -760,35 +784,42 @@
         )(table, normed_one, stream_zero, gathered_one, other_one, head_rows, rep_params)
     )
 
+    pair = 1
     two_grads = shape((up, nh, 2, size, hid), BF16)
-    two_spec = pl.BlockSpec((up, 1, 2, size, hid), lambda j, s: (0, j, 0, 0, 0))
+    two_spec = pl.BlockSpec((up, pair, 2, size, hid), lambda j, s: (0, j, 0, 0, 0))
+    all_hidden = shape((nh, 8, hid), F32)
+
+    def resident(dims):
+        zeros = (0,) * len(dims)
+        return pl.BlockSpec(dims, lambda j, s: zeros, pipeline_mode=pl.Buffered(1))
+
+    def pair_spec(n):
+        return pl.BlockSpec(
+            (up, 1, 2, size, hid), lambda j, s: (0, s[slots.head_in + pair * j + n], 0, 0, 0)
+        )
+
+    pair_specs = [pair_spec(n) for n in range(pair)]
     output, grad_norm_two, keep_two, send_two, bias_grad = pl.pallas_call(
-        partial(mlp_kernel, imgs=imgs, slots=slots, hid=hid),
-        out_shape=(low, wide, two_grads, two_grads, shape((nh, 8, hid), F32)),
+        partial(mlp_kernel, imgs=imgs, slots=slots, hid=hid, heads=pair),
+        out_shape=(low, wide, two_grads, two_grads, all_hidden),
         grid_spec=pltpu.PrefetchScalarGridSpec(
             num_scalar_prefetch=1,
-            grid=(nh,),
-            in_specs=[full, turned, full, turned, full]
-            + [weight_spec(2, hid)] * 2
-            + [pl.BlockSpec((1, 1, hid), lambda j, s: (s[slots.head_col + j], 0, 0)), rp_spec],
-            out_specs=[
-                full,
-                full,
-                two_spec,
-                two_spec,
-                pl.BlockSpec((1, 8, hid), lambda j, s: (s[slots.head_col + j], 0, 0)),
-            ],
+            grid=(nh // pair,),
+            in_specs=[resident(v) for v in ((rows, width), (width, rows)) * 2 + ((rows, width),)]
+            + pair_specs * 2
+            + [whole((nh, 1, hid)), rp_spec],
+            out_specs=[full, full, two_spec, two_spec, whole((nh, 8, hid))],
             scratch_shapes=[
-                pltpu.VMEM((width, 2 * hid), BF16),
-                pltpu.VMEM((rows, hid), F32),
-                pltpu.VMEM((rows, hid), F32),
-                pltpu.VMEM((rows, hid), BF16),
-                pltpu.VMEM((rows, hid), BF16),
+                pltpu.VMEM((width, 2 * pair * hid), BF16),
+                pltpu.VMEM((rows, pair * hid), F32),
+                pltpu.VMEM((rows, pair * hid), F32),
+                pltpu.VMEM((rows, pair * hid), BF16),
+                pltpu.VMEM((rows, pair * hid), BF16),
                 pltpu.VMEM((rows, width), F32),
             ],
         ),
         compiler_params=params(26, "arbitrary"),
-        cost_estimate=cost(26),
+        cost_estimate=cost(20),
         name="mlp",
     )(
         table,
@@ -797,8 +828,8 @@
         cot,
         cot_t,
         stream_one,
-        gathered_two,
-        other_two,
+        *[gathered_two] * pair,
+        *[other_two] * pair,
         bias_up,
         rep_params,
     )

time: 243 us -> 242 us (level)
  Pallas kernels: 89.1 us -> 84.6 us
  waiting for transfers between devices: 84 us -> 87.6 us
    ppermute x39, waiting for transfers between devices: 84 us -> 87.6 us  [turn(): return lax.ppermute(value, axis, pairs)]
    pallas_call x1, Pallas kernels: 17.6 us -> 15.2 us  [per_device(): pl.pallas_call(partial(attn_kernel, imgs=imgs, slots=slots), out_shape=(p...]
    pallas_call x1 -> x2, Pallas kernels: 21.1 us -> 20.5 us  [the longest x1 19.9 us: per_device(): pl.pallas_call(partial(mlp_kernel, imgs=imgs, slots=slots, hid=hid, heads...]
  transfers between devices with their start and end apart: 39 -> 39, of which waited for: 25 -> 28; matrix products, arithmetic and copies ran while one was open for 1% -> 1% of each run, Pallas kernels for 27% -> 26%
where the time goes in v4:
time: 242 us
  waiting for transfers between devices  87.6 us (36%)
  Pallas kernels  84.6 us (35%)
  starting transfers between devices  52.8 us (22%)
  local copies, waits for them, and re-layouts  8.21 us (3%)
  other arithmetic  6 us (2%)
  between operations  2.88 us (1%)
    ppermute x39, waiting for transfers between devices, turn(): return lax.ppermute(value, axis, pairs)  87.6 us
    ppermute x39, starting transfers between devices, turn(): return lax.ppermute(value, axis, pairs)  52.8 us
    pallas_call x2, Pallas kernels, attn_back(): pl.pallas_call(partial(attn_back_kernel, imgs=imgs, slots=slots, begin=be...  32 us
    pallas_call x1, Pallas kernels, per_device(): pl.pallas_call(partial(mlp_kernel, imgs=imgs, slots=slots, hid=hid, heads...  19.9 us
    pallas_call x1, Pallas kernels, per_device(): pl.pallas_call(partial(attn_kernel, imgs=imgs, slots=slots), out_shape=(p...  15.2 us
    unnamed x74, local copies, waits for them, and re-layouts  7.91 us
    pallas_call x1, Pallas kernels, per_device(): pl.pallas_call(partial(tail_kernel, imgs=imgs, slots=slots), out_shape=(l...  7 us
  transfers between devices with their start and end apart: 39, of which 28 were waited for; matrix products, arithmetic and copies ran while one was open for 1% of the time, Pallas kernels for 26%

profile of v4, /device:TPU:0, one launch (start us, length us, event | category | flops | bytes accessed | tf_op | source)
XLA Modules:
  0.0 242.1 jit_solution(9584962139352564332)
XLA Ops:
  1.7 4.1 %collective-permute-start.8 = (bf16[2,64,512]{2,1,0:T(8,128)(2,1)S(1)}, bf16[2,64,512]{2,1,0:T(8,128)(2,1)S(1)}, u32[]{:S(2)}, u32[]{:S(2)}) collective-permute-start(bf16[2,64,512]{2,1,0:T(8,128)(2,1)S(1)} %get-tuple-element.205), channel_id=1, source_target_pairs={{0,2},{1,3},{2,0},{3,1},{4,6},{5,7},{6,4},{7,5},{8,10},{9,11},{10,... | collective-permute-start | bytes 393224 | tf_op jit(solution)/shard_map/ppermute | solution.py:609
  9.7 6.2 %collective-permute-done.8 = bf16[2,64,512]{2,1,0:T(8,128)(2,1)S(1)} collective-permute-done((bf16[2,64,512]{2,1,0:T(8,128)(2,1)S(1)}, bf16[2,64,512]{2,1,0:T(8,128)(2,1)S(1)}, u32[]{:S(2)}, u32[]{:S(2)}) %collective-permute-start.8) | collective-permute-done | bytes 131104 | tf_op jit(solution)/shard_map/ppermute | solution.py:609
  21.2 19.1 %collective-permute-done.11 = bf16[4,2,64,512]{3,2,1,0:T(8,128)(2,1)S(1)} collective-permute-done((bf16[4,2,64,512]{3,2,1,0:T(8,128)(2,1)S(1)}, bf16[4,2,64,512]{3,2,1,0:T(8,128)(2,1)S(1)}, u32[]{:S(2)}, u32[]{:S(2)}) %collective-permute-start.11) | collective-permute-done | bytes 524320 | tf_op jit(solution)/shard_map/ppermute | solution.py:609
  43.2 5.4 %collective-permute-start.1 = (bf16[4,64,128]{2,1,0:T(8,128)(2,1)S(1)}, bf16[4,64,128]{2,1,0:T(8,128)(2,1)S(1)}, u32[]{:S(2)}, u32[]{:S(2)}) collective-permute-start(bf16[4,64,128]{2,1,0:T(8,128)(2,1)S(1)} %get-tuple-element.209), channel_id=1, source_target_pairs={{0,2},{1,3},{2,0},{3,1},{4,6},{5,7},{6,4},{7,5},{8,10},{9,11},{10,... | collective-permute-start | bytes 196616 | tf_op jit(solution)/shard_map/ppermute | solution.py:609
  48.6 3.8 %collective-permute-start.2 = (bf16[4,64,128]{2,1,0:T(8,128)(2,1)S(1)}, bf16[4,64,128]{2,1,0:T(8,128)(2,1)S(1)}, u32[]{:S(2)}, u32[]{:S(2)}) collective-permute-start(bf16[4,64,128]{2,1,0:T(8,128)(2,1)S(1)} %get-tuple-element.209), channel_id=1, source_target_pairs={{0,3},{1,0},{2,1},{3,2},{4,7},{5,4},{6,5},{7,6},{8,11},{9,8},{10,9... | collective-permute-start | bytes 196616 | tf_op jit(solution)/shard_map/ppermute | solution.py:609
  59.9 8.9 %collective-permute-done.4 = bf16[4,4,64,128]{3,2,1,0:T(8,128)(2,1)S(1)} collective-permute-done((bf16[4,4,64,128]{3,2,1,0:T(8,128)(2,1)S(1)}, bf16[4,4,64,128]{3,2,1,0:T(8,128)(2,1)S(1)}, u32[]{:S(2)}, u32[]{:S(2)}) %collective-permute-start.4) | collective-permute-done | bytes 262176 | tf_op jit(solution)/shard_map/ppermute | solution.py:609
  73.4 3.6 %pre.1 = (f32[800,512]{1,0:T(8,128)S(1)}, bf16[800,512]{1,0:T(8,128)(2,1)S(1)}, bf16[512,800]{1,0:T(8,128)(2,1)S(1)}) custom-call(bf16[800,512]{1,0:T(8,128)(2,1)S(1)} %bitcast.124, f32[16,512]{1,0:T(8,128)S(1)} %copy-done.8), custom_call_target="tpu_custom_call" | custom-call | bytes 27000000 | tf_op jit(solution)/shard_map/pre/pallas_call | solution.py:727
  82.7 15.2 %attn.1 = (f32[4,800,128]{2,1,0:T(8,128)S(1)}, f32[4,800,128]{2,1,0:T(8,128)S(1)}, f32[4,800,128]{2,1,0:T(8,128)S(1)}, f32[4,800,128]{2,1,0:T(8,128)S(1)}, bf16[...) custom-call(s32[25]{0:T(128)S(1)} %concatenate.15.table.refs_0_, ...), custom_call_target="tpu_custom_call" | custom-call | bytes 63000000 | tf_op jit(solution)/shard_map/attn/pallas_call | solution.py:762
  97.9 19.9 %mlp.1 = (bf16[800,512]{1,0:T(8,128)(2,1)}, f32[800,512]{1,0:T(8,128)S(1)}, bf16[4,4,2,64,512]{4,3,2,1,0:T(8,128)(2,1)S(1)}, bf16[4,4,2,64,512]{4,3,2,1,0:T(8,128)(2,1)S(1)}, f32[4,8,512]{2,1,0:T(8,128)S(1)}) custom-call(s32[25]{0:T(128)S(1)} %concatenate.15.table.refs_0_, bf16[800,512]{1,0:T(8,128)(2,1)S(1)} %get-tuple-element.113.n2, ...), custom_call_target="tpu_custom_call" | custom-call | bytes 60000000 | tf_op jit(solution)/shard_map/mlp/pallas_call | solution.py:802
  118.3 3.3 %mid.1 = (f32[800,512]{1,0:T(8,128)S(1)}, bf16[800,512]{1,0:T(8,128)(2,1)S(1)}, bf16[512,800]{1,0:T(8,128)(2,1)S(1)}, f32[8,512]{1,0:T(8,128)S(1)}) custom-call(f32[800,512]{1,0:T(8,128)S(1)} %get-tuple-element.118.gn2, f32[800,512]{1,0:T(8,128)S(1)} %get-tuple-element.116.s1, bf16[800,512]{1,0:T(8,128)(2,1)S(1)} %bitcast.123, f32[16,512]{1,0:T(8,128)S(1)} %copy-done.8), custom_call_target="tpu_custom_call" | custom-call | bytes 12000000 | tf_op jit(solution)/shard_map/mid/pallas_call | solution.py:837
  121.6 23.6 %attn_back_a.1 = (bf16[4,3,4,64,128]{4,3,2,1,0:T(8,128)(2,1)S(1)}, bf16[4,3,4,64,128]{4,3,2,1,0:T(8,128)(2,1)S(1)}, f32[800,512]{1,0:T(8,128)S(1)}, f32[3,56,128]{2,1,0:T(8,128)S(1)}) custom-call(s32[25]{0:T(128)S(1)} %concatenate.15.table.refs_0_, bf16[512,800]{1,0:T(8,128)(2,1)S(1)} %copy-done.5, bf16[800,512]{1,0:T(8,128)(2,1)S(1)} %get-tuple-element.121.refs_2_, ...), custom_call_target="tpu_custom_call" | custom-call | bytes 63000000 | tf_op jit(solution)/shard_map/attn_back_a/pallas_call | solution.py:857
  145.4 8.4 %attn_back_b.1 = (bf16[4,1,4,64,128]{4,3,2,1,0:T(8,128)(2,1)S(1)}, bf16[4,1,4,64,128]{4,3,2,1,0:T(8,128)(2,1)S(1)}, f32[800,512]{1,0:T(8,128)S(1)}, f32[1,56,128]{2,1,0:T(8,128)S(1)}) custom-call(s32[25]{0:T(128)S(1)} %concatenate.15.table.refs_0_, bf16[512,800]{1,0:T(8,128)(2,1)S(1)} %copy-done.5, bf16[800,512]{1,0:T(8,128)(2,1)S(1)} %get-tuple-element.121.refs_2_, ...), custom_call_target="tpu_custom_call" | custom-call | bytes 21000000 | tf_op jit(solution)/shard_map/attn_back_b/pallas_call | solution.py:857
  154.3 7.0 %tail.1 = (bf16[800,512]{1,0:T(8,128)(2,1)}, f32[4,4,24,128]{3,2,1,0:T(8,128)S(1)}) custom-call(s32[25]{0:T(128)S(1)} %concatenate.15.table.refs_0_, f32[800,512]{1,0:T(8,128)S(1)} %copy-done.3, f32[800,512]{1,0:T(8,128)S(1)} %get-tuple-element.119.gs1, f32[800,512]{1,0:T(8,128)S(1)} %get-tuple-element.129.gn1, bf16[800,512]{1,0:T(8,128)(2,1)S(1)} %bitcast.125, ...), custom_call_target="tpu_custom_call" | custom-call | bytes 27000000 | tf_op jit(solution)/shard_map/tail/pallas_call | solution.py:902
  171.7 4.7 %collective-permute-done.16 = bf16[4,4,64,128]{3,2,1,0:T(8,128)(2,1)S(1)} collective-permute-done((bf16[4,4,64,128]{3,2,1,0:T(8,128)(2,1)S(1)}, bf16[4,4,64,128]{3,2,1,0:T(8,128)(2,1)S(1)}, u32[]{:S(2)}, u32[]{:S(2)}) %collective-permute-start.16) | collective-permute-done | bytes 262176 | tf_op jit(solution)/shard_map/ppermute | solution.py:609
  176.4 2.9 %collective-permute-done.18 = bf16[4,4,64,128]{3,2,1,0:T(8,128)(2,1)S(1)} collective-permute-done((bf16[4,4,64,128]{3,2,1,0:T(8,128)(2,1)S(1)}, bf16[4,4,64,128]{3,2,1,0:T(8,128)(2,1)S(1)}, u32[]{:S(2)}, u32[]{:S(2)}) %collective-permute-start.18) | collective-permute-done | bytes 262176 | tf_op jit(solution)/shard_map/ppermute | solution.py:609
  186.6 2.6 %collective-permute-start.24 = (bf16[288,128]{1,0:T(8,128)(2,1)S(1)}, bf16[288,128]{1,0:T(8,128)(2,1)S(1)}, u32[]{:S(2)}, u32[]{:S(2)}) collective-permute-start(bf16[288,128]{1,0:T(8,128)(2,1)S(1)} %get-tuple-element.195), channel_id=1, source_target_pairs={{0,3},{1,0},{2,1},{3,2},{4,7},{5,4},{6,5},{7,6},{8,11},{9,8},{10,9... | collective-permute-start | bytes 221192 | tf_op jit(solution)/shard_map/ppermute | solution.py:609
  189.2 2.4 %collective-permute-done.22 = bf16[288,128]{1,0:T(8,128)(2,1)S(1)} collective-permute-done((bf16[288,128]{1,0:T(8,128)(2,1)S(1)}, bf16[288,128]{1,0:T(8,128)(2,1)S(1)}, u32[]{:S(2)}, u32[]{:S(2)}) %collective-permute-start.22) | collective-permute-done | bytes 73760 | tf_op jit(solution)/shard_map/ppermute | solution.py:609
  191.7 5.2 %collective-permute-done.23 = bf16[288,128]{1,0:T(8,128)(2,1)S(1)} collective-permute-done((bf16[288,128]{1,0:T(8,128)(2,1)S(1)}, bf16[288,128]{1,0:T(8,128)(2,1)S(1)}, u32[]{:S(2)}, u32[]{:S(2)}) %collective-permute-start.23) | collective-permute-done | bytes 73760 | tf_op jit(solution)/shard_map/ppermute | solution.py:609
  197.2 9.5 %collective-permute-done.28 = bf16[4,2,64,512]{3,2,1,0:T(8,128)(2,1)S(1)} collective-permute-done((bf16[4,2,64,512]{3,2,1,0:T(8,128)(2,1)S(1)}, bf16[4,2,64,512]{3,2,1,0:T(8,128)(2,1)S(1)}, u32[]{:S(2)}, u32[]{:S(2)}) %collective-permute-start.28) | collective-permute-done | bytes 524320 | tf_op jit(solution)/shard_map/ppermute | solution.py:609
  209.1 2.6 %collective-permute-start.31 = (bf16[2,64,512]{2,1,0:T(8,128)(2,1)S(1)}, bf16[2,64,512]{2,1,0:T(8,128)(2,1)S(1)}, u32[]{:S(2)}, u32[]{:S(2)}) collective-permute-start(bf16[2,64,512]{2,1,0:T(8,128)(2,1)S(1)} %get-tuple-element.190), channel_id=1, source_target_pairs={{0,3},{1,0},{2,1},{3,2},{4,7},{5,4},{6,5},{7,6},{8,11},{9,8},{10,9... | collective-permute-start | bytes 393224 | tf_op jit(solution)/shard_map/ppermute | solution.py:609
  212.3 3.8 %collective-permute-done.29 = bf16[2,64,512]{2,1,0:T(8,128)(2,1)S(1)} collective-permute-done((bf16[2,64,512]{2,1,0:T(8,128)(2,1)S(1)}, bf16[2,64,512]{2,1,0:T(8,128)(2,1)S(1)}, u32[]{:S(2)}, u32[]{:S(2)}) %collective-permute-start.29) | collective-permute-done | bytes 131104 | tf_op jit(solution)/shard_map/ppermute | solution.py:609
  217.6 5.0 %collective-permute-done.30 = bf16[2,64,512]{2,1,0:T(8,128)(2,1)S(1)} collective-permute-done((bf16[2,64,512]{2,1,0:T(8,128)(2,1)S(1)}, bf16[2,64,512]{2,1,0:T(8,128)(2,1)S(1)}, u32[]{:S(2)}, u32[]{:S(2)}) %collective-permute-start.30) | collective-permute-done | bytes 131104 | tf_op jit(solution)/shard_map/ppermute | solution.py:609
  233.3 2.9 %collective-permute-start.38 = (f32[4,32,128]{2,1,0:T(8,128)S(1)}, f32[4,32,128]{2,1,0:T(8,128)S(1)}, u32[]{:S(2)}, u32[]{:S(2)}) collective-permute-start(f32[4,32,128]{2,1,0:T(8,128)S(1)} %get-tuple-element.207), channel_id=1, source_target_pairs={{0,24},{4,28},{8,0},{12,4},{16,8},{20,12},{24,16},{28,20},{1,25},{... | collective-permute-start | bytes 196616 | tf_op jit(solution)/shard_map/ppermute | solution.py:609
  239.2 2.7 %adam.1 = (f32[1,1]{1,0:T(1,128)}, f32[3,64,128]{2,1,0:T(8,128)}, f32[3,64,128]{2,1,0:T(8,128)}, f32[3,64,128]{2,1,0:T(8,128)}, f32[3,64,128]{2,1,0:T(8,128)}, /...) custom-call(s32[25]{0:T(128)S(1)} %concatenate.15.table.refs_0_, ...), custom_call_target="tpu_custom_call" | custom-call | bytes 12000000 | tf_op jit(solution)/shard_map/adam/pallas_call | solution.py:984
  (173 shorter events, 66.3 us)
Async XLA Ops:
  1.7 14.1 %collective-permute-start.8 = (bf16[2,64,512]{2,1,0:T(8,128)(2,1)S(1)}, bf16[2,64,512]{2,1,0:T(8,128)(2,1)S(1)}, u32[]{:S(2)}, u32[]{:S(2)}) collective-permute-start(bf16[2,64,512]{2,1,0:T(8,128)(2,1)S(1)} %get-tuple-element.205), channel_id=1, source_target_pairs={{0,2},{1,3},{2,0},{3,1},{4,6},{5,7},{6,4},{7,5},{8,10},{9,11},{10,... | collective-permute-start | bytes 393224 | tf_op jit(solution)/shard_map/ppermute | solution.py:609
  5.8 10.0 %collective-permute-start.7 = (bf16[2,64,512]{2,1,0:T(8,128)(2,1)S(1)}, bf16[2,64,512]{2,1,0:T(8,128)(2,1)S(1)}, u32[]{:S(2)}, u32[]{:S(2)}) collective-permute-start(bf16[2,64,512]{2,1,0:T(8,128)(2,1)S(1)} %get-tuple-element.205), channel_id=1, source_target_pairs={{0,1},{1,2},{2,3},{3,0},{4,5},{5,6},{6,7},{7,4},{8,9},{9,10},{10,1... | collective-permute-start | bytes 393224 | tf_op jit(solution)/shard_map/ppermute | solution.py:609
  7.4 9.1 %collective-permute-start.9 = (bf16[2,64,512]{2,1,0:T(8,128)(2,1)S(1)}, bf16[2,64,512]{2,1,0:T(8,128)(2,1)S(1)}, u32[]{:S(2)}, u32[]{:S(2)}) collective-permute-start(bf16[2,64,512]{2,1,0:T(8,128)(2,1)S(1)} %get-tuple-element.205), channel_id=1, source_target_pairs={{0,3},{1,0},{2,1},{3,2},{4,7},{5,4},{6,5},{7,6},{8,11},{9,8},{10,9... | collective-permute-start | bytes 393224 | tf_op jit(solution)/shard_map/ppermute | solution.py:609
  16.6 23.7 %collective-permute-start.11 = (bf16[4,2,64,512]{3,2,1,0:T(8,128)(2,1)S(1)}, bf16[4,2,64,512]{3,2,1,0:T(8,128)(2,1)S(1)}, u32[]{:S(2)}, u32[]{:S(2)}) collective-permute-start(bf16[4,2,64,512]{3,2,1,0:T(8,128)(2,1)S(1)} %get-tuple-element.193), channel_id=1, source_target_pairs={{0,16},{4,20},{8,24},{12,28},{16,0},{20,4},{24,8},{28,12},{1,17},{... | collective-permute-start | bytes 1572872 | tf_op jit(solution)/shard_map/ppermute | solution.py:609
  18.3 22.0 %collective-permute-start.10 = (bf16[4,2,64,512]{3,2,1,0:T(8,128)(2,1)S(1)}, bf16[4,2,64,512]{3,2,1,0:T(8,128)(2,1)S(1)}, u32[]{:S(2)}, u32[]{:S(2)}) collective-permute-start(bf16[4,2,64,512]{3,2,1,0:T(8,128)(2,1)S(1)} %get-tuple-element.193), channel_id=1, source_target_pairs={{0,8},{4,12},{8,16},{12,20},{16,24},{20,28},{24,0},{28,4},{1,9},{5... | collective-permute-start | bytes 1572872 | tf_op jit(solution)/shard_map/ppermute | solution.py:609
  19.8 21.8 %collective-permute-start.12 = (bf16[4,2,64,512]{3,2,1,0:T(8,128)(2,1)S(1)}, bf16[4,2,64,512]{3,2,1,0:T(8,128)(2,1)S(1)}, u32[]{:S(2)}, u32[]{:S(2)}) collective-permute-start(bf16[4,2,64,512]{3,2,1,0:T(8,128)(2,1)S(1)} %get-tuple-element.193), channel_id=1, source_target_pairs={{0,24},{4,28},{8,0},{12,4},{16,8},{20,12},{24,16},{28,20},{1,25},{... | collective-permute-start | bytes 1572872 | tf_op jit(solution)/shard_map/ppermute | solution.py:609
  43.1 54.8 %collective-permute-start.13 = (bf16[4,4,2,64,512]{4,3,2,1,0:T(8,128)(2,1)}, bf16[4,4,2,64,512]{4,3,2,1,0:T(8,128)(2,1)}, u32[]{:S(2)}, u32[]{:S(2)}) collective-permute-start(bf16[4,4,2,64,512]{4,3,2,1,0:T(8,128)(2,1)} %pad_maximum_fusion.refs_0_), channel_id=1, source_target_pairs={{0,4},{4,0},{8,12},{12,8},{16,20},{20,16},{24,28},{28,24},{1,5},{5... | collective-permute-start | bytes 6291464 | tf_op jit(solution)/shard_map/ppermute | solution.py:609
  43.2 9.8 %collective-permute-start.1 = (bf16[4,64,128]{2,1,0:T(8,128)(2,1)S(1)}, bf16[4,64,128]{2,1,0:T(8,128)(2,1)S(1)}, u32[]{:S(2)}, u32[]{:S(2)}) collective-permute-start(bf16[4,64,128]{2,1,0:T(8,128)(2,1)S(1)} %get-tuple-element.209), channel_id=1, source_target_pairs={{0,2},{1,3},{2,0},{3,1},{4,6},{5,7},{6,4},{7,5},{8,10},{9,11},{10,... | collective-permute-start | bytes 196616 | tf_op jit(solution)/shard_map/ppermute | solution.py:609
  55.4 13.4 %collective-permute-start.4 = (bf16[4,4,64,128]{3,2,1,0:T(8,128)(2,1)S(1)}, bf16[4,4,64,128]{3,2,1,0:T(8,128)(2,1)S(1)}, u32[]{:S(2)}, u32[]{:S(2)}) collective-permute-start(bf16[4,4,64,128]{3,2,1,0:T(8,128)(2,1)S(1)} %get-tuple-element.198), channel_id=1, source_target_pairs={{0,16},{4,20},{8,24},{12,28},{16,0},{20,4},{24,8},{28,12},{1,17},{... | collective-permute-start | bytes 786440 | tf_op jit(solution)/shard_map/ppermute | solution.py:609
  57.0 11.8 %collective-permute-start.3 = (bf16[4,4,64,128]{3,2,1,0:T(8,128)(2,1)S(1)}, bf16[4,4,64,128]{3,2,1,0:T(8,128)(2,1)S(1)}, u32[]{:S(2)}, u32[]{:S(2)}) collective-permute-start(bf16[4,4,64,128]{3,2,1,0:T(8,128)(2,1)S(1)} %get-tuple-element.198), channel_id=1, source_target_pairs={{0,8},{4,12},{8,16},{12,20},{16,24},{20,28},{24,0},{28,4},{1,9},{5... | collective-permute-start | bytes 786440 | tf_op jit(solution)/shard_map/ppermute | solution.py:609
  58.4 11.6 %collective-permute-start.5 = (bf16[4,4,64,128]{3,2,1,0:T(8,128)(2,1)S(1)}, bf16[4,4,64,128]{3,2,1,0:T(8,128)(2,1)S(1)}, u32[]{:S(2)}, u32[]{:S(2)}) collective-permute-start(bf16[4,4,64,128]{3,2,1,0:T(8,128)(2,1)S(1)} %get-tuple-element.198), channel_id=1, source_target_pairs={{0,24},{4,28},{8,0},{12,4},{16,8},{20,12},{24,16},{28,20},{1,25},{... | collective-permute-start | bytes 786440 | tf_op jit(solution)/shard_map/ppermute | solution.py:609
  70.1 10.0 %collective-permute-start.6 = (bf16[4,4,4,64,128]{4,3,2,1,0:T(8,128)(2,1)S(1)}, bf16[4,4,4,64,128]{4,3,2,1,0:T(8,128)(2,1)S(1)}, u32[]{:S(2)}, u32[]{:S(2)}) collective-permute-start(bf16[4,4,4,64,128]{4,3,2,1,0:T(8,128)(2,1)S(1)} %pad_maximum_fusion.1.own.refs_4_), channel_id=1, source_target_pairs={{0,4},{4,0},{8,12},{12,8},{16,20},{20,16},{24,28},{28,24},{1,5},{5... | collective-permute-start | bytes 3145736 | tf_op jit(solution)/shard_map/ppermute | solution.py:609
  117.9 62.6 %collective-permute-start.25 = (bf16[4,4,2,64,512]{4,3,2,1,0:T(8,128)(2,1)S(1)}, bf16[4,4,2,64,512]{4,3,2,1,0:T(8,128)(2,1)S(1)}, u32[]{:S(2)}, u32[]{:S(2)}) collective-permute-start(bf16[4,4,2,64,512]{4,3,2,1,0:T(8,128)(2,1)S(1)} %get-tuple-element.143), channel_id=1, source_target_pairs={{0,4},{4,0},{8,12},{12,8},{16,20},{20,16},{24,28},{28,24},{1,5},{5... | collective-permute-start | bytes 6291464 | tf_op jit(solution)/shard_map/ppermute | solution.py:609
  145.3 20.6 %collective-permute-start.14 = (bf16[4,3,4,64,128]{4,3,2,1,0:T(8,128)(2,1)S(1)}, bf16[4,3,4,64,128]{4,3,2,1,0:T(8,128)(2,1)S(1)}, u32[]{:S(2)}, u32[]{:S(2)}) collective-permute-start(bf16[4,3,4,64,128]{4,3,2,1,0:T(8,128)(2,1)S(1)} %get-tuple-element.138), channel_id=1, source_target_pairs={{0,4},{4,0},{8,12},{12,8},{16,20},{20,16},{24,28},{28,24},{1,5},{5... | collective-permute-start | bytes 2359304 | tf_op jit(solution)/shard_map/ppermute | solution.py:609
  153.8 10.5 %collective-permute-start.15 = (bf16[4,1,4,64,128]{4,3,2,1,0:T(8,128)(2,1)S(1)}, bf16[4,1,4,64,128]{4,3,2,1,0:T(8,128)(2,1)S(1)}, u32[]{:S(2)}, u32[]{:S(2)}) collective-permute-start(bf16[4,1,4,64,128]{4,3,2,1,0:T(8,128)(2,1)S(1)} %get-tuple-element.140), channel_id=1, source_target_pairs={{0,4},{4,0},{8,12},{12,8},{16,20},{20,16},{24,28},{28,24},{1,5},{5... | collective-permute-start | bytes 786440 | tf_op jit(solution)/shard_map/ppermute | solution.py:609
  166.3 10.2 %collective-permute-start.16 = (bf16[4,4,64,128]{3,2,1,0:T(8,128)(2,1)S(1)}, bf16[4,4,64,128]{3,2,1,0:T(8,128)(2,1)S(1)}, u32[]{:S(2)}, u32[]{:S(2)}) collective-permute-start(bf16[4,4,64,128]{3,2,1,0:T(8,128)(2,1)S(1)} %get-tuple-element.186), channel_id=1, source_target_pairs={{0,8},{4,12},{8,16},{12,20},{16,24},{20,28},{24,0},{28,4},{1,9},{5... | collective-permute-start | bytes 786440 | tf_op jit(solution)/shard_map/ppermute | solution.py:609
  166.8 12.5 %collective-permute-start.18 = (bf16[4,4,64,128]{3,2,1,0:T(8,128)(2,1)S(1)}, bf16[4,4,64,128]{3,2,1,0:T(8,128)(2,1)S(1)}, u32[]{:S(2)}, u32[]{:S(2)}) collective-permute-start(bf16[4,4,64,128]{3,2,1,0:T(8,128)(2,1)S(1)} %get-tuple-element.187), channel_id=1, source_target_pairs={{0,24},{4,28},{8,0},{12,4},{16,8},{20,12},{24,16},{28,20},{1,25},{... | collective-permute-start | bytes 786440 | tf_op jit(solution)/shard_map/ppermute | solution.py:609
  169.2 11.0 %collective-permute-start.17 = (bf16[4,4,64,128]{3,2,1,0:T(8,128)(2,1)S(1)}, bf16[4,4,64,128]{3,2,1,0:T(8,128)(2,1)S(1)}, u32[]{:S(2)}, u32[]{:S(2)}) collective-permute-start(bf16[4,4,64,128]{3,2,1,0:T(8,128)(2,1)S(1)} %get-tuple-element.188), channel_id=1, source_target_pairs={{0,16},{4,20},{8,24},{12,28},{16,0},{20,4},{24,8},{28,12},{1,17},{... | collective-permute-start | bytes 786440 | tf_op jit(solution)/shard_map/ppermute | solution.py:609
  181.4 15.8 %collective-permute-start.26 = (bf16[4,2,64,512]{3,2,1,0:T(8,128)(2,1)S(1)}, bf16[4,2,64,512]{3,2,1,0:T(8,128)(2,1)S(1)}, u32[]{:S(2)}, u32[]{:S(2)}) collective-permute-start(bf16[4,2,64,512]{3,2,1,0:T(8,128)(2,1)S(1)} %get-tuple-element.183), channel_id=1, source_target_pairs={{0,8},{4,12},{8,16},{12,20},{16,24},{20,28},{24,0},{28,4},{1,9},{5... | collective-permute-start | bytes 1572872 | tf_op jit(solution)/shard_map/ppermute | solution.py:609
  183.2 23.5 %collective-permute-start.28 = (bf16[4,2,64,512]{3,2,1,0:T(8,128)(2,1)S(1)}, bf16[4,2,64,512]{3,2,1,0:T(8,128)(2,1)S(1)}, u32[]{:S(2)}, u32[]{:S(2)}) collective-permute-start(bf16[4,2,64,512]{3,2,1,0:T(8,128)(2,1)S(1)} %get-tuple-element.184), channel_id=1, source_target_pairs={{0,24},{4,28},{8,0},{12,4},{16,8},{20,12},{24,16},{28,20},{1,25},{... | collective-permute-start | bytes 1572872 | tf_op jit(solution)/shard_map/ppermute | solution.py:609
  184.4 23.1 %collective-permute-start.27 = (bf16[4,2,64,512]{3,2,1,0:T(8,128)(2,1)S(1)}, bf16[4,2,64,512]{3,2,1,0:T(8,128)(2,1)S(1)}, u32[]{:S(2)}, u32[]{:S(2)}) collective-permute-start(bf16[4,2,64,512]{3,2,1,0:T(8,128)(2,1)S(1)} %get-tuple-element.185), channel_id=1, source_target_pairs={{0,16},{4,20},{8,24},{12,28},{16,0},{20,4},{24,8},{28,12},{1,17},{... | collective-permute-start | bytes 1572872 | tf_op jit(solution)/shard_map/ppermute | solution.py:609
  207.8 8.3 %collective-permute-start.29 = (bf16[2,64,512]{2,1,0:T(8,128)(2,1)S(1)}, bf16[2,64,512]{2,1,0:T(8,128)(2,1)S(1)}, u32[]{:S(2)}, u32[]{:S(2)}) collective-permute-start(bf16[2,64,512]{2,1,0:T(8,128)(2,1)S(1)} %get-tuple-element.189), channel_id=1, source_target_pairs={{0,1},{1,2},{2,3},{3,0},{4,5},{5,6},{6,7},{7,4},{8,9},{9,10},{10,1... | collective-permute-start | bytes 393224 | tf_op jit(solution)/shard_map/ppermute | solution.py:609
  209.1 8.5 %collective-permute-start.31 = (bf16[2,64,512]{2,1,0:T(8,128)(2,1)S(1)}, bf16[2,64,512]{2,1,0:T(8,128)(2,1)S(1)}, u32[]{:S(2)}, u32[]{:S(2)}) collective-permute-start(bf16[2,64,512]{2,1,0:T(8,128)(2,1)S(1)} %get-tuple-element.190), channel_id=1, source_target_pairs={{0,3},{1,0},{2,1},{3,2},{4,7},{5,4},{6,5},{7,6},{8,11},{9,8},{10,9... | collective-permute-start | bytes 393224 | tf_op jit(solution)/shard_map/ppermute | solution.py:609
  211.7 11.0 %collective-permute-start.30 = (bf16[2,64,512]{2,1,0:T(8,128)(2,1)S(1)}, bf16[2,64,512]{2,1,0:T(8,128)(2,1)S(1)}, u32[]{:S(2)}, u32[]{:S(2)}) collective-permute-start(bf16[2,64,512]{2,1,0:T(8,128)(2,1)S(1)} %get-tuple-element.191), channel_id=1, source_target_pairs={{0,2},{1,3},{2,0},{3,1},{4,6},{5,7},{6,4},{7,5},{8,10},{9,11},{10,... | collective-permute-start | bytes 393224 | tf_op jit(solution)/shard_map/ppermute | solution.py:609
  (52 other events, 1080.6 us)
